TPU v7x, 32 devices: a whole 2x2x4 slice. The times are simulated.
32 devices in a mesh: dp: 16 (over z, y, core), tensor: 2 (over x).
Axes of the slice: x: 2, y: 2, z: 4, core: 2. Of those that a mesh axis runs over, the one named last changes fastest.
Arguments:
- inputs: bfloat16 [64, 320, 1024], P(('dp', 'tensor')), may hold values from -6 to 6
- keep_mask: int32 [64, 256], P(('dp', 'tensor')), may hold values 0 or 1
- cotangent: bfloat16 [64, 320, 1024], P(('dp', 'tensor')), may hold values from -6 to 6
- ln1_gain: float32 [1024], replicated, may hold values from 0.1 to 1.9
- ln1_bias: float32 [1024], replicated, may hold values from -3 to 3
- w_qkv: bfloat16 [3, 1024, 1024], P(None, None, 'tensor'), may hold values from -0.1875 to 0.1875
- qv_bias: float32 [2, 1024], P(None, 'tensor'), may hold values from -2.5 to 2.5
- w_out: bfloat16 [1024, 1024], P('tensor'), may hold values from -0.75 to 0.75
- out_bias: float32 [1024], replicated, may hold values from -3 to 3
- ln2_gain: float32 [1024], replicated, may hold values from 0.1 to 1.9
- ln2_bias: float32 [1024], replicated, may hold values from -3 to 3
- w_fc1: bfloat16 [1024, 4096], P(None, 'tensor'), may hold values from -0.1875 to 0.1875
- fc1_bias: float32 [4096], P('tensor'), may hold values from -3 to 3
- w_fc2: bfloat16 [4096, 1024], P('tensor'), may hold values from -0.09375 to 0.09375
- fc2_bias: float32 [1024], replicated, may hold values from -3 to 3
Outputs:
- layer_out: bfloat16 [64, 320, 1024], P(('dp', 'tensor'))
- grad_input: bfloat16 [64, 320, 1024], P(('dp', 'tensor'))
- grad_ln1_gain: float32 [1024], replicated
- grad_ln1_bias: float32 [1024], replicated
- grad_qkv: float32 [3, 1024, 1024], P(None, None, 'tensor')
- grad_qv_bias: float32 [2, 1024], P(None, 'tensor')
- grad_out: float32 [1024, 1024], P('tensor')
- grad_out_bias: float32 [1024], replicated
- grad_ln2_gain: float32 [1024], replicated
- grad_ln2_bias: float32 [1024], replicated
- grad_fc1: float32 [1024, 4096], P(None, 'tensor')
- grad_fc1_bias: float32 [4096], P('tensor')
- grad_fc2: float32 [4096, 1024], P('tensor')
- grad_fc2_bias: float32 [1024], replicated
Inputs may be any that keep to these rules, and one draw needn't show every extreme that they name: keep_mask is 1 for a kept slot and 0 for a masked one.
All inputs are finite; a program needn't handle non-finite values. No bound on the sum of `keep_mask` on one device may be relied on, other than what follows from the above.
Results may differ from a plain program's by a relative error of at most 0.02.
Values may be sent and summed in bfloat16 or wider, within the bound.
No kernel may reach another device: no remote copies, remote signals or barrier semaphores. Data moves between devices by JAX's collectives and lax.ppermute only.
A program may use at most 256 MiB of HBM per device.

v0:
```python
import jax
import jax.numpy as jnp
from jax import lax
from jax.sharding import PartitionSpec as P

HD = 64
BUF = 64
MICRO = 2


epsilon = 1e-06


def layer_norm(values, gain_vec, shift_vec):
    row_mean = jnp.mean(values, axis=-1, keepdims=True)
    centred = values - row_mean
    inverse = lax.rsqrt(jnp.mean(centred * centred, axis=-1, keepdims=True) + epsilon)
    normed = centred * inverse
    return (normed * gain_vec + shift_vec, normed, inverse)


def norm_back(grad_rows, normed, inverse, gain_vec):
    scaled = grad_rows * gain_vec
    centred_grad = (
        scaled
        - jnp.mean(scaled, axis=-1, keepdims=True)
        - normed * jnp.mean(scaled * normed, axis=-1, keepdims=True)
    )
    return (
        centred_grad * inverse,
        jnp.sum(grad_rows * normed, axis=(0, 1)),
        jnp.sum(grad_rows, axis=(0, 1)),
    )


def gelu_slope(pre_act):
    normal_cdf = 0.5 * (1.0 + lax.erf(pre_act * 0.7071067811865476))
    return normal_cdf + pre_act * jnp.exp(-0.5 * pre_act * pre_act) * 0.3989422804014327


def masked_scores(query, key_rows, keep_all, score_scale):
    raw_scores = (
        jnp.einsum("iqhd,ikhd->ihqk", query, key_rows, preferred_element_type=jnp.float32)
        * score_scale
    )
    return jnp.where(keep_all[:, None, None, :] > 0.5, raw_scores, -1e30)


def local(
    inputs,
    keep_mask,
    cotangent,
    ln1_gain,
    ln1_bias,
    w_qkv,
    qv_bias,
    w_out,
    out_bias,
    ln2_gain,
    ln2_bias,
    w_fc1,
    fc1_bias,
    w_fc2,
    fc2_bias,
):
    f32 = jnp.float32
    bf16 = jnp.bfloat16
    micro_img = inputs.shape[0] // MICRO
    seq_len = inputs.shape[1]
    model_width = inputs.shape[2]
    local_width = w_qkv.shape[2]
    local_heads = local_width // HD
    score_scale = HD ** (-0.5)
    qkv_bias = jnp.stack([qv_bias[0], jnp.zeros_like(qv_bias[0]), qv_bias[1]])[:, None, None, :]
    fc1_use, fc1_bias_use, fc2_use = (w_fc1, fc1_bias, w_fc2)
    grad_qkv = jnp.zeros(w_qkv.shape, f32)
    grad_qv_bias = jnp.zeros(qv_bias.shape, f32)
    grad_out = jnp.zeros(w_out.shape, f32)
    grad_fc1 = jnp.zeros(fc1_use.shape, f32)
    grad_fc1_bias = jnp.zeros(fc1_bias_use.shape, f32)
    grad_fc2 = jnp.zeros(fc2_use.shape, f32)
    grad_ln1_gain = jnp.zeros((model_width,), f32)
    grad_ln1_bias = jnp.zeros((model_width,), f32)
    grad_out_bias = jnp.zeros((model_width,), f32)
    grad_ln2_gain = jnp.zeros((model_width,), f32)
    grad_ln2_bias = jnp.zeros((model_width,), f32)
    grad_fc2_bias = jnp.zeros((model_width,), f32)
    layer_parts = []
    input_parts = []
    for micro in range(MICRO):
        first_row = micro * micro_img
        x_part = lax.slice_in_dim(inputs, first_row, first_row + micro_img, axis=0).astype(f32)
        mask_part = lax.slice_in_dim(keep_mask, first_row, first_row + micro_img, axis=0)
        cot_part = lax.slice_in_dim(cotangent, first_row, first_row + micro_img, axis=0)
        keep_own = jnp.concatenate([jnp.ones((micro_img, BUF), f32), mask_part.astype(f32)], axis=1)
        norm1_val, norm1_unit, norm1_inv = layer_norm(x_part, ln1_gain, ln1_bias)
        norm1_low = norm1_val.astype(bf16)
        norm1_all, keep_sent = (
            lax.all_gather(norm1_low, "tensor", axis=0, tiled=True),
            lax.all_gather(keep_own.astype(bf16), "tensor", axis=0, tiled=True),
        )
        keep_all = keep_sent.astype(f32)
        group_img = norm1_all.shape[0]
        projected = jnp.einsum("isd,cde->cise", norm1_all, w_qkv, preferred_element_type=f32)
        proj_low = (projected + qkv_bias).astype(bf16)
        query = proj_low[0].reshape(group_img, seq_len, local_heads, HD)
        key_rows = proj_low[1].reshape(group_img, seq_len, local_heads, HD)
        value = proj_low[2].reshape(group_img, seq_len, local_heads, HD)
        scores = masked_scores(query, key_rows, keep_all, score_scale)
        row_top = jnp.max(scores, axis=-1, keepdims=True)
        exp_scores = jnp.exp(scores - row_top)
        row_total = jnp.sum(exp_scores, axis=-1, keepdims=True)
        log_total = row_top + jnp.log(row_total)
        prob_low = (exp_scores / row_total).astype(bf16)
        mixed_rows = jnp.einsum("ihqk,ikhd->iqhd", prob_low, value, preferred_element_type=f32)
        mixed_low = mixed_rows.reshape(group_img, seq_len, local_width).astype(bf16)
        attn_own = (
            lax.psum_scatter(
                jnp.einsum("isd,de->ise", mixed_low, w_out, preferred_element_type=f32).astype(
                    jnp.bfloat16
                ),
                "tensor",
                scatter_dimension=0,
                tiled=True,
            ).astype(jnp.float32)
            + out_bias
        )
        mid = x_part + attn_own
        norm2_val, norm2_unit, norm2_inv = layer_norm(mid, ln2_gain, ln2_bias)
        norm2_low = norm2_val.astype(bf16)
        norm2_all = lax.all_gather(norm2_low, "tensor", axis=0, tiled=True)
        pre_act = (
            jnp.einsum("isd,df->isf", norm2_all, fc1_use, preferred_element_type=f32) + fc1_bias_use
        )
        act_low = jax.nn.gelu(pre_act, approximate=False).astype(bf16)
        mlp_own = (
            lax.psum_scatter(
                jnp.einsum("isf,fd->isd", act_low, fc2_use, preferred_element_type=f32).astype(
                    jnp.bfloat16
                ),
                "tensor",
                scatter_dimension=0,
                tiled=True,
            ).astype(jnp.float32)
            + fc2_bias
        )
        layer_parts.append((keep_own[:, :, None] * (mid + mlp_own)).astype(bf16))
        grad_top = keep_own[:, :, None] * cot_part.astype(f32)
        grad_fc2_bias = grad_fc2_bias + jnp.sum(grad_top, axis=(0, 1))
        grad_top_low = grad_top.astype(bf16)
        grad_top_all = lax.all_gather(grad_top_low, "tensor", axis=0, tiled=True)
        grad_fc2 = grad_fc2 + jnp.einsum(
            "isf,isd->fd", act_low, grad_top_all, preferred_element_type=f32
        )
        grad_act = jnp.einsum("isd,fd->isf", grad_top_all, fc2_use, preferred_element_type=f32)
        grad_pre = (grad_act * gelu_slope(pre_act)).astype(bf16)
        grad_fc1_bias = grad_fc1_bias + jnp.sum(grad_pre, axis=(0, 1), dtype=f32)
        grad_fc1 = grad_fc1 + jnp.einsum(
            "isd,isf->df", norm2_all, grad_pre, preferred_element_type=f32
        )
        grad_norm2 = lax.psum_scatter(
            jnp.einsum("isf,df->isd", grad_pre, fc1_use, preferred_element_type=f32).astype(
                jnp.bfloat16
            ),
            "tensor",
            scatter_dimension=0,
            tiled=True,
        ).astype(jnp.float32)
        grad_ln2_part, gain2_part, bias2_part = norm_back(
            grad_norm2, norm2_unit, norm2_inv, ln2_gain
        )
        grad_ln2_gain = grad_ln2_gain + gain2_part
        grad_ln2_bias = grad_ln2_bias + bias2_part
        grad_mid = grad_top + grad_ln2_part
        grad_attn_low = grad_mid.astype(bf16)
        grad_out_bias = grad_out_bias + jnp.sum(grad_attn_low, axis=(0, 1), dtype=f32)
        grad_attn_all = lax.all_gather(grad_attn_low, "tensor", axis=0, tiled=True)
        grad_out = grad_out + jnp.einsum(
            "isd,ise->de", mixed_low, grad_attn_all, preferred_element_type=f32
        )
        grad_mixed = jnp.einsum("ise,de->isd", grad_attn_all, w_out, preferred_element_type=f32)
        grad_mixed = grad_mixed.astype(bf16).reshape(group_img, seq_len, local_heads, HD)
        again_scores = masked_scores(query, key_rows, keep_all, score_scale)
        prob_rows = jnp.exp(again_scores - log_total)
        again_low = prob_rows.astype(bf16)
        grad_value = jnp.einsum(
            "ihqk,iqhd->ikhd", again_low, grad_mixed, preferred_element_type=f32
        )
        grad_prob = jnp.einsum("iqhd,ikhd->ihqk", grad_mixed, value, preferred_element_type=f32)
        row_delta = jnp.sum(prob_rows * grad_prob, axis=-1, keepdims=True)
        grad_scores = (prob_rows * (grad_prob - row_delta)).astype(bf16)
        grad_query = (
            jnp.einsum("ihqk,ikhd->iqhd", grad_scores, key_rows, preferred_element_type=f32)
            * score_scale
        )
        grad_key = (
            jnp.einsum("ihqk,iqhd->ikhd", grad_scores, query, preferred_element_type=f32)
            * score_scale
        )
        grad_proj = (
            jnp.stack([grad_query, grad_key, grad_value])
            .reshape(3, group_img, seq_len, local_width)
            .astype(bf16)
        )
        grad_qv_bias = grad_qv_bias + jnp.stack(
            [
                jnp.sum(grad_proj[0], axis=(0, 1), dtype=f32),
                jnp.sum(grad_proj[2], axis=(0, 1), dtype=f32),
            ]
        )
        grad_qkv = grad_qkv + jnp.einsum(
            "isd,cise->cde", norm1_all, grad_proj, preferred_element_type=f32
        )
        grad_norm1 = lax.psum_scatter(
            jnp.einsum("cise,cde->isd", grad_proj, w_qkv, preferred_element_type=f32).astype(
                jnp.bfloat16
            ),
            "tensor",
            scatter_dimension=0,
            tiled=True,
        ).astype(jnp.float32)
        grad_ln1_part, gain1_part, bias1_part = norm_back(
            grad_norm1, norm1_unit, norm1_inv, ln1_gain
        )
        grad_ln1_gain = grad_ln1_gain + gain1_part
        grad_ln1_bias = grad_ln1_bias + bias1_part
        input_parts.append((grad_mid + grad_ln1_part).astype(bf16))
    grad_qkv, grad_qv_bias, grad_out, grad_fc1, grad_fc1_bias, grad_fc2 = (
        lax.psum(grad_qkv.astype(jnp.bfloat16), "dp").astype(jnp.float32),
        lax.psum(grad_qv_bias.astype(jnp.bfloat16), "dp").astype(jnp.float32),
        lax.psum(grad_out.astype(jnp.bfloat16), "dp").astype(jnp.float32),
        lax.psum(grad_fc1.astype(jnp.bfloat16), "dp").astype(jnp.float32),
        lax.psum(grad_fc1_bias.astype(jnp.bfloat16), "dp").astype(jnp.float32),
        lax.psum(grad_fc2.astype(jnp.bfloat16), "dp").astype(jnp.float32),
    )
    grad_ln1_gain, grad_ln1_bias, grad_out_bias, grad_ln2_gain, grad_ln2_bias, grad_fc2_bias = (
        lax.psum(
            (
                grad_ln1_gain,
                grad_ln1_bias,
                grad_out_bias,
                grad_ln2_gain,
                grad_ln2_bias,
                grad_fc2_bias,
            ),
            ("dp", "tensor"),
        )
    )
    layer_out = jnp.concatenate(layer_parts, axis=0)
    grad_input = jnp.concatenate(input_parts, axis=0)
    return (
        layer_out,
        grad_input,
        grad_ln1_gain,
        grad_ln1_bias,
        grad_qkv,
        grad_qv_bias,
        grad_out,
        grad_out_bias,
        grad_ln2_gain,
        grad_ln2_bias,
        grad_fc1,
        grad_fc1_bias,
        grad_fc2,
        grad_fc2_bias,
    )


def solution(mesh):
    return jax.shard_map(
        local,
        mesh=mesh,
        in_specs=(
            P(("dp", "tensor"), None, None),
            P(("dp", "tensor"), None),
            P(("dp", "tensor"), None, None),
            P(),
            P(),
            P(None, None, "tensor"),
            P(None, "tensor"),
            P("tensor", None),
            P(),
            P(),
            P(),
            P(None, "tensor"),
            P("tensor"),
            P("tensor", None),
            P(),
        ),
        out_specs=(
            P(("dp", "tensor"), None, None),
            P(("dp", "tensor"), None, None),
            P(),
            P(),
            P(None, None, "tensor"),
            P(None, "tensor"),
            P("tensor", None),
            P(),
            P(),
            P(),
            P(None, "tensor"),
            P("tensor"),
            P("tensor", None),
            P(),
        ),
        check_vma=False,
    )
```

profile of v0, /device:TPU:0, one launch (start us, length us, event | category | flops | bytes accessed | tf_op | source)
XLA Modules:
  0.0 750.7 jit_solution(11010200674479311292)
XLA Ops:
  14.1 5.2 all-gather.1
  23.9 16.5 %all-gather.11.cloned.1.call-done = bf16[2,320,1024]{2,1,0:T(8,128)(2,1)} async-done(((bf16[1,320,1024]{2,1,0:T(8,128)(2,1)}), bf16[2,320,1024]{2,1,0:T(8,128)(2,1)}) %all-gather.11.cloned.1.call-update) | async-done | bytes 1310736 | tf_op jit(solution)/shard_map/all_gather | solution.py:99
  52.0 14.7 %all-gather.15.cloned.1.call-done = bf16[2,320,1024]{2,1,0:T(8,128)(2,1)} async-done(((bf16[1,320,1024]{2,1,0:T(8,128)(2,1)}), bf16[2,320,1024]{2,1,0:T(8,128)(2,1)}) %all-gather.15.cloned.1.call-update) | async-done | bytes 1310736 | tf_op jit(solution)/shard_map/all_gather | solution.py:99
  102.9 10.6 %reduce-scatter.13.cloned.1.call-done = bf16[1,320,1024]{2,1,0:T(8,128)(2,1)} async-done(((bf16[2,320,1024]{2,1,0:T(8,128)(2,1)}), bf16[1,320,1024]{2,1,0:T(8,128)(2,1)}) %reduce-scatter.13.cloned.1.call-update) | async-done | bytes 655376 | tf_op jit(solution)/shard_map/reduce_scatter | solution.py:118
  113.6 26.0 %reduce-scatter.9.cloned.1.call-done = bf16[1,320,1024]{2,1,0:T(8,128)(2,1)} async-done(((bf16[2,320,1024]{2,1,0:T(8,128)(2,1)}), bf16[1,320,1024]{2,1,0:T(8,128)(2,1)}) %reduce-scatter.9.cloned.1.call-update) | async-done | bytes 655376 | tf_op jit(solution)/shard_map/reduce_scatter | solution.py:118
  150.2 20.0 %all-gather.17.cloned.1.call-done = bf16[2,320,1024]{2,1,0:T(8,128)(2,1)} async-done(((bf16[1,320,1024]{2,1,0:T(8,128)(2,1)}), bf16[2,320,1024]{2,1,0:T(8,128)(2,1)}) %all-gather.17.cloned.1.call-update) | async-done | bytes 1310736 | tf_op jit(solution)/shard_map/all_gather | solution.py:131
  170.2 7.8 %fusion.49 = f32[2,320,2048]{2,1,0:T(8,128)} fusion(bf16[2,320,1024]{2,1,0:T(8,128)(2,1)} %all-gather.17.cloned.1.call-done, bf16[1024,2048]{1,0:T(8,128)(2,1)} %param.26), kind=kOutput, calls=%fused_computation.93 | convolution fusion | flops 2684354560 | bytes 10747904 | tf_op jit(solution)/shard_map/isd,df->isf/dot_general | solution.py:133
  178.1 18.4 %all-gather.23.cloned.1.call-done = bf16[2,320,1024]{2,1,0:T(8,128)(2,1)} async-done(((bf16[1,320,1024]{2,1,0:T(8,128)(2,1)}), bf16[2,320,1024]{2,1,0:T(8,128)(2,1)}) %all-gather.23.cloned.1.call-update) | async-done | bytes 1310736 | tf_op jit(solution)/shard_map/all_gather | solution.py:151
  196.5 8.2 %convert_reduce_fusion = (f32[2048]{0:T(1024)}, bf16[2,320,2048]{2,1,0:T(8,128)(2,1)S(1)}) fusion(f32[2,320,2048]{2,1,0:T(8,128)} %fusion.49, f32[2048]{0:T(1024)S(1)} %copy-done.37, bf16[2,320,1024]{2,1,0:T(8,128)(2,1)} %all-gather.23.cloned.1.call-done, bf16[2048,1024]{1,0:T(8,128)(2,1)} %param.28), kind=kOutput, calls=%fused_computation.53 | convolution fusion | flops 2701391872 | bytes 13385728 | tf_op jit(solution)/shard_map/isd,fd->isf/dot_general | solution.py:155
  210.5 12.5 %all-gather.13.cloned.1.call-done = bf16[2,320,1024]{2,1,0:T(8,128)(2,1)} async-done(((bf16[1,320,1024]{2,1,0:T(8,128)(2,1)}), bf16[2,320,1024]{2,1,0:T(8,128)(2,1)}) %all-gather.13.cloned.1.call-update) | async-done | bytes 1310736 | tf_op jit(solution)/shard_map/all_gather | solution.py:131
  222.9 15.0 %fusion.166 = (u8[320,2048]{1,0:T(8,128)(4,1)}, u8[320,2048]{1,0:T(8,128)(4,1)}, u8[320,2048]{1,0:T(8,128)(4,1)}, u8[320,2048]{1,0:T(8,128)(4,1)}, f32[2,320,2048]{2,1,0:T(8,128)}) fusion(f32[2048]{0:T(1024)S(1)} %copy-done.37, f32[2,320,2048]{2,1,0:T(8,128)} %fusion.49, bf16[2,320,1024]{2,1,0:T(8,128)(2,1)} %all-gather.13.cloned.1.call-done, ...), kind=kOutput, calls=%fused_computation.233 | convolution fusion | flops 2718433280 | bytes 18620416 | tf_op jit(solution)/shard_map/isd,df->isf/dot_general | solution.py:133
  237.9 10.9 %all-gather.19.cloned.1.call-done = bf16[2,320,1024]{2,1,0:T(8,128)(2,1)} async-done(((bf16[1,320,1024]{2,1,0:T(8,128)(2,1)}), bf16[2,320,1024]{2,1,0:T(8,128)(2,1)}) %all-gather.19.cloned.1.call-update) | async-done | bytes 1310736 | tf_op jit(solution)/shard_map/all_gather | solution.py:151
  248.8 7.6 %convert_reduce_fusion.1 = (f32[2048]{0:T(1024)S(1)}, bf16[2,320,2048]{2,1,0:T(8,128)(2,1)S(1)}) fusion(f32[2,320,2048]{2,1,0:T(8,128)} %get-tuple-element.154, f32[2048]{0:T(1024)S(1)} %copy-done.37, bf16[2,320,1024]{2,1,0:T(8,128)(2,1)} %all-gather.19.cloned.1.call-done, bf16[2048,1024]{1,0:T(8,128)(2,1)} %param.28), kind=kOutput, calls=%fused_computation.54 | convolution fusion | flops 2701391872 | bytes 13385728 | tf_op jit(solution)/shard_map/isd,fd->isf/dot_general | solution.py:155
  262.3 27.0 %fusion.9 = (bf16[2,320,2048]{2,1,0:T(8,128)(2,1)}, bf16[2,320,2048]{2,1,0:T(8,128)(2,1)S(1)}) fusion(f32[2,320,2048]{2,1,0:T(8,128)} %get-tuple-element.154, f32[2048]{0:T(1024)S(1)} %copy-done.37, u8[320,2048]{1,0:T(8,128)(4,1)} %get-tuple-element.71, u8[320,2048]{1,0:T(8,128)(4,1)} %get-tuple-element.70, u8[320,2048]{1,0:T(8,128)(4,1)} %get-tuple-element.104, ...), kind=kLoop, calls=%fused_computation.28 | loop fusion | flops 184811520 | bytes 18358272 | tf_op jit(solution)/shard_map/convert_element_type | solution.py:135
  295.0 6.9 fusion.105
  302.0 5.8 fusion.193
  307.9 5.3 fusion.1
  316.8 10.0 %reduce-scatter.15.cloned.1.call-done = bf16[1,320,1024]{2,1,0:T(8,128)(2,1)} async-done(((bf16[2,320,1024]{2,1,0:T(8,128)(2,1)}), bf16[1,320,1024]{2,1,0:T(8,128)(2,1)}) %reduce-scatter.15.cloned.1.call-update) | async-done | bytes 655376 | tf_op jit(solution)/shard_map/reduce_scatter | solution.py:137
  331.2 9.0 %fusion.194 = f32[2048,1024,1]{1,0,2:T(8,128)} fusion(bf16[2,320,2048]{2,1,0:T(8,128)(2,1)} %get-tuple-element.144, bf16[2,320,1024]{2,1,0:T(8,128)(2,1)} %all-gather.19.cloned.1.call-done), kind=kOutput, calls=%fused_computation.292 | convolution fusion | flops 2684354560 | bytes 12320768 | tf_op jit(solution)/shard_map/isf,isd->fd/dot_general | solution.py:152
  340.2 12.1 %reduce-scatter.11.cloned.1.call-done = bf16[1,320,1024]{2,1,0:T(8,128)(2,1)} async-done(((bf16[2,320,1024]{2,1,0:T(8,128)(2,1)}), bf16[1,320,1024]{2,1,0:T(8,128)(2,1)}) %reduce-scatter.11.cloned.1.call-update) | async-done | bytes 655376 | tf_op jit(solution)/shard_map/reduce_scatter | solution.py:137
  356.4 22.3 %all-gather.25.cloned.1.call-done = bf16[2,320,1024]{2,1,0:T(8,128)(2,1)} async-done(((bf16[1,320,1024]{2,1,0:T(8,128)(2,1)}), bf16[2,320,1024]{2,1,0:T(8,128)(2,1)}) %all-gather.25.cloned.1.call-update) | async-done | bytes 1310736 | tf_op jit(solution)/shard_map/all_gather | solution.py:177
  384.2 7.5 multiply_reduce_fusion
  409.9 6.3 fusion.121
  425.2 4.8 bitcast_convert_fusion
  430.3 6.9 multiply_reduce_fusion.1
  454.5 4.8 bitcast_convert_fusion.1
  459.8 10.2 %fusion = bf16[2048,1024]{1,0:T(8,128)(2,1)} fusion(f32[2048,1024,1]{1,0,2:T(8,128)} %fusion.194, bf16[2,320,2048]{2,1,0:T(8,128)(2,1)} %copy-done.18, bf16[2,320,1024]{2,1,0:T(8,128)(2,1)} %all-gather.23.cloned.1.call-done), kind=kOutput, calls=%fused_computation.1 | convolution fusion | flops 2688548864 | bytes 16515072 | tf_op jit(solution)/shard_map/isf,isd->fd/dot_general | solution.py:152
  485.8 35.7 %all-reduce.3 = (bf16[2,512]{1,0:T(2,128)(2,1)S(1)}, bf16[2048]{0:T(1024)(128)(2,1)S(1)}) all-reduce(bf16[2,512]{1,0:T(2,128)(2,1)S(1)} %fusion.174, bf16[2048]{0:T(1024)(128)(2,1)S(1)} %add_convert_fusion.4), channel_id=1, replica_groups=mesh['dp'=16,'tensor'=2] {'dp'}, use_global_device_ids=true, to_apply=%region_41.42 | all-reduce | flops 3072 | bytes 12288 | tf_op jit(solution)/shard_map/psum | solution.py:230
  525.8 39.5 %all-reduce.2 = (f32[1024]{0:T(1024)}, f32[1024]{0:T(1024)}, f32[1024]{0:T(1024)}, f32[1024]{0:T(1024)}, f32[1024]{0:T(1024)}, /*index=5*/f32[1024]{0:T(1024)}) all-reduce(f32[1024]{0:T(1024)S(1)} %add.287, f32[1024]{0:T(1024)S(1)} %add.288, f32[1024]{0:T(1024)S(1)} %add.292, ...), channel_id=1, replica_groups=mesh['dp'=16,'tensor'=2] {'dp','tensor'}, use_global_device_ids=true, to_apply=%region_32.33 | all-reduce | flops 6144 | bytes 49152 | tf_op jit(solution)/shard_map/psum | solution.py:237
  569.6 154.9 %all-reduce.7.cloned.1.call-done = (bf16[3,1024,512]{1,2,0:T(8,128)(2,1)}, bf16[512,1024]{1,0:T(8,128)(2,1)}, bf16[1024,2048]{1,0:T(8,128)(2,1)}, bf16[2048,1024]{1,0:T(8,128)(2,1)}) async-done(((bf16[3,1024,512]{1,2,0:T(8,128)(2,1)}, bf16[512,1024]{1,0:T(8,128)(2,1)}, bf16[1024,2048]{1,0:T(8,128)(2,1)}, bf16[2048,1024]{1,0:T(8,128)(2,1)}), (bf16[3,1024,512]{1,2,0:T(8,128)(2,1)}, ...) | async-done | bytes 12582928 | tf_op jit(solution)/shard_map/psum | solution.py:229
  727.3 5.4 copy.148
  732.7 6.8 convert_element_type.323
  (264 shorter events, 181.2 us)
Async XLA Ops:
  7.2 33.2 %copy-start = (bf16[3,1024,512]{2,1,0:T(8,128)(2,1)S(1)}, bf16[3,1024,512]{2,1,0:T(8,128)(2,1)}, u32[]{:S(2)}) copy-start(bf16[3,1024,512]{2,1,0:T(8,128)(2,1)} %param.20) | copy-start | bytes 9437188
  7.2 16.6 %copy-start.40 = (f32[2,512]{1,0:T(2,128)S(1)}, f32[2,512]{1,0:T(2,128)}, u32[]{:S(2)}) copy-start(f32[2,512]{1,0:T(2,128)} %param.21) | copy-start | bytes 12292
  7.2 33.1 %all-gather.11.cloned.1.call-start = ((), (), s32[]{:S(2)}) async-start(), calls=%async_computation.8 | async-start | bytes 1966080 | tf_op jit(solution)/shard_map/all_gather | solution.py:99
  13.2 53.6 %all-gather.15.cloned.1.call-start = ((), (), s32[]{:S(2)}) async-start(), calls=%async_computation.12 | async-start | bytes 1966080 | tf_op jit(solution)/shard_map/all_gather | solution.py:99
  13.9 99.6 %reduce-scatter.13.cloned.1.call-start = ((), (), s32[]{:S(2)}) async-start(), calls=%async_computation.13 | async-start | bytes 1966080 | tf_op jit(solution)/shard_map/reduce_scatter | solution.py:118
  90.2 49.3 %reduce-scatter.9.cloned.1.call-start = ((), (), s32[]{:S(2)}) async-start(), calls=%async_computation.9 | async-start | bytes 1966080 | tf_op jit(solution)/shard_map/reduce_scatter | solution.py:118
  100.0 39.5 %copy-start.25 = (f32[1024]{0:T(1024)S(1)}, f32[1024]{0:T(1024)}, u32[]{:S(2)}) copy-start(f32[1024]{0:T(1024)} %param.23) | copy-start | bytes 12292
  102.9 41.1 %copy-start.26 = (f32[1024]{0:T(1024)S(1)}, f32[1024]{0:T(1024)}, u32[]{:S(2)}) copy-start(f32[1024]{0:T(1024)} %param.24) | copy-start | bytes 12292
  102.9 41.1 %copy-start.39 = (f32[1024]{0:T(1024)S(1)}, f32[1024]{0:T(1024)}, u32[]{:S(2)}) copy-start(f32[1024]{0:T(1024)} %param.25) | copy-start | bytes 12292
  102.9 67.4 %all-gather.17.cloned.1.call-start = ((), (), s32[]{:S(2)}) async-start(), calls=%async_computation.14 | async-start | bytes 1966080 | tf_op jit(solution)/shard_map/all_gather | solution.py:131
  145.8 50.7 %all-gather.23.cloned.1.call-start = ((), (), s32[]{:S(2)}) async-start(), calls=%async_computation.20 | async-start | bytes 1966080 | tf_op jit(solution)/shard_map/all_gather | solution.py:151
  148.7 74.2 %all-gather.13.cloned.1.call-start = ((), (), s32[]{:S(2)}) async-start(), calls=%async_computation.10 | async-start | bytes 1966080 | tf_op jit(solution)/shard_map/all_gather | solution.py:131
  149.4 99.3 %all-gather.19.cloned.1.call-start = ((), (), s32[]{:S(2)}) async-start(), calls=%async_computation.16 | async-start | bytes 1966080 | tf_op jit(solution)/shard_map/all_gather | solution.py:151
  150.2 46.3 %copy-start.37 = (f32[2048]{0:T(1024)S(1)}, f32[2048]{0:T(1024)}, u32[]{:S(2)}) copy-start(f32[2048]{0:T(1024)} %param.27) | copy-start | bytes 24580
  150.2 163.0 %reduce-scatter.21.cloned.1.call-start = ((), (), s32[]{:S(2)}) async-start(), calls=%async_computation.21 | async-start | bytes 1966080 | tf_op jit(solution)/shard_map/reduce_scatter | solution.py:161
  210.2 102.9 %reduce-scatter.17.cloned.1.call-start = ((), (), s32[]{:S(2)}) async-start(), calls=%async_computation.17 | async-start | bytes 1966080 | tf_op jit(solution)/shard_map/reduce_scatter | solution.py:161
  261.8 65.0 %reduce-scatter.15.cloned.1.call-start = ((), (), s32[]{:S(2)}) async-start(), calls=%async_computation.15 | async-start | bytes 1966080 | tf_op jit(solution)/shard_map/reduce_scatter | solution.py:137
  262.3 28.6 %copy-start.44 = (bf16[2048,1024]{1,0:T(8,128)(2,1)S(1)}, bf16[2048,1024]{1,0:T(8,128)(2,1)}, u32[]{:S(2)}) copy-start(bf16[2048,1024]{1,0:T(8,128)(2,1)} %param.28) | copy-start | bytes 12582916
  294.9 57.3 %reduce-scatter.11.cloned.1.call-start = ((), (), s32[]{:S(2)}) async-start(), calls=%async_computation.11 | async-start | bytes 1966080 | tf_op jit(solution)/shard_map/reduce_scatter | solution.py:137
  302.0 76.7 %all-gather.25.cloned.1.call-start = ((), (), s32[]{:S(2)}) async-start(), calls=%async_computation.22 | async-start | bytes 1966080 | tf_op jit(solution)/shard_map/all_gather | solution.py:177
  313.2 13.7 %copy-start.36 = (f32[1024]{0:T(1024)S(1)}, f32[1024]{0:T(1024)}, u32[]{:S(2)}) copy-start(f32[1024]{0:T(1024)} %param.29) | copy-start | bytes 12292
  331.1 73.2 %all-gather.21.cloned.1.call-start = ((), (), s32[]{:S(2)}) async-start(), calls=%async_computation.18 | async-start | bytes 1966080 | tf_op jit(solution)/shard_map/all_gather | solution.py:177
  356.1 166.6 %reduce-scatter.23.cloned.1.call-start = ((), (), s32[]{:S(2)}) async-start(), calls=%async_computation.23 | async-start | bytes 1966080 | tf_op jit(solution)/shard_map/reduce_scatter | solution.py:214
  430.0 92.7 %reduce-scatter.19.cloned.1.call-start = ((), (), s32[]{:S(2)}) async-start(), calls=%async_computation.19 | async-start | bytes 1966080 | tf_op jit(solution)/shard_map/reduce_scatter | solution.py:214
  459.3 265.2 %all-reduce.7.cloned.1.call-start = ((), (), s32[]{:S(2)}) async-start(), calls=%async_computation.24 | async-start | bytes 25165824 | tf_op jit(solution)/shard_map/psum | solution.py:229
  459.8 10.2 %copy-start.49 = (bf16[2,320,1024]{2,1,0:T(8,128)(2,1)S(1)}, bf16[2,320,1024]{2,1,0:T(8,128)(2,1)}, u32[]{:S(2)}) copy-start(bf16[2,320,1024]{2,1,0:T(8,128)(2,1)} %all-gather.21.cloned.1.call-done) | copy-start | bytes 3932164
  459.8 10.2 %copy-start.55 = (bf16[2,8,64,320]{3,2,1,0:T(8,128)(2,1)S(1)}, bf16[2,8,64,320]{3,2,1,0:T(8,128)(2,1)}, u32[]{:S(2)}) copy-start(bf16[2,8,64,320]{3,2,1,0:T(8,128)(2,1)} %copy-done.54) | copy-start | bytes 1966084
  480.5 42.2 %copy-start.28 = (f32[320]{0:T(512)S(1)}, f32[320]{0:T(512)}, u32[]{:S(2)}) copy-start(f32[320]{0:T(512)} %copy-done.27) | copy-start | bytes 3844
  480.5 42.2 %copy-start.30 = (f32[320]{0:T(512)S(1)}, f32[320]{0:T(512)}, u32[]{:S(2)}) copy-start(f32[320]{0:T(512)} %copy-done.29) | copy-start | bytes 3844
  480.6 42.2 %copy-start.31 = (f32[1024]{0:T(1024)S(1)}, f32[1024]{0:T(1024)}, u32[]{:S(2)}) copy-start(f32[1024]{0:T(1024)} %param.18) | copy-start | bytes 12292
  480.6 42.2 %copy-start.33 = (f32[320]{0:T(512)S(1)}, f32[320]{0:T(512)}, u32[]{:S(2)}) copy-start(f32[320]{0:T(512)} %copy-done.32) | copy-start | bytes 3844
  480.6 42.2 %copy-start.35 = (f32[320]{0:T(512)S(1)}, f32[320]{0:T(512)}, u32[]{:S(2)}) copy-start(f32[320]{0:T(512)} %copy-done.34) | copy-start | bytes 3844
  (46 other events, 164.4 us)
Sparse Core Ops, SparseCore 0:
  13.3 26.9 all-gather.10
  42.5 24.2 all-gather.14
  90.3 23.1 reduce-scatter.12
  116.3 23.1 reduce-scatter.8
  145.9 24.2 all-gather.16
  172.2 24.2 all-gather.22
  198.6 24.2 all-gather.12
  224.5 24.2 all-gather.18
  251.6 23.1 reduce-scatter.20
  277.6 23.1 reduce-scatter.16
  303.6 23.1 reduce-scatter.14
  329.0 23.1 reduce-scatter.10
  354.3 24.2 all-gather.24
  380.0 24.2 all-gather.20
  430.1 23.1 reduce-scatter.22
  459.4 23.2 reduce-scatter.18
  488.3 236.1 all-reduce.6
where the time goes:
time: 760 us; the launch traced here: 751 us
  waiting for transfers between devices  334 us (44%)
  matrix products  170 us (22%)
  other arithmetic  91.5 us (12%)
  blocking collectives  84.7 us (11%)
  local copies, waits for them, and re-layouts  52.1 us (7%)
  between operations  15 us (2%)
    psum x1, waiting for transfers between devices, local(): lax.psum(grad_qkv.astype(jnp.bfloat16), 'dp').astype(jnp.float32)  155 us
    psum x1, blocking collectives, local(): lax.psum((grad_ln1_gain, grad_ln1_bias, grad_out_bias, grad_ln2_gain, gra...  39.5 us
    reduce_scatter x2, waiting for transfers between devices, local(): lax.psum_scatter(jnp.einsum('isd,de->ise', mixed_low, w_out, preferred_el...  36.6 us
    psum x1, blocking collectives, local(): lax.psum(grad_qv_bias.astype(jnp.bfloat16), 'dp').astype(jnp.float32)  35.7 us
    all_gather x2, waiting for transfers between devices, local(): norm2_all = lax.all_gather(norm2_low, 'tensor', axis=0, tiled=True)  32.5 us
    all_gather x2, waiting for transfers between devices, local(): lax.all_gather(norm1_low, 'tensor', axis=0, tiled=True)  31.2 us
    all_gather x2, waiting for transfers between devices, local(): grad_top_all = lax.all_gather(grad_top_low, 'tensor', axis=0, tiled=True)  29.3 us
    convert_element_type x1, other arithmetic, local(): act_low = jax.nn.gelu(pre_act, approximate=False).astype(bf16)  27 us
  transfers between devices with their start and end apart: 17, of which 13 were waited for; matrix products, arithmetic and copies ran while one was open for 30% of the time, Pallas kernels for 0%

commit v1 on v0

v1 whole, which is shorter than its diff:
```python
import functools

import jax
import jax.numpy as jnp
from jax import lax
from jax.experimental import pallas as pl
from jax.experimental.pallas import tpu as pltpu
from jax.sharding import Mesh, PartitionSpec as P

HD = 64
BUF = 64
EPS = 1e-06
CORES = 2
FAST = 192
LANES = 256
TILE = 512

f32 = jnp.float32
bf16 = jnp.bfloat16
NT = ((1,), (1,))
TN = ((0,), (0,))


def dot(a, b, dims=((1,), (0,))):
    return lax.dot_general(a, b, (dims, ((), ())), preferred_element_type=f32)


def spans(flags, seq_len, body):
    if seq_len <= FAST:
        body(seq_len)
        return

    @pl.when(flags[0] == 1)
    def _():
        body(FAST)

    @pl.when(flags[0] == 0)
    def _():
        body(seq_len)


def whole(shape):
    return pl.BlockSpec(shape, lambda *_: (0,) * len(shape), pipeline_mode=pl.Buffered(1))


def kernel_call(name, body, flags, args, in_specs, out_specs, out_shape, grid=(1,), **kw):
    return pl.pallas_call(
        body,
        name=name,
        grid_spec=pltpu.PrefetchScalarGridSpec(
            num_scalar_prefetch=1,
            grid=grid,
            in_specs=in_specs,
            out_specs=out_specs,
            scratch_shapes=kw.pop("scratch", ()),
        ),
        out_shape=out_shape,
        compiler_params=pltpu.CompilerParams(vmem_limit_bytes=kw.pop("vmem", 28 << 20)),
        cost_estimate=pl.CostEstimate(flops=1000, bytes_accessed=1000, transcendentals=0),
        **kw,
    )(flags, *args)


def picks(keep_row, span):
    seq_len = keep_row.shape[1]
    upto = lax.broadcasted_iota(jnp.int32, (seq_len, seq_len), 0) <= lax.broadcasted_iota(
        jnp.int32, (seq_len, seq_len), 1
    )
    keep_rows = jnp.broadcast_to(keep_row, (16, seq_len))
    rank = dot(keep_rows.astype(bf16), upto.astype(f32).astype(bf16))[0:1]
    place = lax.broadcasted_iota(jnp.int32, (span, seq_len), 0).astype(f32) + 1.0
    hit = jnp.where(place == rank, keep_row, 0.0)
    return hit.astype(bf16)


def norm_parts(values):
    centred = values - jnp.mean(values, axis=-1, keepdims=True)
    inverse = lax.rsqrt(jnp.mean(centred * centred, axis=-1, keepdims=True) + EPS)
    return centred * inverse, inverse


def norm_grad(grad_rows, unit, inverse, gain):
    scaled = grad_rows * gain
    centred = (
        scaled
        - jnp.mean(scaled, axis=-1, keepdims=True)
        - unit * jnp.mean(scaled * unit, axis=-1, keepdims=True)
    )
    return centred * inverse


def col_sum(values):
    return jnp.sum(values, axis=0, keepdims=True)


def prep_kernel(seq_len, images, flags, x, cot, keep, gain, bias, xc, normed, top, top_sum):
    def body(span):
        total = jnp.zeros(top_sum.shape, f32)
        for i in range(images):
            pick = picks(keep[i : i + 1, :], span)
            rows = slice(i * span, (i + 1) * span)
            source = slice(i * seq_len, (i + 1) * seq_len)
            kept = dot(pick, x[source, :])
            xc[rows, :] = kept.astype(bf16)
            normed[rows, :] = (norm_parts(kept)[0] * gain[...] + bias[...]).astype(bf16)
            grad = dot(pick, cot[source, :])
            top[rows, :] = grad.astype(bf16)
            total = total + col_sum(grad)
        top_sum[...] = total

    spans(flags, seq_len, body)


def head_masks(heads):
    lane = lax.broadcasted_iota(jnp.int32, (1, heads * HD), 1)
    return [(lane >= h * HD) & (lane < (h + 1) * HD) for h in range(heads)]


def softmax_rows(q, k, count):
    raw = dot(q, k, NT)
    column = lax.broadcasted_iota(jnp.int32, raw.shape, 1)
    raw = jnp.where(column < count, raw, -1e30)
    raised = jnp.exp(raw - jnp.max(raw, axis=-1, keepdims=True))
    return raised / jnp.sum(raised, axis=-1, keepdims=True)


def attend_kernel(seq_len, images, flags, normed, w, shift, proj, mixed):
    heads = mixed.shape[1] // HD

    def body(span):
        masks = head_masks(heads)
        for c in range(3):
            value = dot(normed[: images * span, :], w[c]) + shift[c]
            proj[c, : images * span, :] = value.astype(bf16)
        for i in range(images):
            rows = slice(i * span, (i + 1) * span)
            count = flags[1 + i]
            q, k, v = proj[0, rows, :], proj[1, rows, :], proj[2, rows, :]
            q = (q.astype(f32) * HD ** (-0.5)).astype(bf16)
            joined = jnp.zeros(q.shape, f32)
            for h in range(heads):
                probs = softmax_rows(jnp.where(masks[h], q, 0), k, count)
                joined = jnp.where(masks[h], dot(probs.astype(bf16), v), joined)
            mixed[rows, :] = joined.astype(bf16)

    spans(flags, seq_len, body)


def middle_kernel(seq_len, images, slots, flags, *refs):
    mixed, w, (xc, out_bias, gain, bias, mid, normed) = (
        refs[:slots],
        refs[slots : 2 * slots],
        refs[2 * slots :],
    )

    def body(span):
        for i in range(images):
            rows = slice(i * span, (i + 1) * span)
            total = xc[rows, :].astype(f32) + out_bias[...]
            for slot in range(slots):
                total = total + dot(mixed[slot][rows, :], w[slot][...])
            mid[rows, :] = total
            normed[rows, :] = (norm_parts(total)[0] * gain[...] + bias[...]).astype(bf16)

    spans(flags, seq_len, body)


def hidden_kernel(seq_len, images, flags, normed, w, bias, act, slope):
    def body(span):
        rows = images * span
        step = rows // 2
        for part in range(2):
            at = slice(part * step, (part + 1) * step)
            pre = dot(normed[at, :], w[...]) + bias[...]
            cdf = 0.5 * (1.0 + lax.erf(pre * 0.7071067811865476))
            act[at, :] = (pre * cdf).astype(bf16)
            slope[at, :] = (cdf + pre * jnp.exp(-0.5 * pre * pre) * 0.3989422804014327).astype(bf16)

    spans(flags, seq_len, body)


def ffn_kernel(seq_len, images, first, flags, act, slope, top, w2, w1, base, *refs):
    if first:
        total, grad_pre, grad_norm, sums = refs
        grad_base = None
    else:
        grad_base, total, grad_pre, grad_norm, sums = refs
    start = pl.program_id(0) == 0

    def body(span):
        rows = images * span

        @pl.when(start)
        def _():
            total[:rows, :] = base[:rows, :]
            if first:
                grad_norm[:rows, :] = jnp.zeros((rows, grad_norm.shape[1]), f32)
            else:
                grad_norm[:rows, :] = grad_base[:rows, :]

        total[:rows, :] += dot(act[:rows, :], w2[...])
        grad = dot(top[:rows, :], w2[...], NT) * slope[:rows, :].astype(f32)
        grad_pre[:rows, :] = grad.astype(bf16)
        sums[...] = col_sum(grad_pre[:rows, :].astype(f32))
        grad_norm[:rows, :] += dot(grad_pre[:rows, :], w1[...], NT)

    spans(flags, seq_len, body)


def mid_back_kernel(seq_len, images, flags, grad_norm, mid, top, gain, grad_mid, grad_attn, sums):
    def body(span):
        for i in range(images):
            rows = slice(i * span, (i + 1) * span)
            unit, inverse = norm_parts(mid[rows, :])
            grad = grad_norm[rows, :]
            full = top[rows, :].astype(f32) + norm_grad(grad, unit, inverse, gain[...])
            low = full.astype(bf16)
            grad_mid[rows, :] = full
            grad_attn[rows, :] = low
            part = [col_sum(grad * unit), col_sum(grad), col_sum(low.astype(f32))]
            for n, row in enumerate(part):
                sums[n : n + 1, :] = row if i == 0 else sums[n : n + 1, :] + row

    spans(flags, seq_len, body)


def attend_back_kernel(seq_len, images, first, flags, grad_attn, w_out, proj, w, *refs):
    if first:
        grad_proj, grad_norm, sums = refs
        base = None
    else:
        base, grad_proj, grad_norm, sums = refs
    heads = proj.shape[2] // HD
    start = pl.program_id(0) == 0

    def body(span):
        rows_all = images * span
        masks = head_masks(heads)

        @pl.when(start)
        def _():
            if first:
                grad_norm[:rows_all, :] = jnp.zeros((rows_all, grad_norm.shape[1]), f32)
            else:
                grad_norm[:rows_all, :] = base[:rows_all, :]

        for i in range(images):
            rows = slice(i * span, (i + 1) * span)
            count = flags[1 + i]
            grad_mixed = dot(grad_attn[rows, :], w_out[...], NT).astype(bf16)
            q, k, v = proj[0, rows, :], proj[1, rows, :], proj[2, rows, :]
            q_low = (q.astype(f32) * HD ** (-0.5)).astype(bf16)
            dq = jnp.zeros(q.shape, f32)
            dk, dv = dq, dq
            for h in range(heads):
                probs = softmax_rows(jnp.where(masks[h], q_low, 0), k, count)
                grad_prob = dot(jnp.where(masks[h], grad_mixed, 0), v, NT)
                delta = jnp.sum(probs * grad_prob, axis=-1, keepdims=True)
                grad_score = (probs * (grad_prob - delta)).astype(bf16)
                dv = jnp.where(masks[h], dot(probs.astype(bf16), grad_mixed, TN), dv)
                dq = jnp.where(masks[h], dot(grad_score, k), dq)
                dk = jnp.where(masks[h], dot(grad_score, q_low, TN), dk)
            grad_proj[0, rows, :] = (dq * HD ** (-0.5)).astype(bf16)
            grad_proj[1, rows, :] = dk.astype(bf16)
            grad_proj[2, rows, :] = dv.astype(bf16)
        for c in range(3):
            grad_norm[:rows_all, :] += dot(grad_proj[c, :rows_all, :], w[c], NT)
        sums[0:1, :] = col_sum(grad_proj[0, :rows_all, :].astype(f32))
        sums[1:2, :] = col_sum(grad_proj[2, :rows_all, :].astype(f32))

    spans(flags, seq_len, body)


def spread_kernel(seq_len, images, flags, value, bias, keep, out):
    def body(span):
        for i in range(images):
            rows = slice(i * span, (i + 1) * span)
            low = (value[rows, :] + bias[...]).astype(bf16)
            pick = picks(keep[i : i + 1, :], span)
            out[i * seq_len : (i + 1) * seq_len, :] = dot(pick, low, TN).astype(bf16)

    spans(flags, seq_len, body)


def last_kernel(seq_len, images, flags, grad_norm, xc, grad_mid, gain, keep, out, sums):
    def body(span):
        for i in range(images):
            rows = slice(i * span, (i + 1) * span)
            unit, inverse = norm_parts(xc[rows, :].astype(f32))
            grad = grad_norm[rows, :]
            low = (grad_mid[rows, :] + norm_grad(grad, unit, inverse, gain[...])).astype(bf16)
            pick = picks(keep[i : i + 1, :], span)
            out[i * seq_len : (i + 1) * seq_len, :] = dot(pick, low, TN).astype(bf16)
            part = [col_sum(grad * unit), col_sum(grad)]
            for n, row in enumerate(part):
                sums[n : n + 1, :] = row if i == 0 else sums[n : n + 1, :] + row

    spans(flags, seq_len, body)


def grad_kernel(seq_len, images, slots, flags, *refs):
    left, right, rest = refs[: len(slots)], refs[len(slots) : 2 * len(slots)], refs[2 * len(slots) :]
    out = rest[-1]

    def body(span):
        rows = images * span
        for n in range(len(slots)):
            value = dot(left[n][:rows, :], right[n][:rows, :], TN)
            for came in rest[:-1]:
                value = value + came[n].astype(f32)
            out[n] = value.astype(bf16)

    spans(flags, seq_len, body)


def last_grad_kernel(seq_len, images, first, slots, flags, normed, top, *refs):
    mixed, right, rest = (
        refs[: len(slots)],
        refs[len(slots) : 2 * len(slots)],
        refs[2 * len(slots) :],
    )
    out = rest[-1]

    def finish(n, value):
        for came in rest[:-1]:
            value = value + came[n, 0].astype(f32)
        out[n, 0] = value.astype(bf16)

    def body(span):
        rows = images * span
        which = first + pl.program_id(0)

        @pl.when(which == 0)
        def _():
            for n in range(len(slots)):
                finish(n, dot(top[:rows, :], mixed[n][:rows, :], TN))

        @pl.when(which > 0)
        def _():
            for n in range(len(slots)):
                finish(n, dot(normed[:rows, :], right[n][0, :rows, :], TN))

    spans(flags, seq_len, body)


def assemble_kernel(offsets, count, flags, *refs):
    pieces, out, sems = refs[:count], refs[count], refs[count + 1]
    copies = []
    for n, piece in enumerate(pieces):
        start = pl.multiple_of(offsets(flags)[n], 8)
        copy = pltpu.make_async_copy(piece, out.at[pl.ds(start, piece.shape[0]), :], sems.at[n])
        copy.start()
        copies.append(copy)
    for copy in copies:
        copy.wait()


def swap(value, axis, size, mask):
    return lax.ppermute(value, axis, [(i, i ^ mask) for i in range(size)])


def after(values, *waits):
    return lax.optimization_barrier((values, waits))[0]


def build(chips, tensor):
    def core_swap(value):
        return swap(value, "core", CORES, 1)

    def chip_swap(value, mask):
        return swap(value, "chip", chips, mask)

    def peer(value, slot):
        return swap(value, "tensor", tensor, slot)

    def local(
        inputs,
        keep_mask,
        cotangent,
        ln1_gain,
        ln1_bias,
        w_qkv,
        qv_bias,
        w_out,
        out_bias,
        ln2_gain,
        ln2_bias,
        w_fc1,
        fc1_bias,
        w_fc2,
        fc2_bias,
    ):
        images, seq_len, width = inputs.shape
        tokens = images * seq_len
        part = w_qkv.shape[2]
        hidden = w_fc1.shape[1]
        slots = range(tensor)
        others = range(1, tensor)
        lanes = min(LANES, part)
        tile = min(TILE, hidden)
        core, chip = lax.axis_index("core"), lax.axis_index("chip")
        low, high = chip & 1, (chip >> 1) & 1
        like = jax.ShapeDtypeStruct
        static = functools.partial
        row = lambda v: v.reshape(1, -1)

        keep = jnp.concatenate([jnp.ones((images, BUF), f32), keep_mask.astype(f32)], axis=1)
        counts = BUF + jnp.sum(keep_mask, axis=1)
        place = jnp.stack([core, low, high]).astype(jnp.int32)
        flags = jnp.concatenate([jnp.all(counts <= FAST).astype(jnp.int32)[None], counts, place])
        shape2 = (tokens, width)
        g1, b1, g2, b2 = row(ln1_gain), row(ln1_bias), row(ln2_gain), row(ln2_bias)


        class Box:
            def __init__(self, value):
                self.value = value
                opened.append(self)

        opened = []
        gate = Box(flags)

        def step():
            values = lax.optimization_barrier([box.value for box in opened])
            for box, value in zip(opened, values):
                box.value = value
            opened[:] = [gate]

        def run(name, body, args, in_specs, out_specs, out_shape, grid=(1,), **kw):
            args = [a.value if isinstance(a, Box) else a for a in args]
            got = kernel_call(
                name, body, gate.value, args, in_specs, out_specs, out_shape, grid, **kw
            )
            return [Box(g) for g in got] if isinstance(got, (list, tuple)) else Box(got)

        def start(move, value, *mask):
            value = value.value if isinstance(value, Box) else value
            return Box(move(after(value, gate.value), *mask))


        def assemble(pieces, offsets):
            rows = sum(p.value.shape[0] for p in pieces)
            shape = (rows, pieces[0].value.shape[1])
            return run(
                "assemble",
                static(assemble_kernel, offsets, len(pieces)),
                pieces,
                [pl.BlockSpec(memory_space=pl.ANY)] * len(pieces),
                whole(shape),
                like(shape, bf16),
                scratch=[pltpu.SemaphoreType.DMA((len(pieces),))],
            )

        class Fetch:
            def __init__(self, shard, mask):
                self.mask, self.rows = mask, shard.shape[0] // 4
                spot = core * 2 + (low if mask == 1 else high)
                piece = lax.dynamic_slice_in_dim(shard, spot * self.rows, self.rows, axis=0)
                self.mine = [start(peer, piece, slot) for slot in others]

            def second(self):
                self.beside = [start(chip_swap, m, self.mask) for m in self.mine]
                self.mine2 = [start(core_swap, m) for m in self.mine]

            def third(self):
                self.beside2 = [start(core_swap, m) for m in self.beside]

            def full(self):
                rows, at = self.rows, (2 if self.mask == 1 else 3) + images

                def offsets(f):
                    co, bit = f[1 + images], f[at]
                    return (
                        (2 * co + bit) * rows,
                        (2 * co + 1 - bit) * rows,
                        (2 * (1 - co) + bit) * rows,
                        (2 * (1 - co) + 1 - bit) * rows,
                    )

                return [
                    assemble(pieces, offsets)
                    for pieces in zip(self.mine, self.beside, self.mine2, self.beside2)
                ]


        half_of = lambda own: (lambda f: f[1 + images]) if own else (lambda f: 1 - f[1 + images])

        class Plain:
            def __init__(self, name, left, right, begin, size, block):
                self.name, self.left, self.right = name, left, right
                self.begin, self.size, self.block = begin, size, min(block, size)

            def make(self, which, own, came):
                pick = lambda v: [v[slot] if len(v) > 1 else v[0] for slot in which]
                left, right = pick(self.left), pick(self.right)
                block, first = self.block, self.begin // self.block
                per_half = left[0].value.shape[1] // 2 // block
                cols = right[0].value.shape[1]
                spot = pl.BlockSpec((len(which), block, cols), lambda g, f: (0, g, 0))
                half = half_of(own)
                return run(
                    f"{self.name}{which[0]}{'own' if own else 'away'}",
                    static(grad_kernel, seq_len, images, which),
                    (*left, *right, *came),
                    [
                        pl.BlockSpec((tokens, block), lambda g, f: (0, half(f) * per_half + first + g))
                        for _ in left
                    ]
                    + [whole((tokens, cols)) for _ in right]
                    + [spot] * len(came),
                    spot,
                    like((len(which), self.size, cols), bf16),
                    grid=(self.size // block,),
                )

        class Packed:
            def __init__(self, name, begin, size):
                self.name, self.begin, self.size = name, begin, size

            def make(self, which, own, came):
                begin, half = self.begin, half_of(own)
                mats = [mixes[slot] for slot in which]
                rights = [grad_projs[slot] for slot in which]
                spot = pl.BlockSpec((len(which), 1, width // 2, part), lambda g, f: (0, g, 0, 0))
                return run(
                    f"{self.name}{which[0]}{'own' if own else 'away'}",
                    static(last_grad_kernel, seq_len, images, begin, which),
                    (normed1, grad_attn, *mats, *rights, *came),
                    [pl.BlockSpec((tokens, width // 2), lambda g, f: (0, half(f)))] * 2
                    + [whole((tokens, part)) for _ in mats]
                    + [
                        pl.BlockSpec(
                            (1, tokens, part), lambda g, f: (jnp.maximum(begin + g - 1, 0), 0, 0)
                        )
                        for _ in rights
                    ]
                    + [spot] * len(came),
                    spot,
                    like((len(which), self.size, width // 2, part), bf16),
                    grid=(self.size,),
                )

        class Reduce:
            def __init__(self, source):
                self.source = source
                self.made, self.came, self.ready, self.sent = {}, {}, {}, []
                self.trail = []

            def k_away(self, *which):
                for slot in which:
                    self.made[slot] = self.source.make([slot], False, ())

            def t_core(self, *which):
                for slot in which:
                    self.came[slot] = start(core_swap, self.made[slot])

            def k_send(self):
                for slot in others:
                    self.ready[slot] = self.source.make([slot], True, (self.came[slot],))

            def t_x(self):
                self.sent = [start(peer, self.ready[slot], slot) for slot in others]

            def k_keep(self):
                total = self.source.make([0], True, (self.came[0], *self.sent))
                self.shape = total.value.shape
                self.held = total.value.reshape(-1, self.shape[-1])
                self.moving = None

            def settle(self):
                if self.moving is not None:
                    self.held = self.held.astype(f32) + self.moving.value.astype(f32)
                    self.moving = None

            def t_scatter(self, bit, mask):
                self.settle()
                size = self.held.shape[0] // 2
                sent = lax.dynamic_slice_in_dim(self.held, (1 - bit) * size, size).astype(bf16)
                self.held = lax.dynamic_slice_in_dim(self.held, bit * size, size)
                self.moving = start(chip_swap, sent, mask)

            def t_full(self):
                mask = 4
                while mask < chips:
                    self.settle()
                    self.held = self.held.astype(bf16)
                    self.moving = start(chip_swap, self.held, mask)
                    mask *= 2

            def t_y(self):
                self.t_scatter(low, 1)

            def t_z(self):
                self.t_scatter(high, 2)

            def t_up(self):
                self.settle()
                self.held = self.held.astype(bf16)
                self.moving = start(chip_swap, self.held, 2)

            def t_out(self):
                self.join(high)
                self.moving = start(chip_swap, self.held, 1)

            def join(self, bit):
                moving = self.moving.value
                self.held = jnp.where(
                    bit == 0,
                    jnp.concatenate([self.held, moving]),
                    jnp.concatenate([moving, self.held]),
                )

            def t_share(self):
                self.join(low)
                self.moving = start(core_swap, self.held)

        def joined(chunks):
            mine = [c.held for c in chunks]
            other = [c.moving.value for c in chunks]
            return jnp.where(
                core == 0, jnp.concatenate(mine + other), jnp.concatenate(other + mine)
            ).astype(f32)


        def attend(slot, w):
            qv = biases[slot].value[: 2 * part].reshape(2, 1, part)
            shift = jnp.stack([qv[0], jnp.zeros_like(qv[0]), qv[1]])
            return run(
                f"attend{slot}",
                static(attend_kernel, seq_len, images),
                (normed1, w, shift),
                [
                    whole(shape2),
                    pl.BlockSpec((3, width, lanes), lambda g, f: (0, 0, g)),
                    pl.BlockSpec((3, 1, lanes), lambda g, f: (0, 0, g)),
                ],
                [
                    pl.BlockSpec((3, tokens, lanes), lambda g, f: (0, 0, g)),
                    pl.BlockSpec((tokens, lanes), lambda g, f: (0, g)),
                ],
                [like((3, tokens, part), bf16), like((tokens, part), bf16)],
                grid=(part // lanes,),
            )

        def hide(slot):
            acts[slot], slopes[slot] = run(
                f"hidden{slot}",
                static(hidden_kernel, seq_len, images),
                (normed2, fc1[slot], row(biases[slot].value[2 * part :])),
                [
                    whole(shape2),
                    pl.BlockSpec((width, tile), lambda g, f: (0, g)),
                    pl.BlockSpec((1, tile), lambda g, f: (0, g)),
                ],
                [pl.BlockSpec((tokens, tile), lambda g, f: (0, g))] * 2,
                [like((tokens, hidden), bf16)] * 2,
                grid=(hidden // tile,),
            )

        def ffn(slot):
            nonlocal total, grad_norm2
            first = grad_norm2 is None
            tiles = pl.BlockSpec((tokens, tile), lambda g, f: (0, g))
            total, grad_pres[slot], grad_norm2, pre_sums[slot] = run(
                f"ffn{slot}",
                static(ffn_kernel, seq_len, images, first),
                (acts[slot], slopes[slot], top, fc2[slot], fc1[slot], total)
                + (() if first else (grad_norm2,)),
                [
                    tiles,
                    tiles,
                    whole(shape2),
                    pl.BlockSpec((tile, width), lambda g, f: (g, 0)),
                    pl.BlockSpec((width, tile), lambda g, f: (0, g)),
                    whole(shape2),
                ]
                + ([] if first else [whole(shape2)]),
                [whole(shape2), tiles, whole(shape2), pl.BlockSpec((1, tile), lambda g, f: (0, g))],
                [
                    like(shape2, f32),
                    like((tokens, hidden), bf16),
                    like(shape2, f32),
                    like((1, hidden), f32),
                ],
                grid=(hidden // tile,),
                vmem=36 << 20,
            )

        def attend_back(slot):
            nonlocal grad_norm1
            first = grad_norm1 is None
            tiles = pl.BlockSpec((3, tokens, lanes), lambda g, f: (0, 0, g))
            grad_projs[slot], grad_norm1, proj_sums[slot] = run(
                f"aback{slot}",
                static(attend_back_kernel, seq_len, images, first),
                (grad_attn, out[slot], projs[slot], qkv[slot]) + (() if first else (grad_norm1,)),
                [
                    whole(shape2),
                    pl.BlockSpec((lanes, width), lambda g, f: (g, 0)),
                    tiles,
                    pl.BlockSpec((3, width, lanes), lambda g, f: (0, 0, g)),
                ]
                + ([] if first else [whole(shape2)]),
                [tiles, whole(shape2), pl.BlockSpec((2, lanes), lambda g, f: (0, g))],
                [like((3, tokens, part), bf16), like(shape2, f32), like((2, part), f32)],
                grid=(part // lanes,),
            )

        acts, slopes = [None] * tensor, [None] * tensor
        total, grad_norm2 = None, None
        grad_pres, pre_sums = [None] * tensor, [None] * tensor
        grad_projs, proj_sums, grad_norm1 = [None] * tensor, [None] * tensor, None


        small = jnp.concatenate([qv_bias.reshape(-1), fc1_bias])
        get_qkv = Fetch(w_qkv.reshape(3 * width, part), 1)
        get_out = Fetch(w_out, 1)
        biases = [Box(small)] + [start(peer, small, slot) for slot in others]
        xc, normed1, top, top_sum = run(
            "prep",
            static(prep_kernel, seq_len, images),
            (inputs.reshape(shape2), cotangent.reshape(shape2), keep, g1, b1),
            [whole(shape2), whole(shape2), whole(keep.shape), whole(g1.shape), whole(b1.shape)],
            [whole(shape2), whole(shape2), whole(shape2), whole((1, width))],
            [like(shape2, bf16), like(shape2, bf16), like(shape2, bf16), like((1, width), f32)],
        )
        seen = [attend(0, w_qkv)]
        step()

        get_qkv.second()
        get_out.second()
        get_fc1 = Fetch(w_fc1, 2)
        step()

        get_qkv.third()
        get_out.third()
        get_fc1.second()
        get_fc2 = Fetch(w_fc2, 1)
        qkv = [w_qkv] + [w.value.reshape(3, width, part) for w in get_qkv.full()]
        for slot in others:
            seen.append(attend(slot, qkv[slot]))
        projs, mixes = [s[0] for s in seen], [s[1] for s in seen]
        out = [w_out] + get_out.full()
        mid, normed2 = run(
            "middle",
            static(middle_kernel, seq_len, images, tensor),
            (*mixes, *out, xc, row(out_bias), g2, b2),
            [whole((tokens, part))] * tensor
            + [whole((part, width))] * tensor
            + [whole(shape2), whole((1, width)), whole((1, width)), whole((1, width))],
            [whole(shape2), whole(shape2)],
            [like(shape2, f32), like(shape2, bf16)],
        )
        step()

        get_fc1.third()
        get_fc2.second()
        fc1 = [w_fc1] + get_fc1.full()
        for slot in others:
            hide(slot)
        rest = hidden // 4
        w1 = [Reduce(Plain(f"fc2{n}", acts, [top], n * rest, rest, TILE)) for n in range(2)]
        for p in w1:
            p.k_away(*others)
        step()

        for p in w1:
            p.t_core(*others)
        get_fc2.third()
        hide(0)
        fc2 = [w_fc2] + get_fc2.full()
        for p in w1:
            p.k_send()
        step()


        total = mid
        rest = width // 4
        w2 = [
            Reduce(Plain(f"fc1{n}", [normed2], grad_pres, n * rest, rest, 256)) for n in range(2)
        ]
        w1[0].t_x()
        for slot in others:
            ffn(slot)
        for p in w2:
            p.k_away(*others)
        for p in w1:
            p.k_away(0)
        step()

        w1[1].t_x()
        for p in w2:
            p.t_core(*others)
        for p in w1:
            p.t_core(0)
        ffn(0)
        for p in w2:
            p.k_send()
        w1[0].k_keep()
        step()

        w2[0].t_x()
        w1[0].t_y()
        w1[1].k_keep()
        grad_mid, grad_attn, sums2 = run(
            "midback",
            static(mid_back_kernel, seq_len, images),
            (grad_norm2, mid, top, g2),
            [whole(shape2), whole(shape2), whole(shape2), whole((1, width))],
            [whole(shape2), whole(shape2), whole((3, width))],
            [like(shape2, f32), like(shape2, bf16), like((3, width), f32)],
        )
        for slot in others:
            attend_back(slot)
        for p in w2:
            p.k_away(0)
        w3 = [Reduce(Packed("qkv0", 0, 2)), Reduce(Packed("qkv1", 2, 2))]
        for p in w3:
            p.k_away(*others)
        step()

        w2[1].t_x()
        w1[1].t_y()
        w1[0].t_z()
        for p in w2:
            p.t_core(0)
        for p in w3:
            p.t_core(*others)
        attend_back(0)
        for p in w3:
            p.k_send()
        w2[0].k_keep()
        step()

        w3[0].t_x()
        w2[0].t_y()
        w1[1].t_z()
        w1[0].t_full()
        w2[1].k_keep()
        for p in w3:
            p.k_away(0)
        grad_input, sums1 = run(
            "last",
            static(last_kernel, seq_len, images),
            (grad_norm1, xc, grad_mid, g1, keep),
            [whole(shape2), whole(shape2), whole(shape2), whole((1, width)), whole(keep.shape)],
            [whole(shape2), whole((2, width))],
            [like(shape2, bf16), like((2, width), f32)],
        )
        step()

        w3[1].t_x()
        for p in w3:
            p.t_core(0)
        w2[1].t_y()
        w2[0].t_z()
        w1[1].t_full()
        w1[0].t_up()
        w3[0].k_keep()
        layer_out = run(
            "spread",
            static(spread_kernel, seq_len, images),
            (total, row(fc2_bias), keep),
            [whole(shape2), whole((1, width)), whole(keep.shape)],
            whole(shape2),
            like(shape2, bf16),
        )
        step()

        w3[0].t_y()
        w2[1].t_z()
        w2[0].t_full()
        w1[1].t_up()
        w1[0].t_out()
        w3[1].k_keep()
        step()

        w3[1].t_y()
        w3[0].t_z()
        w2[1].t_full()
        w2[0].t_up()
        w1[1].t_out()
        w1[0].t_share()
        step()

        w3[1].t_z()
        w3[0].t_full()
        w2[1].t_up()
        w2[0].t_out()
        w1[1].t_share()
        step()

        w3[1].t_full()
        w3[0].t_up()
        w2[1].t_out()
        w2[0].t_share()
        step()

        w3[1].t_up()
        w3[0].t_out()
        w2[1].t_share()
        step()

        w3[1].t_out()
        w3[0].t_share()
        step()

        w3[1].t_share()
        grad_fc2, grad_fc1 = joined(w1), joined(w2)

        def unpacked(chunk):
            mine = chunk.held.reshape(-1, width // 2, part)
            other = chunk.moving.value.reshape(-1, width // 2, part)
            return jnp.where(
                core == 0,
                jnp.concatenate([mine, other], axis=1),
                jnp.concatenate([other, mine], axis=1),
            ).astype(f32)

        packs = [unpacked(p) for p in w3]
        grad_out = packs[0][0].T
        grad_qkv = jnp.concatenate([packs[0][1:], packs[1]])
        layer_out = layer_out.value.reshape(inputs.shape)
        grad_input = grad_input.value.reshape(inputs.shape)
        sums1, sums2, top_sum = sums1.value, sums2.value, top_sum.value
        proj_sums = [p.value for p in proj_sums]
        pre_sums = [p.value for p in pre_sums]

        common = jnp.concatenate([sums1.reshape(-1), sums2[2], sums2[0], sums2[1], top_sum[0]])
        owned = [
            jnp.concatenate([proj_sums[slot].reshape(-1), pre_sums[slot].reshape(-1), common])
            for slot in slots
        ]
        vector = owned[0]
        for slot in others:
            vector = vector + peer(owned[slot], slot)
        vector = vector + core_swap(vector)
        mask = 1
        while mask < chips:
            vector = vector + chip_swap(vector, mask)
            mask *= 2
        grad_qv_bias = vector[: 2 * part].reshape(2, part)
        grad_fc1_bias = vector[2 * part : 2 * part + hidden]
        rest = vector[2 * part + hidden :].reshape(6, width)
        return (
            layer_out,
            grad_input,
            rest[0],
            rest[1],
            grad_qkv,
            grad_qv_bias,
            grad_out,
            rest[2],
            rest[3],
            rest[4],
            grad_fc1,
            grad_fc1_bias,
            grad_fc2,
            rest[5],
        )

    return local


def solution(mesh):
    chips, tensor = mesh.shape["dp"] // CORES, mesh.shape["tensor"]
    finer = Mesh(mesh.devices.reshape(chips, CORES, tensor), ("chip", "core", "tensor"))
    rows = ("chip", "core", "tensor")
    return jax.shard_map(
        build(chips, tensor),
        mesh=finer,
        in_specs=(
            P(rows, None, None),
            P(rows, None),
            P(rows, None, None),
            P(),
            P(),
            P(None, None, "tensor"),
            P(None, "tensor"),
            P("tensor", None),
            P(),
            P(),
            P(),
            P(None, "tensor"),
            P("tensor"),
            P("tensor", None),
            P(),
        ),
        out_specs=(
            P(rows, None, None),
            P(rows, None, None),
            P(),
            P(),
            P(None, None, "tensor"),
            P(None, "tensor"),
            P("tensor", None),
            P(),
            P(),
            P(),
            P(None, "tensor"),
            P("tensor"),
            P("tensor", None),
            P(),
        ),
        check_vma=False,
    )
```

time: 760 us -> 466 us (0.61)
  waiting for transfers between devices: 334 us -> 135 us
  matrix products: 170 us -> 0 us
  Pallas kernels: 0 us -> 136 us
  blocking collectives: 84.7 us -> 0 us
  starting transfers between devices: 2.53 us -> 64.4 us
  other arithmetic: 91.5 us -> 59.6 us
  between operations: 15 us -> 2.88 us
  local copies, waits for them, and re-layouts: 52.1 us -> 62.8 us
    dot_general x36 -> x0, matrix products: 170 us -> none  [the longest x2 22.8 us: local(): jnp.einsum('isd,df->isf', norm2_all, fc1_use, preferred_element_type=f32)]
    psum x1 -> x0, waiting for transfers between devices: 155 us -> none  [local(): lax.psum(grad_qkv.astype(jnp.bfloat16), 'dp').astype(jnp.float32)]
    pallas_call x0 -> x41, Pallas kernels: none -> 136 us  [kernel_call(): pl.pallas_call(body, name=name, grid_spec=pltpu.PrefetchScalarGridSpec(nu...]
    ppermute x0 -> x76, waiting for transfers between devices: none -> 135 us  [swap(): return lax.ppermute(value, axis, [(i, i ^ mask) for i in range(size)])]
    all_gather x8 -> x0, waiting for transfers between devices: 118 us -> none  [the longest x2 32.5 us: local(): norm2_all = lax.all_gather(norm2_low, 'tensor', axis=0, tiled=True)]
    psum x2 -> x0, blocking collectives: 75.2 us -> none  [the longest x1 39.5 us: local(): lax.psum((grad_ln1_gain, grad_ln1_bias, grad_out_bias, grad_ln2_gain, gra...]
    ppermute x0 -> x76, starting transfers between devices: none -> 64.4 us  [swap(): return lax.ppermute(value, axis, [(i, i ^ mask) for i in range(size)])]
    reduce_scatter x8 -> x0, waiting for transfers between devices: 58.7 us -> none  [the longest x2 36.6 us: local(): lax.psum_scatter(jnp.einsum('isd,de->ise', mixed_low, w_out, preferred_el...]
  transfers between devices with their start and end apart: 17 -> 76, of which waited for: 13 -> 29; matrix products, arithmetic and copies ran while one was open for 30% -> 15% of each run, Pallas kernels for 0% -> 29%
where the time goes in v1:
time: 466 us; the launch traced here: 461 us
  Pallas kernels  136 us (29%)
  waiting for transfers between devices  135 us (29%)
  starting transfers between devices  64.4 us (14%)
  local copies, waits for them, and re-layouts  62.8 us (13%)
  other arithmetic  59.6 us (13%)
    pallas_call x41, Pallas kernels, kernel_call(): pl.pallas_call(body, name=name, grid_spec=pltpu.PrefetchScalarGridSpec(nu...  136 us
    ppermute x76, waiting for transfers between devices, swap(): return lax.ppermute(value, axis, [(i, i ^ mask) for i in range(size)])  135 us
    ppermute x76, starting transfers between devices, swap(): return lax.ppermute(value, axis, [(i, i ^ mask) for i in range(size)])  64.4 us
    unnamed x220, local copies, waits for them, and re-layouts  40.1 us
    select_n x12, other arithmetic, join(): jnp.where(bit == 0, jnp.concatenate([self.held, moving]), jnp.concatenate...  16.5 us
    convert_element_type x2, other arithmetic, joined(): return jnp.where(core == 0, jnp.concatenate(mine + other), jnp.concatenat...  12.3 us
  transfers between devices with their start and end apart: 76, of which 29 were waited for; matrix products, arithmetic and copies ran while one was open for 15% of the time, Pallas kernels for 29%

profile of v1, /device:TPU:0, one launch (start us, length us, event | category | flops | bytes accessed | tf_op | source)
XLA Modules:
  0.0 461.4 jit_solution(4421686215769994303)
XLA Ops:
  5.0 2.9 collective-permute-start
  25.4 6.0 %attend0.1 = (bf16[3,640,512]{2,1,0:T(8,128)(2,1)S(1)}, bf16[640,512]{1,0:T(8,128)(2,1)S(1)}) custom-call(s32[6]{0:T(128)S(1)} %concatenate.117.flags, bf16[640,1024]{1,0:T(8,128)(2,1)S(1)} %get-tuple-element.266.normed, bf16[3,1024,512]{2,1,0:T(8,128)(2,1)S(1)} %copy-done.27, f32[3,1,512]{2,1,0:T(1,128)S(1)} %pad_maximum_fusion.1.shift), custom_call_target="tpu_custom_call" | custom-call | flops 1000 | bytes 1000 | tf_op jit(solution)/shard_map/attend0/pallas_call | solution.py:47
  37.0 20.4 %collective-permute-done.5.refs_1_ = bf16[128,1024]{1,0:T(8,128)(2,1)} collective-permute-done((bf16[128,1024]{1,0:T(8,128)(2,1)S(1)}, bf16[128,1024]{1,0:T(8,128)(2,1)}, u32[]{:S(2)}, u32[]{:S(2)}) %collective-permute-start.5) | collective-permute-done | bytes 262176 | tf_op jit(solution)/shard_map/ppermute | solution.py:359
  67.4 6.0 %attend1.1 = (bf16[3,640,512]{2,1,0:T(8,128)(2,1)S(1)}, bf16[640,512]{1,0:T(8,128)(2,1)S(1)}) custom-call(s32[6]{0:T(128)S(1)} %concatenate.117.flags, bf16[640,1024]{1,0:T(8,128)(2,1)S(1)} %get-tuple-element.266.normed, bf16[3,1024,512]{2,1,0:T(8,128)(2,1)S(1)} %bitcast.71, f32[3,1,512]{2,1,0:T(1,128)S(1)} %pad_maximum_fusion.2.shift), custom_call_target="tpu_custom_call" | custom-call | flops 1000 | bytes 1000 | tf_op jit(solution)/shard_map/attend1/pallas_call | solution.py:47
  76.9 3.6 collective-permute-done.10.refs_1_
  80.5 4.2 collective-permute-done.12.refs_0_
  89.2 4.8 %hidden1.1 = (bf16[640,2048]{1,0:T(8,128)(2,1)S(1)}, bf16[640,2048]{1,0:T(8,128)(2,1)S(1)}) custom-call(s32[6]{0:T(128)S(1)} %concatenate.117.flags, bf16[640,1024]{1,0:T(8,128)(2,1)S(1)} %get-tuple-element.281.normed.refs_0_, bf16[1024,2048]{1,0:T(8,128)(2,1)S(1)} %assemble.6.w.w1, f32[1,2048]{1,0:T(1,128)S(1)} %bitcast.80), custom_call_target="tpu_custom_call" | custom-call | flops 1000 | bytes 1000 | tf_op jit(solution)/shard_map/hidden1/pallas_call | solution.py:47
  96.7 13.6 %collective-permute-done.14.refs_1_ = bf16[512,1024]{1,0:T(8,128)(2,1)S(1)} collective-permute-done((bf16[512,1024]{1,0:T(8,128)(2,1)S(1)}, bf16[512,1024]{1,0:T(8,128)(2,1)S(1)}, u32[]{:S(2)}, u32[]{:S(2)}) %collective-permute-start.14) | collective-permute-done | bytes 1048608 | tf_op jit(solution)/shard_map/ppermute | solution.py:359
  111.5 4.8 %hidden0.1 = (bf16[640,2048]{1,0:T(8,128)(2,1)S(1)}, bf16[640,2048]{1,0:T(8,128)(2,1)S(1)}) custom-call(s32[6]{0:T(128)S(1)} %concatenate.117.flags, bf16[640,1024]{1,0:T(8,128)(2,1)S(1)} %get-tuple-element.281.normed.refs_0_, bf16[1024,2048]{1,0:T(8,128)(2,1)S(1)} %copy-done.22, f32[1,2048]{1,0:T(1,128)S(1)} %bitcast.81), custom_call_target="tpu_custom_call" | custom-call | flops 1000 | bytes 1000 | tf_op jit(solution)/shard_map/hidden0/pallas_call | solution.py:47
  124.8 8.9 %ffn1.1 = (f32[640,1024]{1,0:T(8,128)S(1)}, bf16[640,2048]{1,0:T(8,128)(2,1)S(1)}, f32[640,1024]{1,0:T(8,128)S(1)}, f32[1,2048]{1,0:T(1,128)S(1)}) custom-call(s32[6]{0:T(128)S(1)} %concatenate.117.flags, bf16[640,2048]{1,0:T(8,128)(2,1)S(1)} %get-tuple-element.296.refs_0_.act, bf16[640,2048]{1,0:T(8,128)(2,1)S(1)} %get-tuple-element.300.slope, ...), custom_call_target="tpu_custom_call" | custom-call | flops 1000 | bytes 1000 | tf_op jit(solution)/shard_map/ffn1/pallas_call | solution.py:47
  140.2 8.7 %collective-permute-done.19.refs_3_ = bf16[1,512,1024]{2,1,0:T(8,128)(2,1)S(1)} collective-permute-done((bf16[1,512,1024]{2,1,0:T(8,128)(2,1)S(1)}, bf16[1,512,1024]{2,1,0:T(8,128)(2,1)S(1)}, u32[]{:S(2)}, u32[]{:S(2)}) %collective-permute-start.19) | collective-permute-done | bytes 1048608 | tf_op jit(solution)/shard_map/ppermute | solution.py:359
  152.3 9.6 %ffn0.1 = (f32[640,1024]{1,0:T(8,128)S(1)}, bf16[640,2048]{1,0:T(8,128)(2,1)S(1)}, f32[640,1024]{1,0:T(8,128)S(1)}, f32[1,2048]{1,0:T(1,128)S(1)}) custom-call(s32[6]{0:T(128)S(1)} %concatenate.117.flags, bf16[640,2048]{1,0:T(8,128)(2,1)S(1)} %get-tuple-element.308.refs_0_.act, bf16[640,2048]{1,0:T(8,128)(2,1)S(1)} %get-tuple-element.320.slope, ...), custom_call_target="tpu_custom_call" | custom-call | flops 1000 | bytes 1000 | tf_op jit(solution)/shard_map/ffn0/pallas_call | solution.py:47
  164.8 3.5 fc111own.1
  171.8 3.0 collective-permute-done.20.refs_3_
  191.2 10.9 %aback1.1 = (bf16[3,640,512]{2,1,0:T(8,128)(2,1)S(1)}, f32[640,1024]{1,0:T(8,128)S(1)}, f32[2,512]{1,0:T(2,128)S(1)}) custom-call(s32[6]{0:T(128)S(1)} %concatenate.117.flags, bf16[640,1024]{1,0:T(8,128)(2,1)S(1)} %get-tuple-element.360.grad_attn.top, bf16[512,1024]{1,0:T(8,128)(2,1)S(1)} %copy-done.32, bf16[3,640,512]{2,1,0:T(8,128)(2,1)S(1)} %copy-done.63, ...), custom_call_target="tpu_custom_call" | custom-call | flops 1000 | bytes 1000 | tf_op jit(solution)/shard_map/aback1/pallas_call | solution.py:47
  226.6 11.0 %aback0.1 = (bf16[3,640,512]{2,1,0:T(8,128)(2,1)S(1)}, f32[640,1024]{1,0:T(8,128)S(1)}, f32[2,512]{1,0:T(2,128)S(1)}) custom-call(s32[6]{0:T(128)S(1)} %concatenate.117.flags, bf16[640,1024]{1,0:T(8,128)(2,1)S(1)} %copy-done.4, bf16[512,1024]{1,0:T(8,128)(2,1)S(1)} %copy-done.34, bf16[3,640,512]{2,1,0:T(8,128)(2,1)S(1)} %copy-done.61, ...), custom_call_target="tpu_custom_call" | custom-call | flops 1000 | bytes 1000 | tf_op jit(solution)/shard_map/aback0/pallas_call | solution.py:47
  240.5 3.6 qkv11own.1
  265.3 3.1 fc110own.1
  268.9 3.3 last.1
  281.3 3.6 collective-permute-done.42
  316.0 8.5 %collective-permute-done.52 = bf16[64,2048]{1,0:T(8,128)(2,1)S(1)} collective-permute-done((bf16[64,2048]{1,0:T(8,128)(2,1)}, bf16[64,2048]{1,0:T(8,128)(2,1)S(1)}, u32[]{:S(2)}, u32[]{:S(2)}) %collective-permute-start.52) | collective-permute-done | bytes 262176 | tf_op jit(solution)/shard_map/ppermute | solution.py:359
  342.9 8.5 %collective-permute-done.57 = bf16[64,2048]{1,0:T(8,128)(2,1)} collective-permute-done((bf16[64,2048]{1,0:T(8,128)(2,1)}, bf16[64,2048]{1,0:T(8,128)(2,1)}, u32[]{:S(2)}, u32[]{:S(2)}) %collective-permute-start.57) | collective-permute-done | bytes 262176 | tf_op jit(solution)/shard_map/ppermute | solution.py:359
  351.4 4.0 collective-permute-done.58
  365.5 8.8 %collective-permute-done.62 = bf16[256,512]{1,0:T(8,128)(2,1)S(1)} collective-permute-done((bf16[256,512]{1,0:T(8,128)(2,1)S(1)}, bf16[256,512]{1,0:T(8,128)(2,1)S(1)}, u32[]{:S(2)}, u32[]{:S(2)}) %collective-permute-start.62) | collective-permute-done | bytes 262176 | tf_op jit(solution)/shard_map/ppermute | solution.py:359
  381.6 11.2 %collective-permute-done.66 = bf16[256,512]{1,0:T(8,128)(2,1)S(1)} collective-permute-done((bf16[256,512]{1,0:T(8,128)(2,1)S(1)}, bf16[256,512]{1,0:T(8,128)(2,1)S(1)}, u32[]{:S(2)}, u32[]{:S(2)}) %collective-permute-start.66) | collective-permute-done | bytes 262176 | tf_op jit(solution)/shard_map/ppermute | solution.py:359
  404.5 6.6 %collective-permute-done.47 = f32[9216]{0:T(1024)S(1)} collective-permute-done((f32[9216]{0:T(1024)S(1)}, f32[9216]{0:T(1024)S(1)}, u32[]{:S(2)}, u32[]{:S(2)}) %collective-permute-start.47) | collective-permute-done | bytes 36896 | tf_op jit(solution)/shard_map/ppermute | solution.py:359
  416.2 3.8 collective-permute-done.49
  427.7 5.7 %fusion.1 = f32[2048,1024]{1,0:T(8,128)} fusion(bf16[512,1024]{1,0:T(8,128)(2,1)} %collective-permute-done.65, bf16[512,1024]{1,0:T(8,128)(2,1)} %collective-permute-done.60, bf16[512,1024]{1,0:T(8,128)(2,1)S(1)} %maximum_select_fusion.5, bf16[512,1024]{1,0:T(8,128)(2,1)S(1)} %maximum_select_fusion.4, pred[]{:T(512)S(6)} %eq.6), kind=kLoop, calls=%fused_computation.4 | loop fusion | flops 37748736 | bytes 12582913 | tf_op jit(solution)/shard_map/convert_element_type | solution.py:622
  433.4 6.9 %collective-permute-done.73 = bf16[512,512]{1,0:T(8,128)(2,1)S(1)} collective-permute-done((bf16[512,512]{1,0:T(8,128)(2,1)S(1)}, bf16[512,512]{1,0:T(8,128)(2,1)S(1)}, u32[]{:S(2)}, u32[]{:S(2)}) %collective-permute-start.73) | collective-permute-done | bytes 524320 | tf_op jit(solution)/shard_map/ppermute | solution.py:359
  441.8 6.6 %fusion = f32[1024,2048]{1,0:T(8,128)} fusion(bf16[256,2048]{1,0:T(8,128)(2,1)} %collective-permute-done.72, bf16[256,2048]{1,0:T(8,128)(2,1)} %collective-permute-done.69, bf16[256,2048]{1,0:T(8,128)(2,1)} %maximum_select_fusion.7, bf16[256,2048]{1,0:T(8,128)(2,1)S(1)} %maximum_select_fusion.6, pred[]{:T(512)S(6)} %eq.6), kind=kLoop, calls=%fused_computation.2 | loop fusion | flops 37748736 | bytes 12582913 | tf_op jit(solution)/shard_map/convert_element_type | solution.py:622
  454.7 3.0 fusion.3
  457.7 3.4 pad_maximum_fusion
  (455 shorter events, 246.0 us)
Async XLA Ops:
  5.0 27.7 %collective-permute-start = (bf16[768,512]{1,0:T(8,128)(2,1)}, bf16[768,512]{1,0:T(8,128)(2,1)}, u32[]{:S(2)}, u32[]{:S(2)}) collective-permute-start(bf16[768,512]{1,0:T(8,128)(2,1)} %constant_dynamic-slice_fusion.5), channel_id=1, source_target_pairs={{0,1},{1,0},{2,3},{3,2},{4,5},{5,4},{6,7},{7,6},{8,9},{9,8},{10,11... | collective-permute-start | bytes 2359304 | tf_op jit(solution)/shard_map/ppermute | solution.py:359
  9.6 23.1 %collective-permute-start.1 = (bf16[128,1024]{1,0:T(8,128)(2,1)}, bf16[128,1024]{1,0:T(8,128)(2,1)S(1)}, u32[]{:S(2)}, u32[]{:S(2)}) collective-permute-start(bf16[128,1024]{1,0:T(8,128)(2,1)} %constant_dynamic-slice_fusion.4), channel_id=1, source_target_pairs={{0,1},{1,0},{2,3},{3,2},{4,5},{5,4},{6,7},{7,6},{8,9},{9,8},{10,11... | collective-permute-start | bytes 786440 | tf_op jit(solution)/shard_map/ppermute | solution.py:359
  32.7 24.7 %collective-permute-start.7 = (bf16[256,2048]{1,0:T(8,128)(2,1)}, bf16[256,2048]{1,0:T(8,128)(2,1)}, u32[]{:S(2)}, u32[]{:S(2)}) collective-permute-start(bf16[256,2048]{1,0:T(8,128)(2,1)} %constant_dynamic-slice_fusion.3), channel_id=1, source_target_pairs={{0,1},{1,0},{2,3},{3,2},{4,5},{5,4},{6,7},{7,6},{8,9},{9,8},{10,11... | collective-permute-start | bytes 3145736 | tf_op jit(solution)/shard_map/ppermute | solution.py:359
  33.4 24.0 %collective-permute-start.3 = (bf16[768,512]{1,0:T(8,128)(2,1)}, bf16[768,512]{1,0:T(8,128)(2,1)}, u32[]{:S(2)}, u32[]{:S(2)}) collective-permute-start(bf16[768,512]{1,0:T(8,128)(2,1)} %collective-permute-done.refs_0_), channel_id=1, source_target_pairs={{0,4},{4,0},{8,12},{12,8},{16,20},{20,16},{24,28},{28,24},{1,5},{5... | collective-permute-start | bytes 2359304 | tf_op jit(solution)/shard_map/ppermute | solution.py:359
  34.9 22.4 %collective-permute-start.4 = (bf16[768,512]{1,0:T(8,128)(2,1)}, bf16[768,512]{1,0:T(8,128)(2,1)}, u32[]{:S(2)}, u32[]{:S(2)}) collective-permute-start(bf16[768,512]{1,0:T(8,128)(2,1)} %collective-permute-done.refs_0_), channel_id=1, source_target_pairs={{0,2},{2,0},{1,3},{3,1},{4,6},{6,4},{5,7},{7,5},{8,10},{10,8},{9,1... | collective-permute-start | bytes 2359304 | tf_op jit(solution)/shard_map/ppermute | solution.py:359
  35.0 22.4 %collective-permute-start.5 = (bf16[128,1024]{1,0:T(8,128)(2,1)S(1)}, bf16[128,1024]{1,0:T(8,128)(2,1)}, u32[]{:S(2)}, u32[]{:S(2)}) collective-permute-start(bf16[128,1024]{1,0:T(8,128)(2,1)S(1)} %collective-permute-done.1.refs_0_), channel_id=1, source_target_pairs={{0,4},{4,0},{8,12},{12,8},{16,20},{20,16},{24,28},{28,24},{1,5},{5... | collective-permute-start | bytes 786440 | tf_op jit(solution)/shard_map/ppermute | solution.py:359
  35.5 21.9 %collective-permute-start.6 = (bf16[128,1024]{1,0:T(8,128)(2,1)S(1)}, bf16[128,1024]{1,0:T(8,128)(2,1)}, u32[]{:S(2)}, u32[]{:S(2)}) collective-permute-start(bf16[128,1024]{1,0:T(8,128)(2,1)S(1)} %collective-permute-done.1.refs_0_), channel_id=1, source_target_pairs={{0,2},{2,0},{1,3},{3,1},{4,6},{6,4},{5,7},{7,5},{8,10},{10,8},{9,1... | collective-permute-start | bytes 786440 | tf_op jit(solution)/shard_map/ppermute | solution.py:359
  57.4 23.1 %collective-permute-start.10 = (bf16[256,2048]{1,0:T(8,128)(2,1)}, bf16[256,2048]{1,0:T(8,128)(2,1)S(1)}, u32[]{:S(2)}, u32[]{:S(2)}) collective-permute-start(bf16[256,2048]{1,0:T(8,128)(2,1)} %collective-permute-done.7.refs_0_), channel_id=1, source_target_pairs={{0,8},{4,12},{8,0},{12,4},{16,24},{20,28},{24,16},{28,20},{1,9},{5... | collective-permute-start | bytes 3145736 | tf_op jit(solution)/shard_map/ppermute | solution.py:359
  59.1 25.6 %collective-permute-start.12 = (bf16[512,1024]{1,0:T(8,128)(2,1)S(1)}, bf16[512,1024]{1,0:T(8,128)(2,1)S(1)}, u32[]{:S(2)}, u32[]{:S(2)}) collective-permute-start(bf16[512,1024]{1,0:T(8,128)(2,1)S(1)} %constant_dynamic-slice_fusion.2), channel_id=1, source_target_pairs={{0,1},{1,0},{2,3},{3,2},{4,5},{5,4},{6,7},{7,6},{8,9},{9,8},{10,11... | collective-permute-start | bytes 3145736 | tf_op jit(solution)/shard_map/ppermute | solution.py:359
  84.7 25.6 %collective-permute-start.14 = (bf16[512,1024]{1,0:T(8,128)(2,1)S(1)}, bf16[512,1024]{1,0:T(8,128)(2,1)S(1)}, u32[]{:S(2)}, u32[]{:S(2)}) collective-permute-start(bf16[512,1024]{1,0:T(8,128)(2,1)S(1)} %collective-permute-done.12.refs_0_), channel_id=1, source_target_pairs={{0,4},{4,0},{8,12},{12,8},{16,20},{20,16},{24,28},{28,24},{1,5},{5... | collective-permute-start | bytes 3145736 | tf_op jit(solution)/shard_map/ppermute | solution.py:359
  86.2 24.1 %collective-permute-start.15 = (bf16[512,1024]{1,0:T(8,128)(2,1)S(1)}, bf16[512,1024]{1,0:T(8,128)(2,1)S(1)}, u32[]{:S(2)}, u32[]{:S(2)}) collective-permute-start(bf16[512,1024]{1,0:T(8,128)(2,1)S(1)} %collective-permute-done.12.refs_0_), channel_id=1, source_target_pairs={{0,2},{2,0},{1,3},{3,1},{4,6},{6,4},{5,7},{7,5},{8,10},{10,8},{9,1... | collective-permute-start | bytes 3145736 | tf_op jit(solution)/shard_map/ppermute | solution.py:359
  123.3 25.5 %collective-permute-start.19 = (bf16[1,512,1024]{2,1,0:T(8,128)(2,1)S(1)}, bf16[1,512,1024]{2,1,0:T(8,128)(2,1)S(1)}, u32[]{:S(2)}, u32[]{:S(2)}) collective-permute-start(bf16[1,512,1024]{2,1,0:T(8,128)(2,1)S(1)} %fc201own.1), channel_id=1, source_target_pairs={{0,1},{1,0},{2,3},{3,2},{4,5},{5,4},{6,7},{7,6},{8,9},{9,8},{10,11... | collective-permute-start | bytes 3145736 | tf_op jit(solution)/shard_map/ppermute | solution.py:359
  149.8 25.0 %collective-permute-start.20 = (bf16[1,512,1024]{2,1,0:T(8,128)(2,1)}, bf16[1,512,1024]{2,1,0:T(8,128)(2,1)S(1)}, u32[]{:S(2)}, u32[]{:S(2)}) collective-permute-start(bf16[1,512,1024]{2,1,0:T(8,128)(2,1)} %fc211own.1), channel_id=1, source_target_pairs={{0,1},{1,0},{2,3},{3,2},{4,5},{5,4},{6,7},{7,6},{8,9},{9,8},{10,11... | collective-permute-start | bytes 3145736 | tf_op jit(solution)/shard_map/ppermute | solution.py:359
  151.8 24.0 %collective-permute-start.24 = (bf16[1,512,1024]{2,1,0:T(8,128)(2,1)S(1)}, bf16[1,512,1024]{2,1,0:T(8,128)(2,1)S(1)}, u32[]{:S(2)}, u32[]{:S(2)}) collective-permute-start(bf16[1,512,1024]{2,1,0:T(8,128)(2,1)S(1)} %fc210away.1), channel_id=1, source_target_pairs={{0,2},{2,0},{1,3},{3,1},{4,6},{6,4},{5,7},{7,5},{8,10},{10,8},{9,1... | collective-permute-start | bytes 3145736 | tf_op jit(solution)/shard_map/ppermute | solution.py:359
  176.8 33.0 %collective-permute-start.25 = (bf16[1,256,2048]{2,1,0:T(8,128)(2,1)}, bf16[1,256,2048]{2,1,0:T(8,128)(2,1)}, u32[]{:S(2)}, u32[]{:S(2)}) collective-permute-start(bf16[1,256,2048]{2,1,0:T(8,128)(2,1)} %fc101own.1), channel_id=1, source_target_pairs={{0,1},{1,0},{2,3},{3,2},{4,5},{5,4},{6,7},{7,6},{8,9},{9,8},{10,11... | collective-permute-start | bytes 3145736 | tf_op jit(solution)/shard_map/ppermute | solution.py:359
  179.3 30.5 %collective-permute-start.26 = (bf16[256,1024]{1,0:T(8,128)(2,1)S(1)}, bf16[256,1024]{1,0:T(8,128)(2,1)S(1)}, u32[]{:S(2)}, u32[]{:S(2)}) collective-permute-start(bf16[256,1024]{1,0:T(8,128)(2,1)S(1)} %dynamic-slice_bitcast_fusion.3), channel_id=1, source_target_pairs={{0,4},{4,0},{8,12},{12,8},{16,20},{20,16},{24,28},{28,24},{1,5},{5... | collective-permute-start | bytes 1572872 | tf_op jit(solution)/shard_map/ppermute | solution.py:359
  211.1 33.1 %collective-permute-start.30 = (bf16[1,256,2048]{2,1,0:T(8,128)(2,1)}, bf16[1,256,2048]{2,1,0:T(8,128)(2,1)}, u32[]{:S(2)}, u32[]{:S(2)}) collective-permute-start(bf16[1,256,2048]{2,1,0:T(8,128)(2,1)} %fc100away.1), channel_id=1, source_target_pairs={{0,2},{2,0},{1,3},{3,1},{4,6},{6,4},{5,7},{7,5},{8,10},{10,8},{9,1... | collective-permute-start | bytes 3145736 | tf_op jit(solution)/shard_map/ppermute | solution.py:359
  211.1 36.0 %collective-permute-start.27 = (bf16[1,256,2048]{2,1,0:T(8,128)(2,1)}, bf16[1,256,2048]{2,1,0:T(8,128)(2,1)}, u32[]{:S(2)}, u32[]{:S(2)}) collective-permute-start(bf16[1,256,2048]{2,1,0:T(8,128)(2,1)} %fc111own.1), channel_id=1, source_target_pairs={{0,1},{1,0},{2,3},{3,2},{4,5},{5,4},{6,7},{7,6},{8,9},{9,8},{10,11... | collective-permute-start | bytes 3145736 | tf_op jit(solution)/shard_map/ppermute | solution.py:359
  211.7 35.4 %collective-permute-start.31 = (bf16[1,256,2048]{2,1,0:T(8,128)(2,1)}, bf16[1,256,2048]{2,1,0:T(8,128)(2,1)}, u32[]{:S(2)}, u32[]{:S(2)}) collective-permute-start(bf16[1,256,2048]{2,1,0:T(8,128)(2,1)} %fc110away.1), channel_id=1, source_target_pairs={{0,2},{2,0},{1,3},{3,1},{4,6},{6,4},{5,7},{7,5},{8,10},{10,8},{9,1... | collective-permute-start | bytes 3145736 | tf_op jit(solution)/shard_map/ppermute | solution.py:359
  214.9 32.2 %collective-permute-start.28 = (bf16[256,1024]{1,0:T(8,128)(2,1)}, bf16[256,1024]{1,0:T(8,128)(2,1)}, u32[]{:S(2)}, u32[]{:S(2)}) collective-permute-start(bf16[256,1024]{1,0:T(8,128)(2,1)} %dynamic-slice_bitcast_fusion.2), channel_id=1, source_target_pairs={{0,4},{4,0},{8,12},{12,8},{16,20},{20,16},{24,28},{28,24},{1,5},{5... | collective-permute-start | bytes 1572872 | tf_op jit(solution)/shard_map/ppermute | solution.py:359
  218.4 28.6 %collective-permute-start.29 = (bf16[128,1024]{1,0:T(8,128)(2,1)}, bf16[128,1024]{1,0:T(8,128)(2,1)}, u32[]{:S(2)}, u32[]{:S(2)}) collective-permute-start(bf16[128,1024]{1,0:T(8,128)(2,1)} %dynamic-slice_convert_fusion.5), channel_id=1, source_target_pairs={{0,8},{4,12},{8,0},{12,4},{16,24},{20,28},{24,16},{28,20},{1,9},{5... | collective-permute-start | bytes 786440 | tf_op jit(solution)/shard_map/ppermute | solution.py:359
  247.1 25.9 %collective-permute-start.34 = (bf16[1,2,512,512]{3,2,1,0:T(8,128)(2,1)}, bf16[1,2,512,512]{3,2,1,0:T(8,128)(2,1)}, u32[]{:S(2)}, u32[]{:S(2)}) collective-permute-start(bf16[1,2,512,512]{3,2,1,0:T(8,128)(2,1)} %qkv01own.1), channel_id=1, source_target_pairs={{0,1},{1,0},{2,3},{3,2},{4,5},{5,4},{6,7},{7,6},{8,9},{9,8},{10,11... | collective-permute-start | bytes 3145736 | tf_op jit(solution)/shard_map/ppermute | solution.py:359
  248.6 24.4 %collective-permute-start.35 = (bf16[128,2048]{1,0:T(8,128)(2,1)}, bf16[128,2048]{1,0:T(8,128)(2,1)}, u32[]{:S(2)}, u32[]{:S(2)}) collective-permute-start(bf16[128,2048]{1,0:T(8,128)(2,1)} %dynamic-slice_bitcast_fusion.1), channel_id=1, source_target_pairs={{0,4},{4,0},{8,12},{12,8},{16,20},{20,16},{24,28},{28,24},{1,5},{5... | collective-permute-start | bytes 1572872 | tf_op jit(solution)/shard_map/ppermute | solution.py:359
  273.1 27.0 %collective-permute-start.38 = (bf16[1,2,512,512]{3,2,1,0:T(8,128)(2,1)}, bf16[1,2,512,512]{3,2,1,0:T(8,128)(2,1)}, u32[]{:S(2)}, u32[]{:S(2)}) collective-permute-start(bf16[1,2,512,512]{3,2,1,0:T(8,128)(2,1)} %qkv11own.1), channel_id=1, source_target_pairs={{0,1},{1,0},{2,3},{3,2},{4,5},{5,4},{6,7},{7,6},{8,9},{9,8},{10,11... | collective-permute-start | bytes 3145736 | tf_op jit(solution)/shard_map/ppermute | solution.py:359
  274.6 25.4 %collective-permute-start.40 = (bf16[1,2,512,512]{3,2,1,0:T(8,128)(2,1)}, bf16[1,2,512,512]{3,2,1,0:T(8,128)(2,1)}, u32[]{:S(2)}, u32[]{:S(2)}) collective-permute-start(bf16[1,2,512,512]{3,2,1,0:T(8,128)(2,1)} %qkv10away.1), channel_id=1, source_target_pairs={{0,2},{2,0},{1,3},{3,1},{4,6},{6,4},{5,7},{7,5},{8,10},{10,8},{9,1... | collective-permute-start | bytes 3145736 | tf_op jit(solution)/shard_map/ppermute | solution.py:359
  275.2 24.9 %collective-permute-start.41 = (bf16[128,2048]{1,0:T(8,128)(2,1)}, bf16[128,2048]{1,0:T(8,128)(2,1)}, u32[]{:S(2)}, u32[]{:S(2)}) collective-permute-start(bf16[128,2048]{1,0:T(8,128)(2,1)} %dynamic-slice_bitcast_fusion), channel_id=1, source_target_pairs={{0,4},{4,0},{8,12},{12,8},{16,20},{20,16},{24,28},{28,24},{1,5},{5... | collective-permute-start | bytes 1572872 | tf_op jit(solution)/shard_map/ppermute | solution.py:359
  303.9 21.7 %collective-permute-start.50 = (bf16[512,512]{1,0:T(8,128)(2,1)}, bf16[512,512]{1,0:T(8,128)(2,1)}, u32[]{:S(2)}, u32[]{:S(2)}) collective-permute-start(bf16[512,512]{1,0:T(8,128)(2,1)} %get-tuple-element.409), channel_id=1, source_target_pairs={{0,4},{4,0},{8,12},{12,8},{16,20},{20,16},{24,28},{28,24},{1,5},{5... | collective-permute-start | bytes 1572872 | tf_op jit(solution)/shard_map/ppermute | solution.py:359
  328.0 27.4 %collective-permute-start.55 = (bf16[512,512]{1,0:T(8,128)(2,1)}, bf16[512,512]{1,0:T(8,128)(2,1)}, u32[]{:S(2)}, u32[]{:S(2)}) collective-permute-start(bf16[512,512]{1,0:T(8,128)(2,1)} %get-tuple-element.422), channel_id=1, source_target_pairs={{0,4},{4,0},{8,12},{12,8},{16,20},{20,16},{24,28},{28,24},{1,5},{5... | collective-permute-start | bytes 1572872 | tf_op jit(solution)/shard_map/ppermute | solution.py:359
  334.0 21.4 %collective-permute-start.60 = (bf16[512,1024]{1,0:T(8,128)(2,1)S(1)}, bf16[512,1024]{1,0:T(8,128)(2,1)}, u32[]{:S(2)}, u32[]{:S(2)}) collective-permute-start(bf16[512,1024]{1,0:T(8,128)(2,1)S(1)} %maximum_select_fusion.4), channel_id=1, source_target_pairs={{0,2},{2,0},{1,3},{3,1},{4,6},{6,4},{5,7},{7,5},{8,10},{10,8},{9,1... | collective-permute-start | bytes 3145736 | tf_op jit(solution)/shard_map/ppermute | solution.py:359
  394.8 25.8 %collective-permute-start.72 = (bf16[256,2048]{1,0:T(8,128)(2,1)}, bf16[256,2048]{1,0:T(8,128)(2,1)}, u32[]{:S(2)}, u32[]{:S(2)}) collective-permute-start(bf16[256,2048]{1,0:T(8,128)(2,1)} %maximum_select_fusion.7), channel_id=1, source_target_pairs={{0,2},{2,0},{1,3},{3,1},{4,6},{6,4},{5,7},{7,5},{8,10},{10,8},{9,1... | collective-permute-start | bytes 3145736 | tf_op jit(solution)/shard_map/ppermute | solution.py:359
  395.8 24.8 %collective-permute-start.71 = (bf16[512,512]{1,0:T(8,128)(2,1)}, bf16[512,512]{1,0:T(8,128)(2,1)}, u32[]{:S(2)}, u32[]{:S(2)}) collective-permute-start(bf16[512,512]{1,0:T(8,128)(2,1)} %maximum_select_fusion.14), channel_id=1, source_target_pairs={{0,4},{4,0},{8,12},{12,8},{16,20},{20,16},{24,28},{28,24},{1,5},{5... | collective-permute-start | bytes 1572872 | tf_op jit(solution)/shard_map/ppermute | solution.py:359
  397.3 23.3 %collective-permute-start.70 = (bf16[256,512]{1,0:T(8,128)(2,1)S(1)}, bf16[256,512]{1,0:T(8,128)(2,1)}, u32[]{:S(2)}, u32[]{:S(2)}) collective-permute-start(bf16[256,512]{1,0:T(8,128)(2,1)S(1)} %add_convert_fusion), channel_id=1, source_target_pairs={{0,8},{4,12},{8,0},{12,4},{16,24},{20,28},{24,16},{28,20},{1,9},{5... | collective-permute-start | bytes 786440 | tf_op jit(solution)/shard_map/ppermute | solution.py:359
  (148 other events, 1271.0 us)

commit v2 on v1

--- a/solution.py
+++ b/solution.py
@@ -343,16 +343,50 @@
     spans(flags, seq_len, body)
 
 
-def assemble_kernel(offsets, count, flags, *refs):
-    pieces, out, sems = refs[:count], refs[count], refs[count + 1]
+def assemble_kernel(spots, units, count, flags, *refs):
+    pieces, outs, sems = refs[:count], refs[count:-1], refs[-1]
     copies = []
-    for n, piece in enumerate(pieces):
-        start = pl.multiple_of(offsets(flags)[n], 8)
-        copy = pltpu.make_async_copy(piece, out.at[pl.ds(start, piece.shape[0]), :], sems.at[n])
-        copy.start()
-        copies.append(copy)
+    for piece, places in zip(pieces, spots(flags)):
+        begin = 0
+        for out in outs:
+            rows = out.shape[0] // units
+            for c in range(0, out.shape[1], piece.shape[1]):
+                for place in places:
+                    copy = pltpu.make_async_copy(
+                        piece.at[pl.ds(begin, rows), :],
+                        out.at[
+                            pl.ds(pl.multiple_of(place * rows, 16), rows), pl.ds(c, piece.shape[1])
+                        ],
+                        sems.at[len(copies)],
+                    )
+                    copy.start()
+                    copies.append(copy)
+                    begin += rows
     for copy in copies:
         copy.wait()
+
+
+def place_kernel(count, flags, *refs):
+    out = refs[count]
+    for n in range(count):
+
+        @pl.when(pl.program_id(0) == n)
+        def _():
+            out[...] = refs[n][...].astype(out.dtype)
+
+
+def last_place_kernel(matrix, count, flags, *refs):
+    pieces, (out, qkv) = refs[:count], refs[count:]
+    for n in range(count):
+        which = matrix(n, flags)
+
+        @pl.when((pl.program_id(0) == n) & (which == 0))
+        def _():
+            out[...] = pieces[n][...].astype(f32).T
+
+        @pl.when((pl.program_id(0) == n) & (which > 0))
+        def _():
+            qkv[0] = pieces[n][...].astype(f32)
 
 
 def swap(value, axis, size, mask):
@@ -438,90 +472,115 @@
             return Box(move(after(value, gate.value), *mask))
 
 
-        def assemble(pieces, offsets):
-            rows = sum(p.value.shape[0] for p in pieces)
-            shape = (rows, pieces[0].value.shape[1])
-            return run(
-                "assemble",
-                static(assemble_kernel, offsets, len(pieces)),
-                pieces,
-                [pl.BlockSpec(memory_space=pl.ANY)] * len(pieces),
-                whole(shape),
-                like(shape, bf16),
-                scratch=[pltpu.SemaphoreType.DMA((len(pieces),))],
-            )
-
         class Fetch:
-            def __init__(self, shard, mask):
-                self.mask, self.rows = mask, shard.shape[0] // 4
-                spot = core * 2 + (low if mask == 1 else high)
-                piece = lax.dynamic_slice_in_dim(shard, spot * self.rows, self.rows, axis=0)
+            def __init__(self, shards, split):
+                self.split, self.shards = split, shards
+                units = self.units = 8 if split else 4
+                own = self.places(core, low, high)[0]
+                cols = min(w.shape[1] for w in shards)
+                parts = []
+                for w in shards:
+                    rows = w.shape[0] // units
+                    for c in range(0, w.shape[1], cols):
+                        for place in own:
+                            parts.append(
+                                lax.dynamic_slice(w, (place * rows, c), (rows, min(cols, w.shape[1])))
+                            )
+                piece = jnp.concatenate(parts) if len(parts) > 1 else parts[0]
                 self.mine = [start(peer, piece, slot) for slot in others]
 
+            def places(self, co, lo, hi):
+                if self.split:
+                    return [(4 * co + lo, 4 * co + 2 + hi), (4 * co + 1 - lo,), (4 * co + 3 - hi,)]
+                return [(2 * co + lo,), (2 * co + 1 - lo,)]
+
             def second(self):
-                self.beside = [start(chip_swap, m, self.mask) for m in self.mine]
-                self.mine2 = [start(core_swap, m) for m in self.mine]
+                self.got = []
+                for m in self.mine:
+                    if self.split:
+                        rows = m.value.shape[0] // 2
+                        beside = [
+                            start(chip_swap, m.value[:rows], 1),
+                            start(chip_swap, m.value[rows:], 2),
+                        ]
+                    else:
+                        beside = [start(chip_swap, m, 1)]
+                    self.got.append([m, *beside, start(core_swap, m)])
 
             def third(self):
-                self.beside2 = [start(core_swap, m) for m in self.beside]
+                for got in self.got:
+                    got += [start(core_swap, g) for g in got[1:-1]]
 
             def full(self):
-                rows, at = self.rows, (2 if self.mask == 1 else 3) + images
-
-                def offsets(f):
-                    co, bit = f[1 + images], f[at]
-                    return (
-                        (2 * co + bit) * rows,
-                        (2 * co + 1 - bit) * rows,
-                        (2 * (1 - co) + bit) * rows,
-                        (2 * (1 - co) + 1 - bit) * rows,
+                shapes = [w.shape for w in self.shards]
+
+                def spots(f):
+                    co, lo, hi = f[1 + images], f[2 + images], f[3 + images]
+                    return self.places(co, lo, hi) + self.places(1 - co, lo, hi)
+
+                return [
+                    run(
+                        "assemble",
+                        static(assemble_kernel, spots, self.units, len(got)),
+                        got,
+                        [pl.BlockSpec(memory_space=pl.ANY)] * len(got),
+                        [whole(shape) for shape in shapes],
+                        [like(shape, bf16) for shape in shapes],
+                        scratch=[pltpu.SemaphoreType.DMA((16,))],
                     )
-
-                return [
-                    assemble(pieces, offsets)
-                    for pieces in zip(self.mine, self.beside, self.mine2, self.beside2)
+                    for got in self.got
                 ]
 
 
         half_of = lambda own: (lambda f: f[1 + images]) if own else (lambda f: 1 - f[1 + images])
 
         class Plain:
-            def __init__(self, name, left, right, begin, size, block):
-                self.name, self.left, self.right = name, left, right
-                self.begin, self.size, self.block = begin, size, min(block, size)
-
-            def make(self, which, own, came):
+            def __init__(self, name, left, right, block):
+                self.name, self.left, self.right, self.block = name, left, right, block
+
+            def make(self, which, own, came, begin=0, share=1):
                 pick = lambda v: [v[slot] if len(v) > 1 else v[0] for slot in which]
                 left, right = pick(self.left), pick(self.right)
-                block, first = self.block, self.begin // self.block
-                per_half = left[0].value.shape[1] // 2 // block
+                half_rows = left[0].value.shape[1] // 2
+                size = half_rows // share
+                block = min(self.block, size)
+                first, per_half = begin * size // block, half_rows // block
                 cols = right[0].value.shape[1]
-                spot = pl.BlockSpec((len(which), block, cols), lambda g, f: (0, g, 0))
                 half = half_of(own)
+                shape = (len(which), block, cols)
+                spots = [
+                    pl.BlockSpec(shape, lambda g, f, s=s, r=r: (s, r * (size // block) + g, 0))
+                    for _, s, r in came
+                ]
                 return run(
                     f"{self.name}{which[0]}{'own' if own else 'away'}",
                     static(grad_kernel, seq_len, images, which),
-                    (*left, *right, *came),
+                    (*left, *right, *[c for c, _, _ in came]),
                     [
                         pl.BlockSpec((tokens, block), lambda g, f: (0, half(f) * per_half + first + g))
                         for _ in left
                     ]
                     + [whole((tokens, cols)) for _ in right]
-                    + [spot] * len(came),
-                    spot,
-                    like((len(which), self.size, cols), bf16),
-                    grid=(self.size // block,),
+                    + spots,
+                    pl.BlockSpec(shape, lambda g, f: (0, g, 0)),
+                    like((len(which), size, cols), bf16),
+                    grid=(size // block,),
                 )
 
         class Packed:
-            def __init__(self, name, begin, size):
-                self.name, self.begin, self.size = name, begin, size
-
-            def make(self, which, own, came):
-                begin, half = self.begin, half_of(own)
+            name = "qkv"
+
+            def make(self, which, own, came, begin=0, share=1):
+                size = 4 // share
+                begin, half = begin * size, half_of(own)
                 mats = [mixes[slot] for slot in which]
                 rights = [grad_projs[slot] for slot in which]
-                spot = pl.BlockSpec((len(which), 1, width // 2, part), lambda g, f: (0, g, 0, 0))
+                shape = (len(which), 1, width // 2, part)
+                spots = [
+                    pl.BlockSpec(shape, lambda g, f, s=s, r=r: (s, r * size + g, 0, 0))
+                    for _, s, r in came
+                ]
+                came = [c for c, _, _ in came]
                 return run(
                     f"{self.name}{which[0]}{'own' if own else 'away'}",
                     static(last_grad_kernel, seq_len, images, begin, which),
@@ -534,92 +593,181 @@
                         )
                         for _ in rights
                     ]
-                    + [spot] * len(came),
-                    spot,
-                    like((len(which), self.size, width // 2, part), bf16),
-                    grid=(self.size,),
+                    + spots,
+                    pl.BlockSpec(shape, lambda g, f: (0, g, 0, 0)),
+                    like((len(which), size, width // 2, part), bf16),
+                    grid=(size,),
                 )
 
         class Reduce:
             def __init__(self, source):
                 self.source = source
-                self.made, self.came, self.ready, self.sent = {}, {}, {}, []
-                self.trail = []
-
-            def k_away(self, *which):
-                for slot in which:
-                    self.made[slot] = self.source.make([slot], False, ())
-
-            def t_core(self, *which):
-                for slot in which:
-                    self.came[slot] = start(core_swap, self.made[slot])
-
-            def k_send(self):
-                for slot in others:
-                    self.ready[slot] = self.source.make([slot], True, (self.came[slot],))
-
-            def t_x(self):
-                self.sent = [start(peer, self.ready[slot], slot) for slot in others]
-
-            def k_keep(self):
-                total = self.source.make([0], True, (self.came[0], *self.sent))
-                self.shape = total.value.shape
-                self.held = total.value.reshape(-1, self.shape[-1])
-                self.moving = None
-
-            def settle(self):
-                if self.moving is not None:
-                    self.held = self.held.astype(f32) + self.moving.value.astype(f32)
-                    self.moving = None
-
-            def t_scatter(self, bit, mask):
-                self.settle()
-                size = self.held.shape[0] // 2
-                sent = lax.dynamic_slice_in_dim(self.held, (1 - bit) * size, size).astype(bf16)
-                self.held = lax.dynamic_slice_in_dim(self.held, bit * size, size)
-                self.moving = start(chip_swap, sent, mask)
+
+            def k_away(self):
+                self.made = self.source.make([*slots], False, ())
+
+            def t_core(self):
+                self.came = start(core_swap, self.made)
+
+            def k_own(self):
+                make, came = self.source.make, self.came
+                self.first = [make([slot], True, [(came, slot, 0)], 0, 2) for slot in others]
+                self.second = make([*slots], True, [(came, 0, 1)], 1, 2)
+
+            def t_one(self):
+                self.sent = [start(peer, value, slot) for value, slot in zip(self.first, others)]
+                total = self.second.value
+                total = total.reshape(tensor, -1, total.shape[-1])
+                sent, self.held_b = halves(total, low, 1)
+                self.moving_b = start(chip_swap, sent, 1)
+
+            def k_mid(self):
+                came = [(self.came, 0, 0)] + [(sent, 0, 0) for sent in self.sent]
+                self.total = self.source.make([0], True, came, 0, 2)
+
+            def t_two(self):
+                total = self.total.value
+                sent, self.held_a = halves(total.reshape(-1, total.shape[-1]), low, 0)
+                self.moving_a = start(chip_swap, sent, 1)
+                total = self.held_b.astype(f32) + self.moving_b.value.astype(f32)
+                self.held_b = total[0]
+                self.moving_b = [start(peer, total[slot].astype(bf16), slot) for slot in others]
+
+            def t_z(self):
+                total_a = self.held_a.astype(f32) + self.moving_a.value.astype(f32)
+                total_b = self.held_b
+                for moving in self.moving_b:
+                    total_b = total_b + moving.value.astype(f32)
+                self.held = jnp.where(high == 0, total_a, total_b)
+                sent = jnp.where(high == 0, total_b, total_a).astype(bf16)
+                self.moving = start(chip_swap, sent, 2)
 
             def t_full(self):
                 mask = 4
                 while mask < chips:
-                    self.settle()
-                    self.held = self.held.astype(bf16)
+                    self.held = (self.held.astype(f32) + self.moving.value.astype(f32)).astype(bf16)
                     self.moving = start(chip_swap, self.held, mask)
                     mask *= 2
 
-            def t_y(self):
-                self.t_scatter(low, 1)
-
-            def t_z(self):
-                self.t_scatter(high, 2)
-
             def t_up(self):
-                self.settle()
-                self.held = self.held.astype(bf16)
+                self.held = (self.held.astype(f32) + self.moving.value.astype(f32)).astype(bf16)
                 self.moving = start(chip_swap, self.held, 2)
 
             def t_out(self):
-                self.join(high)
+                self.held = ordered(high, self.held, self.moving.value)
                 self.moving = start(chip_swap, self.held, 1)
 
-            def join(self, bit):
-                moving = self.moving.value
-                self.held = jnp.where(
-                    bit == 0,
-                    jnp.concatenate([self.held, moving]),
-                    jnp.concatenate([moving, self.held]),
+            def t_share(self):
+                pieces = [self.held, self.moving.value]
+                self.pieces = pieces + [start(core_swap, p) for p in pieces]
+
+            def joined(self):
+                pieces = self.pieces
+                rows, cols = pieces[0].shape
+                rows //= 2
+
+                def spot(n):
+                    return lambda w, i, f: (jnp.where(w == n, i, jnp.where(w < n, 0, 1)), 0)
+
+                def place(w, i, f):
+                    half = f[1 + images] ^ (w // 2)
+                    return (half * 4 + i * 2 + (f[2 + images] ^ (w % 2)), 0)
+
+                return run(
+                    f"{self.source.name}join",
+                    static(place_kernel, 4),
+                    pieces,
+                    [pl.BlockSpec((rows, cols), spot(n)) for n in range(4)],
+                    pl.BlockSpec((rows, cols), place),
+                    like((8 * rows, cols), f32),
+                    grid=(4, 2),
                 )
 
+        def halves(value, bit, axis):
+            size = value.shape[axis] // 2
+            return (
+                lax.dynamic_slice_in_dim(value, (1 - bit) * size, size, axis=axis),
+                lax.dynamic_slice_in_dim(value, bit * size, size, axis=axis),
+            )
+
+        class Apart(Reduce):
+            def t_one(self):
+                self.sent = [start(peer, value, slot) for value, slot in zip(self.first, others)]
+                total = self.second.value
+                total = total.reshape(tensor, -1, total.shape[-1])
+                sent, self.held_b = halves(total, high, 1)
+                self.moving_b = start(chip_swap, sent, 2)
+
+            def t_three(self):
+                total_a = self.held_a.astype(f32) + self.moving_a.value.astype(f32)
+                sent_a, self.held_a = halves(total_a, high, 0)
+                total_b = self.held_b
+                for moving in self.moving_b:
+                    total_b = total_b + moving.value.astype(f32)
+                sent_b, self.held_b = halves(total_b, low, 0)
+                self.moving_a = start(chip_swap, sent_a.astype(bf16), 2)
+                self.moving_b = start(chip_swap, sent_b.astype(bf16), 1)
+
+            def t_full(self):
+                held = [
+                    h.astype(f32) + m.value.astype(f32)
+                    for h, m in ((self.held_a, self.moving_a), (self.held_b, self.moving_b))
+                ]
+                self.held = jnp.concatenate(held).astype(bf16)
+                self.moving = start(chip_swap, self.held, 4)
+                mask = 8
+                while mask < chips:
+                    self.held = (self.held.astype(f32) + self.moving.value.astype(f32)).astype(bf16)
+                    self.moving = start(chip_swap, self.held, mask)
+                    mask *= 2
+
+            def t_up(self):
+                held, moving = (v.reshape(2, -1, v.shape[-1]) for v in (self.held, self.moving.value))
+                self.held_a = (held[0].astype(f32) + moving[0].astype(f32)).astype(bf16)
+                self.held_b = (held[1].astype(f32) + moving[1].astype(f32)).astype(bf16)
+                self.moving_a = start(chip_swap, self.held_a, 2)
+                self.moving_b = start(chip_swap, self.held_b, 1)
+
+            def t_out(self):
+                self.held_a = ordered(high, self.held_a, self.moving_a.value)
+                self.held_b = ordered(low, self.held_b, self.moving_b.value)
+                self.moving_a = start(chip_swap, self.held_a, 1)
+                self.moving_b = start(chip_swap, self.held_b, 2)
+
             def t_share(self):
-                self.join(low)
-                self.moving = start(core_swap, self.held)
-
-        def joined(chunks):
-            mine = [c.held for c in chunks]
-            other = [c.moving.value for c in chunks]
+                pieces = [self.held_a, self.moving_a.value, self.held_b, self.moving_b.value]
+                self.pieces = pieces + [start(core_swap, p) for p in pieces]
+
+            def joined(self):
+                def matrix(n, f):
+                    bit = jnp.where(n % 4 < 2, f[2 + images], f[3 + images])
+                    return 2 * ((n % 4) // 2) + (bit ^ (n % 2))
+
+                half = width // 2
+                return run(
+                    "qkvjoin",
+                    static(last_place_kernel, matrix, 8),
+                    self.pieces,
+                    [whole((half, part))] * 8,
+                    [
+                        pl.BlockSpec((part, half), lambda w, f: (0, f[1 + images] ^ (w // 4))),
+                        pl.BlockSpec(
+                            (1, half, part),
+                            lambda w, f: (
+                                jnp.maximum(matrix(w, f) - 1, 0),
+                                f[1 + images] ^ (w // 4),
+                                0,
+                            ),
+                        ),
+                    ],
+                    [like((part, width), f32), like((3, width, part), f32)],
+                    grid=(8,),
+                )
+
+        def ordered(bit, mine, other):
             return jnp.where(
-                core == 0, jnp.concatenate(mine + other), jnp.concatenate(other + mine)
-            ).astype(f32)
+                bit == 0, jnp.concatenate([mine, other]), jnp.concatenate([other, mine])
+            )
 
 
         def attend(slot, w):
@@ -712,9 +860,8 @@
         grad_projs, proj_sums, grad_norm1 = [None] * tensor, [None] * tensor, None
 
 
+        get_attn = Fetch([w_qkv.reshape(3 * width, part), w_out], False)
         small = jnp.concatenate([qv_bias.reshape(-1), fc1_bias])
-        get_qkv = Fetch(w_qkv.reshape(3 * width, part), 1)
-        get_out = Fetch(w_out, 1)
         biases = [Box(small)] + [start(peer, small, slot) for slot in others]
         xc, normed1, top, top_sum = run(
             "prep",
@@ -727,20 +874,19 @@
         seen = [attend(0, w_qkv)]
         step()
 
-        get_qkv.second()
-        get_out.second()
-        get_fc1 = Fetch(w_fc1, 2)
-        step()
-
-        get_qkv.third()
-        get_out.third()
+        get_attn.second()
+        get_fc1 = Fetch([w_fc1], True)
+        step()
+
+        get_attn.third()
         get_fc1.second()
-        get_fc2 = Fetch(w_fc2, 1)
-        qkv = [w_qkv] + [w.value.reshape(3, width, part) for w in get_qkv.full()]
+        qkv, out = [w_qkv], [w_out]
+        for w, w_2 in get_attn.full():
+            qkv.append(w.value.reshape(3, width, part))
+            out.append(w_2)
         for slot in others:
             seen.append(attend(slot, qkv[slot]))
         projs, mixes = [s[0] for s in seen], [s[1] for s in seen]
-        out = [w_out] + get_out.full()
         mid, normed2 = run(
             "middle",
             static(middle_kernel, seq_len, images, tensor),
@@ -754,54 +900,35 @@
         step()
 
         get_fc1.third()
+        get_fc2 = Fetch([w_fc2], True)
+        fc1 = [w_fc1] + [w for w, in get_fc1.full()]
+        for slot in slots:
+            hide(slot)
+        w1 = Reduce(Plain("fc2", acts, [top], TILE))
+        w1.k_away()
+        step()
+
+        w1.t_core()
         get_fc2.second()
-        fc1 = [w_fc1] + get_fc1.full()
-        for slot in others:
-            hide(slot)
-        rest = hidden // 4
-        w1 = [Reduce(Plain(f"fc2{n}", acts, [top], n * rest, rest, TILE)) for n in range(2)]
-        for p in w1:
-            p.k_away(*others)
-        step()
-
-        for p in w1:
-            p.t_core(*others)
+        w1.k_own()
+        step()
+
+
+        total = mid
+        w1.t_one()
         get_fc2.third()
-        hide(0)
-        fc2 = [w_fc2] + get_fc2.full()
-        for p in w1:
-            p.k_send()
-        step()
-
-
-        total = mid
-        rest = width // 4
-        w2 = [
-            Reduce(Plain(f"fc1{n}", [normed2], grad_pres, n * rest, rest, 256)) for n in range(2)
-        ]
-        w1[0].t_x()
-        for slot in others:
+        fc2 = [w_fc2] + [w for w, in get_fc2.full()]
+        for slot in slots:
             ffn(slot)
-        for p in w2:
-            p.k_away(*others)
-        for p in w1:
-            p.k_away(0)
-        step()
-
-        w1[1].t_x()
-        for p in w2:
-            p.t_core(*others)
-        for p in w1:
-            p.t_core(0)
-        ffn(0)
-        for p in w2:
-            p.k_send()
-        w1[0].k_keep()
-        step()
-
-        w2[0].t_x()
-        w1[0].t_y()
-        w1[1].k_keep()
+        w2 = Reduce(Plain("fc1", [normed2], grad_pres, 256))
+        w2.k_away()
+        step()
+
+        w1.k_mid()
+        step()
+
+        w1.t_two()
+        w2.t_core()
         grad_mid, grad_attn, sums2 = run(
             "midback",
             static(mid_back_kernel, seq_len, images),
@@ -810,35 +937,27 @@
             [whole(shape2), whole(shape2), whole((3, width))],
             [like(shape2, f32), like(shape2, bf16), like((3, width), f32)],
         )
+        attend_back(0)
+        step()
+
+        w1.t_z()
+        w2.k_own()
+        step()
+
+        w2.t_one()
+        w1.t_full()
         for slot in others:
             attend_back(slot)
-        for p in w2:
-            p.k_away(0)
-        w3 = [Reduce(Packed("qkv0", 0, 2)), Reduce(Packed("qkv1", 2, 2))]
-        for p in w3:
-            p.k_away(*others)
-        step()
-
-        w2[1].t_x()
-        w1[1].t_y()
-        w1[0].t_z()
-        for p in w2:
-            p.t_core(0)
-        for p in w3:
-            p.t_core(*others)
-        attend_back(0)
-        for p in w3:
-            p.k_send()
-        w2[0].k_keep()
-        step()
-
-        w3[0].t_x()
-        w2[0].t_y()
-        w1[1].t_z()
-        w1[0].t_full()
-        w2[1].k_keep()
-        for p in w3:
-            p.k_away(0)
+        w3 = Apart(Packed())
+        w3.k_away()
+        step()
+
+        w2.k_mid()
+        step()
+
+        w2.t_two()
+        w3.t_core()
+        w1.t_up()
         grad_input, sums1 = run(
             "last",
             static(last_kernel, seq_len, images),
@@ -847,16 +966,6 @@
             [whole(shape2), whole((2, width))],
             [like(shape2, bf16), like((2, width), f32)],
         )
-        step()
-
-        w3[1].t_x()
-        for p in w3:
-            p.t_core(0)
-        w2[1].t_y()
-        w2[0].t_z()
-        w1[1].t_full()
-        w1[0].t_up()
-        w3[0].k_keep()
         layer_out = run(
             "spread",
             static(spread_kernel, seq_len, images),
@@ -867,78 +976,75 @@
         )
         step()
 
-        w3[0].t_y()
-        w2[1].t_z()
-        w2[0].t_full()
-        w1[1].t_up()
-        w1[0].t_out()
-        w3[1].k_keep()
-        step()
-
-        w3[1].t_y()
-        w3[0].t_z()
-        w2[1].t_full()
-        w2[0].t_up()
-        w1[1].t_out()
-        w1[0].t_share()
-        step()
-
-        w3[1].t_z()
-        w3[0].t_full()
-        w2[1].t_up()
-        w2[0].t_out()
-        w1[1].t_share()
-        step()
-
-        w3[1].t_full()
-        w3[0].t_up()
-        w2[1].t_out()
-        w2[0].t_share()
-        step()
-
-        w3[1].t_up()
-        w3[0].t_out()
-        w2[1].t_share()
-        step()
-
-        w3[1].t_out()
-        w3[0].t_share()
-        step()
-
-        w3[1].t_share()
-        grad_fc2, grad_fc1 = joined(w1), joined(w2)
-
-        def unpacked(chunk):
-            mine = chunk.held.reshape(-1, width // 2, part)
-            other = chunk.moving.value.reshape(-1, width // 2, part)
-            return jnp.where(
-                core == 0,
-                jnp.concatenate([mine, other], axis=1),
-                jnp.concatenate([other, mine], axis=1),
-            ).astype(f32)
-
-        packs = [unpacked(p) for p in w3]
-        grad_out = packs[0][0].T
-        grad_qkv = jnp.concatenate([packs[0][1:], packs[1]])
-        layer_out = layer_out.value.reshape(inputs.shape)
-        grad_input = grad_input.value.reshape(inputs.shape)
-        sums1, sums2, top_sum = sums1.value, sums2.value, top_sum.value
-        proj_sums = [p.value for p in proj_sums]
-        pre_sums = [p.value for p in pre_sums]
-
-        common = jnp.concatenate([sums1.reshape(-1), sums2[2], sums2[0], sums2[1], top_sum[0]])
+        w2.t_z()
+        w3.k_own()
+        step()
+
+        w3.t_one()
+        w1.t_out()
+        common = jnp.concatenate(
+            [
+                sums1.value.reshape(-1),
+                sums2.value[2],
+                sums2.value[0],
+                sums2.value[1],
+                top_sum.value[0],
+            ]
+        )
         owned = [
-            jnp.concatenate([proj_sums[slot].reshape(-1), pre_sums[slot].reshape(-1), common])
+            jnp.concatenate(
+                [proj_sums[slot].value.reshape(-1), pre_sums[slot].value.reshape(-1), common]
+            )
             for slot in slots
         ]
         vector = owned[0]
-        for slot in others:
-            vector = vector + peer(owned[slot], slot)
-        vector = vector + core_swap(vector)
-        mask = 1
+        moving = [start(peer, owned[slot], slot) for slot in others]
+
+        def add(*mask):
+            nonlocal vector, moving
+            for m in moving:
+                vector = vector + m.value
+            moving = [start(chip_swap if mask else core_swap, vector, *mask)] if mask != (0,) else []
+
+        step()
+
+        w3.k_mid()
+        step()
+
+        w3.t_two()
+        w2.t_full()
+        add()
+        step()
+
+        w3.t_three()
+        w2.t_up()
+        w1.t_share()
+        add(1)
+        step()
+
+        w3.t_full()
+        w2.t_out()
+        add(2)
+        grad_fc2 = w1.joined()
+        step()
+
+        w3.t_up()
+        w2.t_share()
+        mask = 4
         while mask < chips:
-            vector = vector + chip_swap(vector, mask)
+            add(mask)
             mask *= 2
+        step()
+
+        w3.t_out()
+        add(0)
+        grad_fc1 = w2.joined()
+        step()
+
+        w3.t_share()
+        grad_out, grad_qkv = (g.value for g in w3.joined())
+        layer_out = layer_out.value.reshape(inputs.shape)
+        grad_input = grad_input.value.reshape(inputs.shape)
         grad_qv_bias = vector[: 2 * part].reshape(2, part)
         grad_fc1_bias = vector[2 * part : 2 * part + hidden]
         rest = vector[2 * part + hidden :].reshape(6, width)
@@ -953,9 +1059,9 @@
             rest[2],
             rest[3],
             rest[4],
-            grad_fc1,
+            grad_fc1.value,
             grad_fc1_bias,
-            grad_fc2,
+            grad_fc2.value,
             rest[5],
         )
 

time: 466 us -> 420 us (0.901)
  other arithmetic: 59.6 us -> 27.9 us
  Pallas kernels: 136 us -> 149 us
  local copies, waits for them, and re-layouts: 62.8 us -> 51.2 us
  starting transfers between devices: 64.4 us -> 56 us
  waiting for transfers between devices: 135 us -> 128 us
    convert_element_type x16 -> x7, other arithmetic: 30 us -> 11.8 us  [the longest x2 4.13 us: t_full(): (self.held.astype(f32) + self.moving.value.astype(f32)).astype(bf16)]
    pallas_call x41 -> x31, Pallas kernels: 136 us -> 149 us  [kernel_call(): pl.pallas_call(body, name=name, grid_spec=pltpu.PrefetchScalarGridSpec(nu...]
    select_n x12 -> x4, other arithmetic: 16.5 us -> 6.46 us  [ordered(): jnp.where(bit == 0, jnp.concatenate([mine, other]), jnp.concatenate([othe...]
    ppermute x76 -> x60, starting transfers between devices: 64.4 us -> 56 us  [swap(): return lax.ppermute(value, axis, [(i, i ^ mask) for i in range(size)])]
    ppermute x76 -> x60, waiting for transfers between devices: 135 us -> 128 us  [swap(): return lax.ppermute(value, axis, [(i, i ^ mask) for i in range(size)])]
    unnamed x220 -> x209, local copies, waits for them, and re-layouts: 40.1 us -> 34.2 us
    dynamic_slice x9 -> x10, local copies, waits for them, and re-layouts: 13.1 us -> 8.62 us  [the longest x4 4.89 us: __init__(): lax.dynamic_slice(w, (place * rows, c), (rows, min(cols, w.shape[1])))]
  transfers between devices with their start and end apart: 76 -> 60, of which waited for: 29 -> 26; matrix products, arithmetic and copies ran while one was open for 15% -> 8% of each run, Pallas kernels for 29% -> 32%
where the time goes in v2:
time: 420 us; the launch traced here: 415 us
  Pallas kernels  149 us (35%)
  waiting for transfers between devices  128 us (30%)
  starting transfers between devices  56 us (13%)
  local copies, waits for them, and re-layouts  51.2 us (12%)
  other arithmetic  27.9 us (7%)
    pallas_call x31, Pallas kernels, kernel_call(): pl.pallas_call(body, name=name, grid_spec=pltpu.PrefetchScalarGridSpec(nu...  149 us
    ppermute x60, waiting for transfers between devices, swap(): return lax.ppermute(value, axis, [(i, i ^ mask) for i in range(size)])  128 us
    ppermute x60, starting transfers between devices, swap(): return lax.ppermute(value, axis, [(i, i ^ mask) for i in range(size)])  56 us
    unnamed x209, local copies, waits for them, and re-layouts  34.2 us
  transfers between devices with their start and end apart: 60, of which 26 were waited for; matrix products, arithmetic and copies ran while one was open for 8% of the time, Pallas kernels for 32%

profile of v2, /device:TPU:0, one launch (start us, length us, event | category | flops | bytes accessed | tf_op | source)
XLA Modules:
  0.0 415.3 jit_solution(326062563036522719)
XLA Ops:
  14.2 6.0 %attend0.1 = (bf16[3,640,512]{2,1,0:T(8,128)(2,1)S(1)}, bf16[640,512]{1,0:T(8,128)(2,1)S(1)}) custom-call(s32[6]{0:T(128)S(1)} %concatenate.55.flags, bf16[640,1024]{1,0:T(8,128)(2,1)S(1)} %get-tuple-element.252.normed, bf16[3,1024,512]{2,1,0:T(8,128)(2,1)S(1)} %copy-done.22, f32[3,1,512]{2,1,0:T(1,128)S(1)} %pad_maximum_fusion.4.shift), custom_call_target="tpu_custom_call" | custom-call | flops 1000 | bytes 1000 | tf_op jit(solution)/shard_map/attend0/pallas_call | solution.py:47
  21.6 11.2 %collective-permute-done.1 = f32[3072]{0:T(1024)S(1)} collective-permute-done((f32[3072]{0:T(1024)S(1)}, f32[3072]{0:T(1024)S(1)}, u32[]{:S(2)}, u32[]{:S(2)}) %collective-permute-start.1) | collective-permute-done | bytes 12320 | tf_op jit(solution)/shard_map/ppermute | solution.py:393
  37.3 20.2 %collective-permute-done.2.refs_1_ = bf16[1024,512]{1,0:T(8,128)(2,1)} collective-permute-done((bf16[1024,512]{1,0:T(8,128)(2,1)}, bf16[1024,512]{1,0:T(8,128)(2,1)}, u32[]{:S(2)}, u32[]{:S(2)}) %collective-permute-start.2) | collective-permute-done | bytes 1048608 | tf_op jit(solution)/shard_map/ppermute | solution.py:393
  67.1 6.0 %attend1.1 = (bf16[3,640,512]{2,1,0:T(8,128)(2,1)S(1)}, bf16[640,512]{1,0:T(8,128)(2,1)S(1)}) custom-call(s32[6]{0:T(128)S(1)} %concatenate.55.flags, bf16[640,1024]{1,0:T(8,128)(2,1)S(1)} %get-tuple-element.252.normed, bf16[3,1024,512]{2,1,0:T(8,128)(2,1)S(1)} %bitcast.82, f32[3,1,512]{2,1,0:T(1,128)S(1)} %pad_maximum_fusion.5.shift), custom_call_target="tpu_custom_call" | custom-call | flops 1000 | bytes 1000 | tf_op jit(solution)/shard_map/attend1/pallas_call | solution.py:47
  80.5 4.8 %hidden0.1 = (bf16[640,2048]{1,0:T(8,128)(2,1)S(1)}, bf16[640,2048]{1,0:T(8,128)(2,1)S(1)}) custom-call(s32[6]{0:T(128)S(1)} %concatenate.55.flags, bf16[640,1024]{1,0:T(8,128)(2,1)S(1)} %get-tuple-element.267.normed.refs_0_.refs_1_, bf16[1024,2048]{1,0:T(8,128)(2,1)S(1)} %copy-done.15, f32[1,2048]{1,0:T(1,128)S(1)} %bitcast.91), custom_call_target="tpu_custom_call" | custom-call | flops 1000 | bytes 1000 | tf_op jit(solution)/shard_map/hidden0/pallas_call | solution.py:47
  89.0 4.8 %hidden1.1 = (bf16[640,2048]{1,0:T(8,128)(2,1)S(1)}, bf16[640,2048]{1,0:T(8,128)(2,1)S(1)}) custom-call(s32[6]{0:T(128)S(1)} %concatenate.55.flags, bf16[640,1024]{1,0:T(8,128)(2,1)S(1)} %get-tuple-element.267.normed.refs_0_.refs_1_, bf16[1024,2048]{1,0:T(8,128)(2,1)S(1)} %assemble.4.w.w1, f32[1,2048]{1,0:T(1,128)S(1)} %bitcast.90), custom_call_target="tpu_custom_call" | custom-call | flops 1000 | bytes 1000 | tf_op jit(solution)/shard_map/hidden1/pallas_call | solution.py:47
  93.9 4.7 %fc20away.1 = bf16[2,1024,1024]{2,1,0:T(8,128)(2,1)} custom-call(s32[6]{0:T(128)S(1)} %concatenate.55.flags, bf16[640,2048]{1,0:T(8,128)(2,1)S(1)} %get-tuple-element.282.refs_0_.act, bf16[640,2048]{1,0:T(8,128)(2,1)S(1)} %get-tuple-element.281.refs_1_.refs_0_.act, bf16[640,1024]{1,0:T(8,128)(2,1)S(1)} %get-tuple-element.273.refs_2_.refs_3_.refs_1_.top, ...), custom_call_target="tpu_custom_call" | custom-call | flops 1000 | bytes 1000 | tf_op jit(solution)/shard_map/fc20away/pallas_call | solution.py:47
  98.6 4.5 %collective-permute-done.11.refs_0_ = bf16[512,1024]{1,0:T(8,128)(2,1)} collective-permute-done((bf16[512,1024]{1,0:T(8,128)(2,1)S(1)}, bf16[512,1024]{1,0:T(8,128)(2,1)}, u32[]{:S(2)}, u32[]{:S(2)}) %collective-permute-start.11) | collective-permute-done | bytes 1048608 | tf_op jit(solution)/shard_map/ppermute | solution.py:393
  112.3 3.5 fc21own.1
  115.8 4.0 fc20own.2
  125.0 8.8 %ffn0.1 = (f32[640,1024]{1,0:T(8,128)S(1)}, bf16[640,2048]{1,0:T(8,128)(2,1)S(1)}, f32[640,1024]{1,0:T(8,128)S(1)}, f32[1,2048]{1,0:T(1,128)S(1)}) custom-call(s32[6]{0:T(128)S(1)} %concatenate.55.flags, bf16[640,2048]{1,0:T(8,128)(2,1)S(1)} %copy-done.6, bf16[640,2048]{1,0:T(8,128)(2,1)S(1)} %copy-done.49, ...), custom_call_target="tpu_custom_call" | custom-call | flops 1000 | bytes 1000 | tf_op jit(solution)/shard_map/ffn0/pallas_call | solution.py:47
  135.3 3.7 assemble.5.w2
  141.0 9.6 %ffn1.1 = (f32[640,1024]{1,0:T(8,128)S(1)}, bf16[640,2048]{1,0:T(8,128)(2,1)S(1)}, f32[640,1024]{1,0:T(8,128)S(1)}, f32[1,2048]{1,0:T(1,128)S(1)}) custom-call(s32[6]{0:T(128)S(1)} %concatenate.55.flags, bf16[640,2048]{1,0:T(8,128)(2,1)S(1)} %copy-done.9, bf16[640,2048]{1,0:T(8,128)(2,1)S(1)} %copy-done.61, ...), custom_call_target="tpu_custom_call" | custom-call | flops 1000 | bytes 1000 | tf_op jit(solution)/shard_map/ffn1/pallas_call | solution.py:47
  150.7 4.7 %fc10away.1 = bf16[2,512,2048]{2,1,0:T(8,128)(2,1)} custom-call(s32[6]{0:T(128)S(1)} %concatenate.55.flags, bf16[640,1024]{1,0:T(8,128)(2,1)S(1)} %get-tuple-element.267.normed.refs_0_.refs_1_, bf16[640,1024]{1,0:T(8,128)(2,1)S(1)} %get-tuple-element.267.normed.refs_0_.refs_1_, bf16[640,2048]{1,0:T(8,128)(2,1)S(1)} %get-tuple-element.329.refs_2_.refs_1_, ...), custom_call_target="tpu_custom_call" | custom-call | flops 1000 | bytes 1000 | tf_op jit(solution)/shard_map/fc10away/pallas_call | solution.py:47
  171.9 11.0 %aback0.1 = (bf16[3,640,512]{2,1,0:T(8,128)(2,1)S(1)}, f32[640,1024]{1,0:T(8,128)S(1)}, f32[2,512]{1,0:T(2,128)S(1)}) custom-call(s32[6]{0:T(128)S(1)} %concatenate.55.flags, bf16[640,1024]{1,0:T(8,128)(2,1)S(1)} %get-tuple-element.337.grad_attn.top, bf16[512,1024]{1,0:T(8,128)(2,1)S(1)} %copy-done.40, bf16[3,640,512]{2,1,0:T(8,128)(2,1)S(1)} %copy-done.66, ...), custom_call_target="tpu_custom_call" | custom-call | flops 1000 | bytes 1000 | tf_op jit(solution)/shard_map/aback0/pallas_call | solution.py:47
  193.7 3.8 fc10own.2
  197.6 4.5 %collective-permute-done.23 = bf16[256,1024]{1,0:T(8,128)(2,1)} collective-permute-done((bf16[256,1024]{1,0:T(8,128)(2,1)}, bf16[256,1024]{1,0:T(8,128)(2,1)}, u32[]{:S(2)}, u32[]{:S(2)}) %collective-permute-start.23) | collective-permute-done | bytes 524320 | tf_op jit(solution)/shard_map/ppermute | solution.py:393
  209.5 10.9 %aback1.1 = (bf16[3,640,512]{2,1,0:T(8,128)(2,1)S(1)}, f32[640,1024]{1,0:T(8,128)S(1)}, f32[2,512]{1,0:T(2,128)S(1)}) custom-call(s32[6]{0:T(128)S(1)} %concatenate.55.flags, bf16[640,1024]{1,0:T(8,128)(2,1)S(1)} %copy-done.3, bf16[512,1024]{1,0:T(8,128)(2,1)S(1)} %copy-done.47, bf16[3,640,512]{2,1,0:T(8,128)(2,1)S(1)} %copy-done.64, ...), custom_call_target="tpu_custom_call" | custom-call | flops 1000 | bytes 1000 | tf_op jit(solution)/shard_map/aback1/pallas_call | solution.py:47
  222.0 5.3 %qkv0away.1 = bf16[2,4,512,512]{3,2,1,0:T(8,128)(2,1)} custom-call(s32[6]{0:T(128)S(1)} %concatenate.55.flags, bf16[640,1024]{1,0:T(8,128)(2,1)S(1)} %copy-done.1, bf16[640,1024]{1,0:T(8,128)(2,1)S(1)} %copy-done.3, bf16[640,512]{1,0:T(8,128)(2,1)S(1)} %get-tuple-element.256.refs_0_, bf16[640,512]{1,0:T(8,128)(2,1)S(1)} %copy-done.27, ...), custom_call_target="tpu_custom_call" | custom-call | flops 1000 | bytes 1000 | tf_op jit(solution)/shard_map/qkv0away/pallas_call | solution.py:47
  227.2 4.1 collective-permute-done.26
  250.0 3.3 last.1
  260.5 3.6 qkv0own.2
  278.9 19.0 %collective-permute-done.35 = f32[9216]{0:T(1024)S(1)} collective-permute-done((f32[9216]{0:T(1024)S(1)}, f32[9216]{0:T(1024)S(1)}, u32[]{:S(2)}, u32[]{:S(2)}) %collective-permute-start.35) | collective-permute-done | bytes 36896 | tf_op jit(solution)/shard_map/ppermute | solution.py:393
  311.3 13.4 %collective-permute-done.38 = bf16[128,2048]{1,0:T(8,128)(2,1)} collective-permute-done((bf16[128,2048]{1,0:T(8,128)(2,1)}, bf16[128,2048]{1,0:T(8,128)(2,1)}, u32[]{:S(2)}, u32[]{:S(2)}) %collective-permute-start.38) | collective-permute-done | bytes 524320 | tf_op jit(solution)/shard_map/ppermute | solution.py:393
  333.8 4.1 collective-permute-done.41
  337.9 9.6 %collective-permute-done.40 = bf16[256,512]{1,0:T(8,128)(2,1)S(1)} collective-permute-done((bf16[256,512]{1,0:T(8,128)(2,1)S(1)}, bf16[256,512]{1,0:T(8,128)(2,1)S(1)}, u32[]{:S(2)}, u32[]{:S(2)}) %collective-permute-start.40) | collective-permute-done | bytes 262176 | tf_op jit(solution)/shard_map/ppermute | solution.py:393
  353.7 7.7 %fc2join.1 = f32[2048,1024]{1,0:T(8,128)} custom-call(s32[6]{0:T(128)S(1)} %concatenate.55.flags, bf16[512,1024]{1,0:T(8,128)(2,1)S(1)} %copy-done.45, bf16[512,1024]{1,0:T(8,128)(2,1)S(1)} %copy-done.70, bf16[512,1024]{1,0:T(8,128)(2,1)} %collective-permute-done.43.refs_2_, bf16[512,1024]{1,0:T(8,128)(2,1)} %collective-permute-done.44.refs_3_), custom_call_target="tpu_custom_call" | custom-call | flops 1000 | bytes 1000 | tf_op jit(solution)/shard_map/fc2join/pallas_call | solution.py:47
  363.4 11.9 %collective-permute-done.46 = bf16[512,512]{1,0:T(8,128)(2,1)S(1)} collective-permute-done((bf16[512,512]{1,0:T(8,128)(2,1)S(1)}, bf16[512,512]{1,0:T(8,128)(2,1)S(1)}, u32[]{:S(2)}, u32[]{:S(2)}) %collective-permute-start.46) | collective-permute-done | bytes 524320 | tf_op jit(solution)/shard_map/ppermute | solution.py:393
  377.1 3.3 collective-permute-start.53
  380.5 3.2 collective-permute-done.53
  393.2 7.7 %fc1join.1 = f32[1024,2048]{1,0:T(8,128)} custom-call(s32[6]{0:T(128)S(1)} %concatenate.55.flags, bf16[256,2048]{1,0:T(8,128)(2,1)S(1)} %maximum_select_fusion.1.refs_0_, bf16[256,2048]{1,0:T(8,128)(2,1)} %collective-permute-done.47.refs_1_, bf16[256,2048]{1,0:T(8,128)(2,1)} %collective-permute-done.51.refs_2_, bf16[256,2048]{1,0:T(8,128)(2,1)S(1)} %copy-done.72), custom_call_target="tpu_custom_call" | custom-call | flops 1000 | bytes 1000 | tf_op jit(solution)/shard_map/fc1join/pallas_call | solution.py:47
  407.8 7.3 %qkvjoin.1 = (f32[512,1024]{1,0:T(8,128)}, f32[3,1024,512]{2,1,0:T(8,128)}) custom-call(s32[6]{0:T(128)S(1)} %concatenate.55.flags, bf16[512,512]{1,0:T(8,128)(2,1)S(1)} %maximum_select_fusion.2.refs_0_, bf16[512,512]{1,0:T(8,128)(2,1)S(1)} %collective-permute-done.54.refs_1_, bf16[512,512]{1,0:T(8,128)(2,1)S(1)} %maximum_select_fusion.3.refs_2_, ...), custom_call_target="tpu_custom_call" | custom-call | flops 1000 | bytes 1000 | tf_op jit(solution)/shard_map/qkvjoin/pallas_call | solution.py:47
  (390 shorter events, 182.2 us)
Async XLA Ops:
  6.2 26.6 %collective-permute-start = (bf16[1024,512]{1,0:T(8,128)(2,1)}, bf16[1024,512]{1,0:T(8,128)(2,1)}, u32[]{:S(2)}, u32[]{:S(2)}) collective-permute-start(bf16[1024,512]{1,0:T(8,128)(2,1)} %pad_maximum_fusion), channel_id=1, source_target_pairs={{0,1},{1,0},{2,3},{3,2},{4,5},{5,4},{6,7},{7,6},{8,9},{9,8},{10,11... | collective-permute-start | bytes 3145736 | tf_op jit(solution)/shard_map/ppermute | solution.py:393
  9.1 23.6 %collective-permute-start.1 = (f32[3072]{0:T(1024)S(1)}, f32[3072]{0:T(1024)S(1)}, u32[]{:S(2)}, u32[]{:S(2)}) collective-permute-start(f32[3072]{0:T(1024)S(1)} %constant_dynamic-update-slice_fusion), channel_id=1, source_target_pairs={{0,1},{1,0},{2,3},{3,2},{4,5},{5,4},{6,7},{7,6},{8,9},{9,8},{10,11... | collective-permute-start | bytes 36872 | tf_op jit(solution)/shard_map/ppermute | solution.py:393
  32.7 24.8 %collective-permute-start.2 = (bf16[1024,512]{1,0:T(8,128)(2,1)}, bf16[1024,512]{1,0:T(8,128)(2,1)}, u32[]{:S(2)}, u32[]{:S(2)}) collective-permute-start(bf16[1024,512]{1,0:T(8,128)(2,1)} %collective-permute-done.refs_0_), channel_id=1, source_target_pairs={{0,4},{4,0},{8,12},{12,8},{16,20},{20,16},{24,28},{28,24},{1,5},{5... | collective-permute-start | bytes 3145736 | tf_op jit(solution)/shard_map/ppermute | solution.py:393
  34.5 23.0 %collective-permute-start.3 = (bf16[1024,512]{1,0:T(8,128)(2,1)}, bf16[1024,512]{1,0:T(8,128)(2,1)}, u32[]{:S(2)}, u32[]{:S(2)}) collective-permute-start(bf16[1024,512]{1,0:T(8,128)(2,1)} %collective-permute-done.refs_0_), channel_id=1, source_target_pairs={{0,2},{2,0},{1,3},{3,1},{4,6},{6,4},{5,7},{7,5},{8,10},{10,8},{9,1... | collective-permute-start | bytes 3145736 | tf_op jit(solution)/shard_map/ppermute | solution.py:393
  34.5 25.9 %collective-permute-start.4 = (bf16[256,2048]{1,0:T(8,128)(2,1)}, bf16[256,2048]{1,0:T(8,128)(2,1)}, u32[]{:S(2)}, u32[]{:S(2)}) collective-permute-start(bf16[256,2048]{1,0:T(8,128)(2,1)} %pad_maximum_fusion.1), channel_id=1, source_target_pairs={{0,1},{1,0},{2,3},{3,2},{4,5},{5,4},{6,7},{7,6},{8,9},{9,8},{10,11... | collective-permute-start | bytes 3145736 | tf_op jit(solution)/shard_map/ppermute | solution.py:393
  60.4 18.0 %collective-permute-start.8 = (bf16[256,2048]{1,0:T(8,128)(2,1)}, bf16[256,2048]{1,0:T(8,128)(2,1)S(1)}, u32[]{:S(2)}, u32[]{:S(2)}) collective-permute-start(bf16[256,2048]{1,0:T(8,128)(2,1)} %collective-permute-done.4.refs_0_), channel_id=1, source_target_pairs={{0,2},{2,0},{1,3},{3,1},{4,6},{6,4},{5,7},{7,5},{8,10},{10,8},{9,1... | collective-permute-start | bytes 3145736 | tf_op jit(solution)/shard_map/ppermute | solution.py:393
  62.2 16.2 %collective-permute-start.7 = (bf16[128,2048]{1,0:T(8,128)(2,1)S(1)}, bf16[128,2048]{1,0:T(8,128)(2,1)S(1)}, u32[]{:S(2)}, u32[]{:S(2)}) collective-permute-start(bf16[128,2048]{1,0:T(8,128)(2,1)S(1)} %get-tuple-element.247), channel_id=1, source_target_pairs={{0,8},{4,12},{8,0},{12,4},{16,24},{20,28},{24,16},{28,20},{1,9},{5... | collective-permute-start | bytes 1572872 | tf_op jit(solution)/shard_map/ppermute | solution.py:393
  78.4 24.7 %collective-permute-start.11 = (bf16[512,1024]{1,0:T(8,128)(2,1)S(1)}, bf16[512,1024]{1,0:T(8,128)(2,1)}, u32[]{:S(2)}, u32[]{:S(2)}) collective-permute-start(bf16[512,1024]{1,0:T(8,128)(2,1)S(1)} %pad_maximum_fusion.2), channel_id=1, source_target_pairs={{0,1},{1,0},{2,3},{3,2},{4,5},{5,4},{6,7},{7,6},{8,9},{9,8},{10,11... | collective-permute-start | bytes 3145736 | tf_op jit(solution)/shard_map/ppermute | solution.py:393
  103.1 17.6 %collective-permute-start.15 = (bf16[512,1024]{1,0:T(8,128)(2,1)}, bf16[512,1024]{1,0:T(8,128)(2,1)}, u32[]{:S(2)}, u32[]{:S(2)}) collective-permute-start(bf16[512,1024]{1,0:T(8,128)(2,1)} %collective-permute-done.11.refs_0_), channel_id=1, source_target_pairs={{0,2},{2,0},{1,3},{3,1},{4,6},{6,4},{5,7},{7,5},{8,10},{10,8},{9,1... | collective-permute-start | bytes 3145736 | tf_op jit(solution)/shard_map/ppermute | solution.py:393
  121.8 33.7 %collective-permute-start.17 = (bf16[2,256,1024]{2,1,0:T(8,128)(2,1)}, bf16[2,256,1024]{2,1,0:T(8,128)(2,1)}, u32[]{:S(2)}, u32[]{:S(2)}) collective-permute-start(bf16[2,256,1024]{2,1,0:T(8,128)(2,1)} %constant_dynamic-slice_fusion.3), channel_id=1, source_target_pairs={{0,4},{4,0},{8,12},{12,8},{16,20},{20,16},{24,28},{28,24},{1,5},{5... | collective-permute-start | bytes 3145736 | tf_op jit(solution)/shard_map/ppermute | solution.py:393
  123.0 32.5 %collective-permute-start.16 = (bf16[1,512,1024]{2,1,0:T(8,128)(2,1)}, bf16[1,512,1024]{2,1,0:T(8,128)(2,1)}, u32[]{:S(2)}, u32[]{:S(2)}) collective-permute-start(bf16[1,512,1024]{2,1,0:T(8,128)(2,1)} %fc21own.1), channel_id=1, source_target_pairs={{0,1},{1,0},{2,3},{3,2},{4,5},{5,4},{6,7},{7,6},{8,9},{9,8},{10,11... | collective-permute-start | bytes 3145736 | tf_op jit(solution)/shard_map/ppermute | solution.py:393
  159.3 26.3 %collective-permute-start.22 = (bf16[2,512,2048]{2,1,0:T(8,128)(2,1)}, bf16[2,512,2048]{2,1,0:T(8,128)(2,1)}, u32[]{:S(2)}, u32[]{:S(2)}) collective-permute-start(bf16[2,512,2048]{2,1,0:T(8,128)(2,1)} %fc10away.1), channel_id=1, source_target_pairs={{0,2},{2,0},{1,3},{3,1},{4,6},{6,4},{5,7},{7,5},{8,10},{10,8},{9,1... | collective-permute-start | bytes 12582920 | tf_op jit(solution)/shard_map/ppermute | solution.py:393
  162.4 23.3 %collective-permute-start.21 = (bf16[256,1024]{1,0:T(8,128)(2,1)}, bf16[256,1024]{1,0:T(8,128)(2,1)}, u32[]{:S(2)}, u32[]{:S(2)}) collective-permute-start(bf16[256,1024]{1,0:T(8,128)(2,1)} %fusion.3), channel_id=1, source_target_pairs={{0,1},{1,0},{2,3},{3,2},{4,5},{5,4},{6,7},{7,6},{8,9},{9,8},{10,11... | collective-permute-start | bytes 1572872 | tf_op jit(solution)/shard_map/ppermute | solution.py:393
  163.7 21.9 %collective-permute-start.20 = (bf16[256,1024]{1,0:T(8,128)(2,1)}, bf16[256,1024]{1,0:T(8,128)(2,1)}, u32[]{:S(2)}, u32[]{:S(2)}) collective-permute-start(bf16[256,1024]{1,0:T(8,128)(2,1)} %dynamic-slice_bitcast_fusion.1), channel_id=1, source_target_pairs={{0,4},{4,0},{8,12},{12,8},{16,20},{20,16},{24,28},{28,24},{1,5},{5... | collective-permute-start | bytes 1572872 | tf_op jit(solution)/shard_map/ppermute | solution.py:393
  202.2 29.2 %collective-permute-start.25 = (bf16[2,128,2048]{2,1,0:T(8,128)(2,1)S(1)}, bf16[2,128,2048]{2,1,0:T(8,128)(2,1)S(1)}, u32[]{:S(2)}, u32[]{:S(2)}) collective-permute-start(bf16[2,128,2048]{2,1,0:T(8,128)(2,1)S(1)} %constant_dynamic-slice_fusion.2), channel_id=1, source_target_pairs={{0,4},{4,0},{8,12},{12,8},{16,20},{20,16},{24,28},{28,24},{1,5},{5... | collective-permute-start | bytes 3145736 | tf_op jit(solution)/shard_map/ppermute | solution.py:393
  203.5 27.9 %collective-permute-start.24 = (bf16[1,256,2048]{2,1,0:T(8,128)(2,1)S(1)}, bf16[1,256,2048]{2,1,0:T(8,128)(2,1)S(1)}, u32[]{:S(2)}, u32[]{:S(2)}) collective-permute-start(bf16[1,256,2048]{2,1,0:T(8,128)(2,1)S(1)} %fc11own.1), channel_id=1, source_target_pairs={{0,1},{1,0},{2,3},{3,2},{4,5},{5,4},{6,7},{7,6},{8,9},{9,8},{10,11... | collective-permute-start | bytes 3145736 | tf_op jit(solution)/shard_map/ppermute | solution.py:393
  206.8 24.5 %collective-permute-start.26 = (bf16[256,1024]{1,0:T(8,128)(2,1)S(1)}, bf16[256,1024]{1,0:T(8,128)(2,1)S(1)}, u32[]{:S(2)}, u32[]{:S(2)}) collective-permute-start(bf16[256,1024]{1,0:T(8,128)(2,1)S(1)} %add_convert_fusion.3), channel_id=1, source_target_pairs={{0,16},{4,20},{8,24},{12,28},{16,0},{20,4},{24,8},{28,12},{1,17},{... | collective-permute-start | bytes 1572872 | tf_op jit(solution)/shard_map/ppermute | solution.py:393
  234.9 22.2 %collective-permute-start.29 = (bf16[2,4,512,512]{3,2,1,0:T(8,128)(2,1)}, bf16[2,4,512,512]{3,2,1,0:T(8,128)(2,1)}, u32[]{:S(2)}, u32[]{:S(2)}) collective-permute-start(bf16[2,4,512,512]{3,2,1,0:T(8,128)(2,1)} %qkv0away.1), channel_id=1, source_target_pairs={{0,2},{2,0},{1,3},{3,1},{4,6},{6,4},{5,7},{7,5},{8,10},{10,8},{9,1... | collective-permute-start | bytes 12582920 | tf_op jit(solution)/shard_map/ppermute | solution.py:393
  237.3 16.0 %collective-permute-start.30 = (bf16[256,1024]{1,0:T(8,128)(2,1)}, bf16[256,1024]{1,0:T(8,128)(2,1)}, u32[]{:S(2)}, u32[]{:S(2)}) collective-permute-start(bf16[256,1024]{1,0:T(8,128)(2,1)} %add_convert_fusion.2), channel_id=1, source_target_pairs={{0,8},{4,12},{8,0},{12,4},{16,24},{20,28},{24,16},{28,20},{1,9},{5... | collective-permute-start | bytes 1572872 | tf_op jit(solution)/shard_map/ppermute | solution.py:393
  271.7 26.2 %collective-permute-start.34 = (bf16[512,1024]{1,0:T(8,128)(2,1)S(1)}, bf16[512,1024]{1,0:T(8,128)(2,1)S(1)}, u32[]{:S(2)}, u32[]{:S(2)}) collective-permute-start(bf16[512,1024]{1,0:T(8,128)(2,1)S(1)} %maximum_select_fusion.refs_0_), channel_id=1, source_target_pairs={{0,4},{4,0},{8,12},{12,8},{16,20},{20,16},{24,28},{28,24},{1,5},{5... | collective-permute-start | bytes 3145736 | tf_op jit(solution)/shard_map/ppermute | solution.py:393
  273.0 24.9 %collective-permute-start.33 = (bf16[2,512,512]{2,1,0:T(8,128)(2,1)S(1)}, bf16[2,512,512]{2,1,0:T(8,128)(2,1)S(1)}, u32[]{:S(2)}, u32[]{:S(2)}) collective-permute-start(bf16[2,512,512]{2,1,0:T(8,128)(2,1)S(1)} %constant_dynamic-slice_fusion.1), channel_id=1, source_target_pairs={{0,8},{4,12},{8,0},{12,4},{16,24},{20,28},{24,16},{28,20},{1,9},{5... | collective-permute-start | bytes 3145736 | tf_op jit(solution)/shard_map/ppermute | solution.py:393
  274.4 24.4 %collective-permute-start.32 = (bf16[1,2,512,512]{3,2,1,0:T(8,128)(2,1)S(1)}, bf16[1,2,512,512]{3,2,1,0:T(8,128)(2,1)S(1)}, u32[]{:S(2)}, u32[]{:S(2)}) collective-permute-start(bf16[1,2,512,512]{3,2,1,0:T(8,128)(2,1)S(1)} %qkv1own.1), channel_id=1, source_target_pairs={{0,1},{1,0},{2,3},{3,2},{4,5},{5,4},{6,7},{7,6},{8,9},{9,8},{10,11... | collective-permute-start | bytes 3145736 | tf_op jit(solution)/shard_map/ppermute | solution.py:393
  275.5 22.4 %collective-permute-start.35 = (f32[9216]{0:T(1024)S(1)}, f32[9216]{0:T(1024)S(1)}, u32[]{:S(2)}, u32[]{:S(2)}) collective-permute-start(f32[9216]{0:T(1024)S(1)} %get-tuple-element.384), channel_id=1, source_target_pairs={{0,1},{1,0},{2,3},{3,2},{4,5},{5,4},{6,7},{7,6},{8,9},{9,8},{10,11... | collective-permute-start | bytes 110600 | tf_op jit(solution)/shard_map/ppermute | solution.py:393
  301.5 23.2 %collective-permute-start.38 = (bf16[128,2048]{1,0:T(8,128)(2,1)}, bf16[128,2048]{1,0:T(8,128)(2,1)}, u32[]{:S(2)}, u32[]{:S(2)}) collective-permute-start(bf16[128,2048]{1,0:T(8,128)(2,1)} %add_convert_fusion.1), channel_id=1, source_target_pairs={{0,16},{4,20},{8,24},{12,28},{16,0},{20,4},{24,8},{28,12},{1,17},{... | collective-permute-start | bytes 1572872 | tf_op jit(solution)/shard_map/ppermute | solution.py:393
  306.6 18.1 %collective-permute-start.37 = (bf16[512,512]{1,0:T(8,128)(2,1)}, bf16[512,512]{1,0:T(8,128)(2,1)}, u32[]{:S(2)}, u32[]{:S(2)}) collective-permute-start(bf16[512,512]{1,0:T(8,128)(2,1)} %fusion.5), channel_id=1, source_target_pairs={{0,1},{1,0},{2,3},{3,2},{4,5},{5,4},{6,7},{7,6},{8,9},{9,8},{10,11... | collective-permute-start | bytes 1572872 | tf_op jit(solution)/shard_map/ppermute | solution.py:393
  308.6 16.1 %collective-permute-start.36 = (bf16[512,512]{1,0:T(8,128)(2,1)}, bf16[512,512]{1,0:T(8,128)(2,1)S(1)}, u32[]{:S(2)}, u32[]{:S(2)}) collective-permute-start(bf16[512,512]{1,0:T(8,128)(2,1)} %constant_dynamic-slice_fusion), channel_id=1, source_target_pairs={{0,4},{4,0},{8,12},{12,8},{16,20},{20,16},{24,28},{28,24},{1,5},{5... | collective-permute-start | bytes 1572872 | tf_op jit(solution)/shard_map/ppermute | solution.py:393
  326.0 21.5 %collective-permute-start.44 = (bf16[512,1024]{1,0:T(8,128)(2,1)}, bf16[512,1024]{1,0:T(8,128)(2,1)}, u32[]{:S(2)}, u32[]{:S(2)}) collective-permute-start(bf16[512,1024]{1,0:T(8,128)(2,1)} %copy-done.69), channel_id=1, source_target_pairs={{0,2},{2,0},{1,3},{3,1},{4,6},{6,4},{5,7},{7,5},{8,10},{10,8},{9,1... | collective-permute-start | bytes 3145736 | tf_op jit(solution)/shard_map/ppermute | solution.py:393
  326.0 21.5 %collective-permute-start.43 = (bf16[512,1024]{1,0:T(8,128)(2,1)S(1)}, bf16[512,1024]{1,0:T(8,128)(2,1)}, u32[]{:S(2)}, u32[]{:S(2)}) collective-permute-start(bf16[512,1024]{1,0:T(8,128)(2,1)S(1)} %copy-done.45), channel_id=1, source_target_pairs={{0,2},{2,0},{1,3},{3,1},{4,6},{6,4},{5,7},{7,5},{8,10},{10,8},{9,1... | collective-permute-start | bytes 3145736 | tf_op jit(solution)/shard_map/ppermute | solution.py:393
  327.9 19.6 %collective-permute-start.42 = (bf16[128,2048]{1,0:T(8,128)(2,1)S(1)}, bf16[128,2048]{1,0:T(8,128)(2,1)}, u32[]{:S(2)}, u32[]{:S(2)}) collective-permute-start(bf16[128,2048]{1,0:T(8,128)(2,1)S(1)} %add_convert_fusion), channel_id=1, source_target_pairs={{0,8},{4,12},{8,0},{12,4},{16,24},{20,28},{24,16},{28,20},{1,9},{5... | collective-permute-start | bytes 1572872 | tf_op jit(solution)/shard_map/ppermute | solution.py:393
  331.7 15.8 %collective-permute-start.40 = (bf16[256,512]{1,0:T(8,128)(2,1)S(1)}, bf16[256,512]{1,0:T(8,128)(2,1)S(1)}, u32[]{:S(2)}, u32[]{:S(2)}) collective-permute-start(bf16[256,512]{1,0:T(8,128)(2,1)S(1)} %dynamic-slice_convert_fusion.1), channel_id=1, source_target_pairs={{0,8},{4,12},{8,0},{12,4},{16,24},{20,28},{24,16},{28,20},{1,9},{5... | collective-permute-start | bytes 786440 | tf_op jit(solution)/shard_map/ppermute | solution.py:393
  349.1 26.1 %collective-permute-start.47 = (bf16[256,2048]{1,0:T(8,128)(2,1)S(1)}, bf16[256,2048]{1,0:T(8,128)(2,1)}, u32[]{:S(2)}, u32[]{:S(2)}) collective-permute-start(bf16[256,2048]{1,0:T(8,128)(2,1)S(1)} %maximum_select_fusion.1.refs_0_), channel_id=1, source_target_pairs={{0,4},{4,0},{8,12},{12,8},{16,20},{20,16},{24,28},{28,24},{1,5},{5... | collective-permute-start | bytes 3145736 | tf_op jit(solution)/shard_map/ppermute | solution.py:393
  350.3 25.0 %collective-permute-start.46 = (bf16[512,512]{1,0:T(8,128)(2,1)S(1)}, bf16[512,512]{1,0:T(8,128)(2,1)S(1)}, u32[]{:S(2)}, u32[]{:S(2)}) collective-permute-start(bf16[512,512]{1,0:T(8,128)(2,1)S(1)} %pad_maximum_fusion.3), channel_id=1, source_target_pairs={{0,16},{4,20},{8,24},{12,28},{16,0},{20,4},{24,8},{28,12},{1,17},{... | collective-permute-start | bytes 1572872 | tf_op jit(solution)/shard_map/ppermute | solution.py:393
  (127 other events, 876.1 us)

commit v3 on v2

--- a/solution.py
+++ b/solution.py
@@ -179,47 +179,48 @@
     spans(flags, seq_len, body)
 
 
-def ffn_kernel(seq_len, images, first, flags, act, slope, top, w2, w1, base, *refs):
-    if first:
-        total, grad_pre, grad_norm, sums = refs
-        grad_base = None
-    else:
-        grad_base, total, grad_pre, grad_norm, sums = refs
-    start = pl.program_id(0) == 0
+def ffn_kernel(seq_len, images, slots, flags, *refs):
+    act, slope, w2, w1 = (refs[n * slots : (n + 1) * slots] for n in range(4))
+    top, mid, bias, gain = refs[4 * slots : 4 * slots + 4]
+    refs = refs[4 * slots + 4 :]
+    grad_pre, pre_sums = refs[:slots], refs[slots : 2 * slots]
+    low, grad_attn, sums, total, grad_norm = refs[2 * slots :]
+    step, steps = pl.program_id(0), pl.num_programs(0)
 
     def body(span):
         rows = images * span
 
-        @pl.when(start)
+        @pl.when(step == 0)
         def _():
-            total[:rows, :] = base[:rows, :]
-            if first:
-                grad_norm[:rows, :] = jnp.zeros((rows, grad_norm.shape[1]), f32)
-            else:
-                grad_norm[:rows, :] = grad_base[:rows, :]
-
-        total[:rows, :] += dot(act[:rows, :], w2[...])
-        grad = dot(top[:rows, :], w2[...], NT) * slope[:rows, :].astype(f32)
-        grad_pre[:rows, :] = grad.astype(bf16)
-        sums[...] = col_sum(grad_pre[:rows, :].astype(f32))
-        grad_norm[:rows, :] += dot(grad_pre[:rows, :], w1[...], NT)
-
-    spans(flags, seq_len, body)
-
-
-def mid_back_kernel(seq_len, images, flags, grad_norm, mid, top, gain, grad_mid, grad_attn, sums):
-    def body(span):
-        for i in range(images):
-            rows = slice(i * span, (i + 1) * span)
-            unit, inverse = norm_parts(mid[rows, :])
-            grad = grad_norm[rows, :]
-            full = top[rows, :].astype(f32) + norm_grad(grad, unit, inverse, gain[...])
-            low = full.astype(bf16)
-            grad_mid[rows, :] = full
-            grad_attn[rows, :] = low
-            part = [col_sum(grad * unit), col_sum(grad), col_sum(low.astype(f32))]
-            for n, row in enumerate(part):
-                sums[n : n + 1, :] = row if i == 0 else sums[n : n + 1, :] + row
+            total[:rows, :] = mid[:rows, :]
+            grad_norm[:rows, :] = jnp.zeros((rows, grad_norm.shape[1]), f32)
+
+        for slot in range(slots):
+
+            @pl.when(step // (steps // slots) == slot)
+            def _():
+                total[:rows, :] += dot(act[slot][:rows, :], w2[slot][...])
+                grad = dot(top[:rows, :], w2[slot][...], NT) * slope[slot][:rows, :].astype(f32)
+                grad_pre[slot][:rows, :] = grad.astype(bf16)
+                pre_sums[slot][...] = col_sum(grad_pre[slot][:rows, :].astype(f32))
+                grad_norm[:rows, :] += dot(grad_pre[slot][:rows, :], w1[slot][...], NT)
+
+        @pl.when(step == steps - 1)
+        def _():
+            for i in range(images):
+                at = slice(i * span, (i + 1) * span)
+                low[at, :] = (total[at, :] + bias[...]).astype(bf16)
+                unit, inverse = norm_parts(mid[at, :])
+                grad = grad_norm[at, :]
+                full = top[at, :].astype(f32) + norm_grad(grad, unit, inverse, gain[...])
+                grad_attn[at, :] = full.astype(bf16)
+                part = [
+                    col_sum(grad * unit),
+                    col_sum(grad),
+                    col_sum(grad_attn[at, :].astype(f32)),
+                ]
+                for n, row in enumerate(part):
+                    sums[n : n + 1, :] = row if i == 0 else sums[n : n + 1, :] + row
 
     spans(flags, seq_len, body)
 
@@ -271,24 +272,24 @@
     spans(flags, seq_len, body)
 
 
-def spread_kernel(seq_len, images, flags, value, bias, keep, out):
+def spread_kernel(seq_len, images, flags, value, keep, out):
     def body(span):
         for i in range(images):
             rows = slice(i * span, (i + 1) * span)
-            low = (value[rows, :] + bias[...]).astype(bf16)
             pick = picks(keep[i : i + 1, :], span)
-            out[i * seq_len : (i + 1) * seq_len, :] = dot(pick, low, TN).astype(bf16)
+            out[i * seq_len : (i + 1) * seq_len, :] = dot(pick, value[rows, :], TN).astype(bf16)
 
     spans(flags, seq_len, body)
 
 
-def last_kernel(seq_len, images, flags, grad_norm, xc, grad_mid, gain, keep, out, sums):
+def last_kernel(seq_len, images, flags, grad_norm, xc, grad_attn, gain, keep, out, sums):
     def body(span):
         for i in range(images):
             rows = slice(i * span, (i + 1) * span)
             unit, inverse = norm_parts(xc[rows, :].astype(f32))
             grad = grad_norm[rows, :]
-            low = (grad_mid[rows, :] + norm_grad(grad, unit, inverse, gain[...])).astype(bf16)
+            low = grad_attn[rows, :].astype(f32) + norm_grad(grad, unit, inverse, gain[...])
+            low = low.astype(bf16)
             pick = picks(keep[i : i + 1, :], span)
             out[i * seq_len : (i + 1) * seq_len, :] = dot(pick, low, TN).astype(bf16)
             part = [col_sum(grad * unit), col_sum(grad)]
@@ -375,9 +376,9 @@
             out[...] = refs[n][...].astype(out.dtype)
 
 
-def last_place_kernel(matrix, count, flags, *refs):
-    pieces, (out, qkv) = refs[:count], refs[count:]
-    for n in range(count):
+def last_place_kernel(matrix, flags, *refs):
+    pieces, (out, qkv) = refs[:4], refs[-2:]
+    for n in range(4):
         which = matrix(n, flags)
 
         @pl.when((pl.program_id(0) == n) & (which == 0))
@@ -622,13 +623,14 @@
                 self.moving_b = start(chip_swap, sent, 1)
 
             def k_mid(self):
-                came = [(self.came, 0, 0)] + [(sent, 0, 0) for sent in self.sent]
-                self.total = self.source.make([0], True, came, 0, 2)
+                self.total = self.source.make([0], True, [(self.came, 0, 0)], 0, 2)
 
             def t_two(self):
-                total = self.total.value
+                total = self.total.value.astype(f32)
+                for sent in self.sent:
+                    total = total + sent.value.astype(f32)
                 sent, self.held_a = halves(total.reshape(-1, total.shape[-1]), low, 0)
-                self.moving_a = start(chip_swap, sent, 1)
+                self.moving_a = start(chip_swap, sent.astype(bf16), 1)
                 total = self.held_b.astype(f32) + self.moving_b.value.astype(f32)
                 self.held_b = total[0]
                 self.moving_b = [start(peer, total[slot].astype(bf16), slot) for slot in others]
@@ -744,25 +746,30 @@
                     return 2 * ((n % 4) // 2) + (bit ^ (n % 2))
 
                 half = width // 2
-                return run(
-                    "qkvjoin",
-                    static(last_place_kernel, matrix, 8),
-                    self.pieces,
-                    [whole((half, part))] * 8,
-                    [
-                        pl.BlockSpec((part, half), lambda w, f: (0, f[1 + images] ^ (w // 4))),
-                        pl.BlockSpec(
-                            (1, half, part),
-                            lambda w, f: (
-                                jnp.maximum(matrix(w, f) - 1, 0),
-                                f[1 + images] ^ (w // 4),
-                                0,
+                placed = ()
+                for far in range(2):
+                    placed = run(
+                        f"qkvjoin{far}",
+                        static(last_place_kernel, matrix),
+                        (*self.pieces[4 * far : 4 * far + 4], *placed),
+                        [whole((half, part))] * 4
+                        + [pl.BlockSpec(memory_space=pl.ANY)] * len(placed),
+                        [
+                            pl.BlockSpec((part, half), lambda w, f: (0, f[1 + images] ^ far)),
+                            pl.BlockSpec(
+                                (1, half, part),
+                                lambda w, f: (
+                                    jnp.maximum(matrix(w, f) - 1, 0),
+                                    f[1 + images] ^ far,
+                                    0,
+                                ),
                             ),
-                        ),
-                    ],
-                    [like((part, width), f32), like((3, width, part), f32)],
-                    grid=(8,),
-                )
+                        ],
+                        [like((part, width), f32), like((3, width, part), f32)],
+                        grid=(4,),
+                        input_output_aliases={5: 0, 6: 1} if placed else {},
+                    )
+                return placed
 
         def ordered(bit, mine, other):
             return jnp.where(
@@ -805,34 +812,59 @@
                 grid=(hidden // tile,),
             )
 
-        def ffn(slot):
-            nonlocal total, grad_norm2
-            first = grad_norm2 is None
-            tiles = pl.BlockSpec((tokens, tile), lambda g, f: (0, g))
-            total, grad_pres[slot], grad_norm2, pre_sums[slot] = run(
-                f"ffn{slot}",
-                static(ffn_kernel, seq_len, images, first),
-                (acts[slot], slopes[slot], top, fc2[slot], fc1[slot], total)
-                + (() if first else (grad_norm2,)),
+        def ffn():
+            block = max(128, 2 * tile // tensor)
+            steps = hidden // block
+
+            def at(slot):
+                return lambda g: jnp.clip(g - slot * steps, 0, steps - 1)
+
+            across = [
+                pl.BlockSpec((tokens, block), lambda g, f, at=at(slot): (0, at(g))) for slot in slots
+            ]
+            got = run(
+                "ffn",
+                static(ffn_kernel, seq_len, images, tensor),
+                (*acts, *slopes, *fc2, *fc1, top, mid, row(fc2_bias), g2),
                 [
-                    tiles,
-                    tiles,
+                    *across,
+                    *across,
+                    *[
+                        pl.BlockSpec((block, width), lambda g, f, at=at(slot): (at(g), 0))
+                        for slot in slots
+                    ],
+                    *[
+                        pl.BlockSpec((width, block), lambda g, f, at=at(slot): (0, at(g)))
+                        for slot in slots
+                    ],
                     whole(shape2),
-                    pl.BlockSpec((tile, width), lambda g, f: (g, 0)),
-                    pl.BlockSpec((width, tile), lambda g, f: (0, g)),
                     whole(shape2),
-                ]
-                + ([] if first else [whole(shape2)]),
-                [whole(shape2), tiles, whole(shape2), pl.BlockSpec((1, tile), lambda g, f: (0, g))],
+                    whole((1, width)),
+                    whole((1, width)),
+                ],
                 [
-                    like(shape2, f32),
-                    like((tokens, hidden), bf16),
-                    like(shape2, f32),
-                    like((1, hidden), f32),
+                    *across,
+                    *[
+                        pl.BlockSpec((1, block), lambda g, f, at=at(slot): (0, at(g)))
+                        for slot in slots
+                    ],
+                    whole(shape2),
+                    whole(shape2),
+                    whole((3, width)),
                 ],
-                grid=(hidden // tile,),
-                vmem=36 << 20,
+                [
+                    *[like((tokens, hidden), bf16)] * tensor,
+                    *[like((1, hidden), f32)] * tensor,
+                    like(shape2, bf16),
+                    like(shape2, bf16),
+                    like((3, width), f32),
+                ],
+                grid=(tensor * steps,),
+                scratch=[pltpu.VMEM(shape2, f32)] * 2,
+                vmem=40 << 20,
             )
+            grad_pres[:], pre_sums[:] = got[:tensor], got[tensor : 2 * tensor]
+            return got[2 * tensor :]
 
         def attend_back(slot):
             nonlocal grad_norm1
@@ -855,7 +887,6 @@
             )
 
         acts, slopes = [None] * tensor, [None] * tensor
-        total, grad_norm2 = None, None
         grad_pres, pre_sums = [None] * tensor, [None] * tensor
         grad_projs, proj_sums, grad_norm1 = [None] * tensor, [None] * tensor, None
 
@@ -914,34 +945,22 @@
         step()
 
 
-        total = mid
         w1.t_one()
         get_fc2.third()
         fc2 = [w_fc2] + [w for w, in get_fc2.full()]
-        for slot in slots:
-            ffn(slot)
+        low_out, grad_attn, sums2 = ffn()
         w2 = Reduce(Plain("fc1", [normed2], grad_pres, 256))
         w2.k_away()
-        step()
-
         w1.k_mid()
         step()
 
         w1.t_two()
         w2.t_core()
-        grad_mid, grad_attn, sums2 = run(
-            "midback",
-            static(mid_back_kernel, seq_len, images),
-            (grad_norm2, mid, top, g2),
-            [whole(shape2), whole(shape2), whole(shape2), whole((1, width))],
-            [whole(shape2), whole(shape2), whole((3, width))],
-            [like(shape2, f32), like(shape2, bf16), like((3, width), f32)],
-        )
+        w2.k_own()
+        step()
+
+        w1.t_z()
         attend_back(0)
-        step()
-
-        w1.t_z()
-        w2.k_own()
         step()
 
         w2.t_one()
@@ -950,18 +969,20 @@
             attend_back(slot)
         w3 = Apart(Packed())
         w3.k_away()
-        step()
-
         w2.k_mid()
         step()
 
         w2.t_two()
         w3.t_core()
         w1.t_up()
+        w3.k_own()
+        step()
+
+        w2.t_z()
         grad_input, sums1 = run(
             "last",
             static(last_kernel, seq_len, images),
-            (grad_norm1, xc, grad_mid, g1, keep),
+            (grad_norm1, xc, grad_attn, g1, keep),
             [whole(shape2), whole(shape2), whole(shape2), whole((1, width)), whole(keep.shape)],
             [whole(shape2), whole((2, width))],
             [like(shape2, bf16), like((2, width), f32)],
@@ -969,19 +990,18 @@
         layer_out = run(
             "spread",
             static(spread_kernel, seq_len, images),
-            (total, row(fc2_bias), keep),
-            [whole(shape2), whole((1, width)), whole(keep.shape)],
+            (low_out, keep),
+            [whole(shape2), whole(keep.shape)],
             whole(shape2),
             like(shape2, bf16),
         )
         step()
 
-        w2.t_z()
-        w3.k_own()
-        step()
-
         w3.t_one()
         w1.t_out()
+        w3.k_mid()
+        step()
+
         common = jnp.concatenate(
             [
                 sums1.value.reshape(-1),
@@ -998,50 +1018,46 @@
             for slot in slots
         ]
         vector = owned[0]
-        moving = [start(peer, owned[slot], slot) for slot in others]
-
-        def add(*mask):
+        moving = []
+
+        def add(move, *mask):
             nonlocal vector, moving
             for m in moving:
                 vector = vector + m.value
-            moving = [start(chip_swap if mask else core_swap, vector, *mask)] if mask != (0,) else []
-
-        step()
-
-        w3.k_mid()
-        step()
-
+            moving = [start(move, vector, *mask)] if move else []
+
+        moving = [start(peer, owned[slot], slot) for slot in others]
         w3.t_two()
         w2.t_full()
-        add()
         step()
 
         w3.t_three()
         w2.t_up()
         w1.t_share()
-        add(1)
+        add(core_swap)
         step()
 
         w3.t_full()
         w2.t_out()
-        add(2)
+        add(chip_swap, 1)
         grad_fc2 = w1.joined()
         step()
 
         w3.t_up()
         w2.t_share()
+        add(chip_swap, 2)
+        step()
+
+        w3.t_out()
         mask = 4
         while mask < chips:
-            add(mask)
+            add(chip_swap, mask)
             mask *= 2
-        step()
-
-        w3.t_out()
-        add(0)
         grad_fc1 = w2.joined()
         step()
 
         w3.t_share()
+        add(None)
         grad_out, grad_qkv = (g.value for g in w3.joined())
         layer_out = layer_out.value.reshape(inputs.shape)
         grad_input = grad_input.value.reshape(inputs.shape)

time: 420 us -> 412 us (0.981)
  waiting for transfers between devices: 128 us -> 122 us
    ppermute x60, waiting for transfers between devices: 128 us -> 122 us  [swap(): return lax.ppermute(value, axis, [(i, i ^ mask) for i in range(size)])]
    unnamed x209 -> x241, local copies, waits for them, and re-layouts: 34.2 us -> 38.2 us
    pallas_call x31 -> x30, Pallas kernels: 149 us -> 145 us  [kernel_call(): pl.pallas_call(body, name=name, grid_spec=pltpu.PrefetchScalarGridSpec(nu...]
  transfers between devices with their start and end apart: 60 -> 60, of which waited for: 26 -> 25; matrix products, arithmetic and copies ran while one was open for 8% -> 8% of each run, Pallas kernels for 32% -> 35%
where the time goes in v3:
time: 412 us; the launch traced here: 407 us
  Pallas kernels  145 us (35%)
  waiting for transfers between devices  122 us (30%)
  local copies, waits for them, and re-layouts  53.8 us (13%)
  starting transfers between devices  52.9 us (13%)
  other arithmetic  30 us (7%)
    pallas_call x30, Pallas kernels, kernel_call(): pl.pallas_call(body, name=name, grid_spec=pltpu.PrefetchScalarGridSpec(nu...  145 us
    ppermute x60, waiting for transfers between devices, swap(): return lax.ppermute(value, axis, [(i, i ^ mask) for i in range(size)])  122 us
    ppermute x60, starting transfers between devices, swap(): return lax.ppermute(value, axis, [(i, i ^ mask) for i in range(size)])  52.9 us
    unnamed x241, local copies, waits for them, and re-layouts  38.2 us
  transfers between devices with their start and end apart: 60, of which 25 were waited for; matrix products, arithmetic and copies ran while one was open for 8% of the time, Pallas kernels for 35%

profile of v3, /device:TPU:0, one launch (start us, length us, event | category | flops | bytes accessed | tf_op | source)
XLA Modules:
  0.0 406.9 jit_solution(18377989115101194517)
XLA Ops:
  6.2 2.9 collective-permute-start
  14.3 6.0 %attend0.1 = (bf16[3,640,512]{2,1,0:T(8,128)(2,1)S(1)}, bf16[640,512]{1,0:T(8,128)(2,1)S(1)}) custom-call(s32[6]{0:T(128)S(1)} %concatenate.55.flags, bf16[640,1024]{1,0:T(8,128)(2,1)S(1)} %get-tuple-element.245.normed, bf16[3,1024,512]{2,1,0:T(8,128)(2,1)S(1)} %copy-done.23, f32[3,1,512]{2,1,0:T(1,128)S(1)} %pad_maximum_fusion.4.shift), custom_call_target="tpu_custom_call" | custom-call | flops 1000 | bytes 1000 | tf_op jit(solution)/shard_map/attend0/pallas_call | solution.py:47
  21.6 11.1 %collective-permute-done.1 = f32[3072]{0:T(1024)S(1)} collective-permute-done((f32[3072]{0:T(1024)S(1)}, f32[3072]{0:T(1024)S(1)}, u32[]{:S(2)}, u32[]{:S(2)}) %collective-permute-start.1) | collective-permute-done | bytes 12320 | tf_op jit(solution)/shard_map/ppermute | solution.py:394
  37.3 20.2 %collective-permute-done.2.refs_1_ = bf16[1024,512]{1,0:T(8,128)(2,1)} collective-permute-done((bf16[1024,512]{1,0:T(8,128)(2,1)}, bf16[1024,512]{1,0:T(8,128)(2,1)}, u32[]{:S(2)}, u32[]{:S(2)}) %collective-permute-start.2) | collective-permute-done | bytes 1048608 | tf_op jit(solution)/shard_map/ppermute | solution.py:394
  57.5 2.9 collective-permute-done.4.refs_0_
  67.1 6.0 %attend1.1 = (bf16[3,640,512]{2,1,0:T(8,128)(2,1)S(1)}, bf16[640,512]{1,0:T(8,128)(2,1)S(1)}) custom-call(s32[6]{0:T(128)S(1)} %concatenate.55.flags, bf16[640,1024]{1,0:T(8,128)(2,1)S(1)} %get-tuple-element.245.normed, bf16[3,1024,512]{2,1,0:T(8,128)(2,1)S(1)} %bitcast.86, f32[3,1,512]{2,1,0:T(1,128)S(1)} %pad_maximum_fusion.5.shift), custom_call_target="tpu_custom_call" | custom-call | flops 1000 | bytes 1000 | tf_op jit(solution)/shard_map/attend1/pallas_call | solution.py:47
  80.5 4.8 %hidden0.1 = (bf16[640,2048]{1,0:T(8,128)(2,1)S(1)}, bf16[640,2048]{1,0:T(8,128)(2,1)S(1)}) custom-call(s32[6]{0:T(128)S(1)} %concatenate.55.flags, bf16[640,1024]{1,0:T(8,128)(2,1)S(1)} %get-tuple-element.260.normed.refs_0_.refs_1_, bf16[1024,2048]{1,0:T(8,128)(2,1)S(1)} %copy-done.16, f32[1,2048]{1,0:T(1,128)S(1)} %bitcast.93), custom_call_target="tpu_custom_call" | custom-call | flops 1000 | bytes 1000 | tf_op jit(solution)/shard_map/hidden0/pallas_call | solution.py:47
  89.1 4.8 %hidden1.1 = (bf16[640,2048]{1,0:T(8,128)(2,1)S(1)}, bf16[640,2048]{1,0:T(8,128)(2,1)S(1)}) custom-call(s32[6]{0:T(128)S(1)} %concatenate.55.flags, bf16[640,1024]{1,0:T(8,128)(2,1)S(1)} %get-tuple-element.260.normed.refs_0_.refs_1_, bf16[1024,2048]{1,0:T(8,128)(2,1)S(1)} %assemble.4.w.refs_7_, f32[1,2048]{1,0:T(1,128)S(1)} %bitcast.92), custom_call_target="tpu_custom_call" | custom-call | flops 1000 | bytes 1000 | tf_op jit(solution)/shard_map/hidden1/pallas_call | solution.py:47
  94.0 4.7 %fc20away.1 = bf16[2,1024,1024]{2,1,0:T(8,128)(2,1)} custom-call(s32[6]{0:T(128)S(1)} %concatenate.55.flags, bf16[640,2048]{1,0:T(8,128)(2,1)S(1)} %get-tuple-element.275.refs_0_, bf16[640,2048]{1,0:T(8,128)(2,1)S(1)} %get-tuple-element.274.refs_1_.refs_0_, bf16[640,1024]{1,0:T(8,128)(2,1)S(1)} %get-tuple-element.266.refs_2_.refs_3_.refs_1_.refs_8_, ...), custom_call_target="tpu_custom_call" | custom-call | flops 1000 | bytes 1000 | tf_op jit(solution)/shard_map/fc20away/pallas_call | solution.py:47
  98.7 4.4 %collective-permute-done.11.refs_0_ = bf16[512,1024]{1,0:T(8,128)(2,1)} collective-permute-done((bf16[512,1024]{1,0:T(8,128)(2,1)S(1)}, bf16[512,1024]{1,0:T(8,128)(2,1)}, u32[]{:S(2)}, u32[]{:S(2)}) %collective-permute-start.11) | collective-permute-done | bytes 1048608 | tf_op jit(solution)/shard_map/ppermute | solution.py:394
  114.9 3.7 fc20own.2
  132.2 19.1 %ffn.1 = (bf16[640,2048]{1,0:T(8,128)(2,1)S(1)}, bf16[640,2048]{1,0:T(8,128)(2,1)S(1)}, f32[1,2048]{1,0:T(1,128)S(1)}, f32[1,2048]{1,0:T(1,128)S(1)}, bf16[640,1...) custom-call(s32[6]{0:T(128)S(1)} %concatenate.55.flags, ...), custom_call_target="tpu_custom_call" | custom-call | flops 1000 | bytes 1000 | tf_op jit(solution)/shard_map/ffn/pallas_call | solution.py:47
  152.4 4.9 %fc10away.1 = bf16[2,512,2048]{2,1,0:T(8,128)(2,1)} custom-call(s32[6]{0:T(128)S(1)} %concatenate.55.flags, bf16[640,1024]{1,0:T(8,128)(2,1)S(1)} %get-tuple-element.260.normed.refs_0_.refs_1_, bf16[640,1024]{1,0:T(8,128)(2,1)S(1)} %get-tuple-element.260.normed.refs_0_.refs_1_, bf16[640,2048]{1,0:T(8,128)(2,1)S(1)} %get-tuple-element.307.refs_2_.refs_1_, ...), custom_call_target="tpu_custom_call" | custom-call | flops 1000 | bytes 1000 | tf_op jit(solution)/shard_map/fc10away/pallas_call | solution.py:47
  172.3 3.9 fc10own.2
  187.9 11.4 %aback0.1 = (bf16[3,640,512]{2,1,0:T(8,128)(2,1)S(1)}, f32[640,1024]{1,0:T(8,128)S(1)}, f32[2,512]{1,0:T(2,128)S(1)}) custom-call(s32[6]{0:T(128)S(1)} %concatenate.55.flags, bf16[640,1024]{1,0:T(8,128)(2,1)S(1)} %copy-done.1, bf16[512,1024]{1,0:T(8,128)(2,1)S(1)} %copy-done.36, bf16[3,640,512]{2,1,0:T(8,128)(2,1)S(1)} %copy-done.56, ...), custom_call_target="tpu_custom_call" | custom-call | flops 1000 | bytes 1000 | tf_op jit(solution)/shard_map/aback0/pallas_call | solution.py:47
  207.2 3.0 fc10own.3
  211.2 11.0 %aback1.1 = (bf16[3,640,512]{2,1,0:T(8,128)(2,1)S(1)}, f32[640,1024]{1,0:T(8,128)S(1)}, f32[2,512]{1,0:T(2,128)S(1)}) custom-call(s32[6]{0:T(128)S(1)} %concatenate.55.flags, bf16[640,1024]{1,0:T(8,128)(2,1)S(1)} %copy-done.1, bf16[512,1024]{1,0:T(8,128)(2,1)S(1)} %copy-done.43, bf16[3,640,512]{2,1,0:T(8,128)(2,1)S(1)} %copy-done.54, ...), custom_call_target="tpu_custom_call" | custom-call | flops 1000 | bytes 1000 | tf_op jit(solution)/shard_map/aback1/pallas_call | solution.py:47
  223.7 5.1 %qkv0away.1 = bf16[2,4,512,512]{3,2,1,0:T(8,128)(2,1)} custom-call(s32[6]{0:T(128)S(1)} %concatenate.55.flags, bf16[640,1024]{1,0:T(8,128)(2,1)S(1)} %copy-done.3, bf16[640,1024]{1,0:T(8,128)(2,1)S(1)} %copy-done.1, bf16[640,512]{1,0:T(8,128)(2,1)S(1)} %get-tuple-element.249.refs_0_, bf16[640,512]{1,0:T(8,128)(2,1)S(1)} %copy-done.28, ...), custom_call_target="tpu_custom_call" | custom-call | flops 1000 | bytes 1000 | tf_op jit(solution)/shard_map/qkv0away/pallas_call | solution.py:47
  238.8 3.5 qkv0own.2
  258.2 3.6 last.1
  272.4 15.8 %collective-permute-done.34.refs_1_ = bf16[512,1024]{1,0:T(8,128)(2,1)S(1)} collective-permute-done((bf16[512,1024]{1,0:T(8,128)(2,1)S(1)}, bf16[512,1024]{1,0:T(8,128)(2,1)S(1)}, u32[]{:S(2)}, u32[]{:S(2)}) %collective-permute-start.34) | collective-permute-done | bytes 1048608 | tf_op jit(solution)/shard_map/ppermute | solution.py:394
  297.6 7.2 %collective-permute-done.35 = f32[9216]{0:T(1024)S(1)} collective-permute-done((f32[9216]{0:T(1024)S(1)}, f32[9216]{0:T(1024)S(1)}, u32[]{:S(2)}, u32[]{:S(2)}) %collective-permute-start.35) | collective-permute-done | bytes 36896 | tf_op jit(solution)/shard_map/ppermute | solution.py:394
  304.8 7.4 %collective-permute-done.38 = bf16[128,2048]{1,0:T(8,128)(2,1)S(1)} collective-permute-done((bf16[128,2048]{1,0:T(8,128)(2,1)S(1)}, bf16[128,2048]{1,0:T(8,128)(2,1)S(1)}, u32[]{:S(2)}, u32[]{:S(2)}) %collective-permute-start.38) | collective-permute-done | bytes 524320 | tf_op jit(solution)/shard_map/ppermute | solution.py:394
  322.7 3.5 collective-permute-done.40
  326.2 9.8 %collective-permute-done.39 = bf16[256,512]{1,0:T(8,128)(2,1)} collective-permute-done((bf16[256,512]{1,0:T(8,128)(2,1)}, bf16[256,512]{1,0:T(8,128)(2,1)}, u32[]{:S(2)}, u32[]{:S(2)}) %collective-permute-start.39) | collective-permute-done | bytes 262176 | tf_op jit(solution)/shard_map/ppermute | solution.py:394
  344.6 7.0 %fc2join.1 = f32[2048,1024]{1,0:T(8,128)} custom-call(s32[6]{0:T(128)S(1)} %concatenate.55.flags, bf16[512,1024]{1,0:T(8,128)(2,1)S(1)} %copy-done.41, bf16[512,1024]{1,0:T(8,128)(2,1)S(1)} %copy-done.62, bf16[512,1024]{1,0:T(8,128)(2,1)} %collective-permute-done.42.refs_2_, bf16[512,1024]{1,0:T(8,128)(2,1)S(1)} %copy-done.64), custom_call_target="tpu_custom_call" | custom-call | flops 1000 | bytes 1000 | tf_op jit(solution)/shard_map/fc2join/pallas_call | solution.py:47
  351.7 12.8 %collective-permute-done.47 = f32[9216]{0:T(1024)S(1)} collective-permute-done((f32[9216]{0:T(1024)S(1)}, f32[9216]{0:T(1024)S(1)}, u32[]{:S(2)}, u32[]{:S(2)}) %collective-permute-start.47) | collective-permute-done | bytes 36896 | tf_op jit(solution)/shard_map/ppermute | solution.py:394
  364.5 3.0 collective-permute-done.45
  371.9 6.7 %collective-permute-done.52 = f32[9216]{0:T(1024)S(1)} collective-permute-done((f32[9216]{0:T(1024)S(1)}, f32[9216]{0:T(1024)S(1)}, u32[]{:S(2)}, u32[]{:S(2)}) %collective-permute-start.52) | collective-permute-done | bytes 36896 | tf_op jit(solution)/shard_map/ppermute | solution.py:394
  387.6 7.0 %fc1join.1 = f32[1024,2048]{1,0:T(8,128)} custom-call(s32[6]{0:T(128)S(1)} %concatenate.55.flags, bf16[256,2048]{1,0:T(8,128)(2,1)S(1)} %maximum_select_fusion.1.refs_0_, bf16[256,2048]{1,0:T(8,128)(2,1)} %collective-permute-done.46.refs_1_, bf16[256,2048]{1,0:T(8,128)(2,1)S(1)} %copy-done.68, bf16[256,2048]{1,0:T(8,128)(2,1)S(1)} %collective-permute-done.51.refs_3_), custom_call_target="tpu_custom_call" | custom-call | flops 1000 | bytes 1000 | tf_op jit(solution)/shard_map/fc1join/pallas_call | solution.py:47
  396.5 4.6 %qkvjoin0.1 = (f32[512,1024]{1,0:T(8,128)}, f32[3,1024,512]{2,1,0:T(8,128)}) custom-call(s32[6]{0:T(128)S(1)} %concatenate.55.flags, bf16[512,512]{1,0:T(8,128)(2,1)S(1)} %maximum_select_fusion.2.refs_0_, bf16[512,512]{1,0:T(8,128)(2,1)} %collective-permute-done.53.refs_1_, bf16[512,512]{1,0:T(8,128)(2,1)S(1)} %maximum_select_fusion.3.refs_2_, ...), custom_call_target="tpu_custom_call" | custom-call | flops 1000 | bytes 1000 | tf_op jit(solution)/shard_map/qkvjoin0/pallas_call | solution.py:47
  403.0 3.4 qkvjoin1.1
  (424 shorter events, 178.5 us)
Async XLA Ops:
  6.2 26.6 %collective-permute-start = (bf16[1024,512]{1,0:T(8,128)(2,1)}, bf16[1024,512]{1,0:T(8,128)(2,1)}, u32[]{:S(2)}, u32[]{:S(2)}) collective-permute-start(bf16[1024,512]{1,0:T(8,128)(2,1)} %pad_maximum_fusion), channel_id=1, source_target_pairs={{0,1},{1,0},{2,3},{3,2},{4,5},{5,4},{6,7},{7,6},{8,9},{9,8},{10,11... | collective-permute-start | bytes 3145736 | tf_op jit(solution)/shard_map/ppermute | solution.py:394
  9.1 23.6 %collective-permute-start.1 = (f32[3072]{0:T(1024)S(1)}, f32[3072]{0:T(1024)S(1)}, u32[]{:S(2)}, u32[]{:S(2)}) collective-permute-start(f32[3072]{0:T(1024)S(1)} %constant_dynamic-update-slice_fusion), channel_id=1, source_target_pairs={{0,1},{1,0},{2,3},{3,2},{4,5},{5,4},{6,7},{7,6},{8,9},{9,8},{10,11... | collective-permute-start | bytes 36872 | tf_op jit(solution)/shard_map/ppermute | solution.py:394
  32.7 24.8 %collective-permute-start.2 = (bf16[1024,512]{1,0:T(8,128)(2,1)}, bf16[1024,512]{1,0:T(8,128)(2,1)}, u32[]{:S(2)}, u32[]{:S(2)}) collective-permute-start(bf16[1024,512]{1,0:T(8,128)(2,1)} %collective-permute-done.refs_0_), channel_id=1, source_target_pairs={{0,4},{4,0},{8,12},{12,8},{16,20},{20,16},{24,28},{28,24},{1,5},{5... | collective-permute-start | bytes 3145736 | tf_op jit(solution)/shard_map/ppermute | solution.py:394
  34.5 23.0 %collective-permute-start.3 = (bf16[1024,512]{1,0:T(8,128)(2,1)}, bf16[1024,512]{1,0:T(8,128)(2,1)}, u32[]{:S(2)}, u32[]{:S(2)}) collective-permute-start(bf16[1024,512]{1,0:T(8,128)(2,1)} %collective-permute-done.refs_0_), channel_id=1, source_target_pairs={{0,2},{2,0},{1,3},{3,1},{4,6},{6,4},{5,7},{7,5},{8,10},{10,8},{9,1... | collective-permute-start | bytes 3145736 | tf_op jit(solution)/shard_map/ppermute | solution.py:394
  34.5 25.9 %collective-permute-start.4 = (bf16[256,2048]{1,0:T(8,128)(2,1)}, bf16[256,2048]{1,0:T(8,128)(2,1)}, u32[]{:S(2)}, u32[]{:S(2)}) collective-permute-start(bf16[256,2048]{1,0:T(8,128)(2,1)} %pad_maximum_fusion.1), channel_id=1, source_target_pairs={{0,1},{1,0},{2,3},{3,2},{4,5},{5,4},{6,7},{7,6},{8,9},{9,8},{10,11... | collective-permute-start | bytes 3145736 | tf_op jit(solution)/shard_map/ppermute | solution.py:394
  60.4 18.1 %collective-permute-start.8 = (bf16[256,2048]{1,0:T(8,128)(2,1)}, bf16[256,2048]{1,0:T(8,128)(2,1)S(1)}, u32[]{:S(2)}, u32[]{:S(2)}) collective-permute-start(bf16[256,2048]{1,0:T(8,128)(2,1)} %collective-permute-done.4.refs_0_), channel_id=1, source_target_pairs={{0,2},{2,0},{1,3},{3,1},{4,6},{6,4},{5,7},{7,5},{8,10},{10,8},{9,1... | collective-permute-start | bytes 3145736 | tf_op jit(solution)/shard_map/ppermute | solution.py:394
  62.2 16.2 %collective-permute-start.7 = (bf16[128,2048]{1,0:T(8,128)(2,1)S(1)}, bf16[128,2048]{1,0:T(8,128)(2,1)S(1)}, u32[]{:S(2)}, u32[]{:S(2)}) collective-permute-start(bf16[128,2048]{1,0:T(8,128)(2,1)S(1)} %get-tuple-element.240), channel_id=1, source_target_pairs={{0,8},{4,12},{8,0},{12,4},{16,24},{20,28},{24,16},{28,20},{1,9},{5... | collective-permute-start | bytes 1572872 | tf_op jit(solution)/shard_map/ppermute | solution.py:394
  63.9 14.6 %collective-permute-start.6 = (bf16[128,2048]{1,0:T(8,128)(2,1)S(1)}, bf16[128,2048]{1,0:T(8,128)(2,1)S(1)}, u32[]{:S(2)}, u32[]{:S(2)}) collective-permute-start(bf16[128,2048]{1,0:T(8,128)(2,1)S(1)} %get-tuple-element.239), channel_id=1, source_target_pairs={{0,4},{4,0},{8,12},{12,8},{16,20},{20,16},{24,28},{28,24},{1,5},{5... | collective-permute-start | bytes 1572872 | tf_op jit(solution)/shard_map/ppermute | solution.py:394
  78.5 24.7 %collective-permute-start.11 = (bf16[512,1024]{1,0:T(8,128)(2,1)S(1)}, bf16[512,1024]{1,0:T(8,128)(2,1)}, u32[]{:S(2)}, u32[]{:S(2)}) collective-permute-start(bf16[512,1024]{1,0:T(8,128)(2,1)S(1)} %pad_maximum_fusion.2), channel_id=1, source_target_pairs={{0,1},{1,0},{2,3},{3,2},{4,5},{5,4},{6,7},{7,6},{8,9},{9,8},{10,11... | collective-permute-start | bytes 3145736 | tf_op jit(solution)/shard_map/ppermute | solution.py:394
  103.1 17.6 %collective-permute-start.15 = (bf16[512,1024]{1,0:T(8,128)(2,1)}, bf16[512,1024]{1,0:T(8,128)(2,1)}, u32[]{:S(2)}, u32[]{:S(2)}) collective-permute-start(bf16[512,1024]{1,0:T(8,128)(2,1)} %collective-permute-done.11.refs_0_), channel_id=1, source_target_pairs={{0,2},{2,0},{1,3},{3,1},{4,6},{6,4},{5,7},{7,5},{8,10},{10,8},{9,1... | collective-permute-start | bytes 3145736 | tf_op jit(solution)/shard_map/ppermute | solution.py:394
  120.8 36.5 %collective-permute-start.17 = (bf16[2,256,1024]{2,1,0:T(8,128)(2,1)S(1)}, bf16[2,256,1024]{2,1,0:T(8,128)(2,1)S(1)}, u32[]{:S(2)}, u32[]{:S(2)}) collective-permute-start(bf16[2,256,1024]{2,1,0:T(8,128)(2,1)S(1)} %constant_dynamic-slice_fusion.2), channel_id=1, source_target_pairs={{0,4},{4,0},{8,12},{12,8},{16,20},{20,16},{24,28},{28,24},{1,5},{5... | collective-permute-start | bytes 3145736 | tf_op jit(solution)/shard_map/ppermute | solution.py:394
  121.9 35.5 %collective-permute-start.16 = (bf16[1,512,1024]{2,1,0:T(8,128)(2,1)S(1)}, bf16[1,512,1024]{2,1,0:T(8,128)(2,1)S(1)}, u32[]{:S(2)}, u32[]{:S(2)}) collective-permute-start(bf16[1,512,1024]{2,1,0:T(8,128)(2,1)S(1)} %fc21own.1), channel_id=1, source_target_pairs={{0,1},{1,0},{2,3},{3,2},{4,5},{5,4},{6,7},{7,6},{8,9},{9,8},{10,11... | collective-permute-start | bytes 3145736 | tf_op jit(solution)/shard_map/ppermute | solution.py:394
  162.4 15.1 %collective-permute-start.21 = (bf16[256,1024]{1,0:T(8,128)(2,1)}, bf16[256,1024]{1,0:T(8,128)(2,1)}, u32[]{:S(2)}, u32[]{:S(2)}) collective-permute-start(bf16[256,1024]{1,0:T(8,128)(2,1)} %fusion.5), channel_id=1, source_target_pairs={{0,1},{1,0},{2,3},{3,2},{4,5},{5,4},{6,7},{7,6},{8,9},{9,8},{10,11... | collective-permute-start | bytes 1572872 | tf_op jit(solution)/shard_map/ppermute | solution.py:394
  181.6 17.8 %collective-permute-start.23 = (bf16[256,1024]{1,0:T(8,128)(2,1)}, bf16[256,1024]{1,0:T(8,128)(2,1)}, u32[]{:S(2)}, u32[]{:S(2)}) collective-permute-start(bf16[256,1024]{1,0:T(8,128)(2,1)} %select_convert_fusion.1), channel_id=1, source_target_pairs={{0,8},{4,12},{8,0},{12,4},{16,24},{20,28},{24,16},{28,20},{1,9},{5... | collective-permute-start | bytes 1572872 | tf_op jit(solution)/shard_map/ppermute | solution.py:394
  199.4 29.9 %collective-permute-start.25 = (bf16[2,128,2048]{2,1,0:T(8,128)(2,1)S(1)}, bf16[2,128,2048]{2,1,0:T(8,128)(2,1)S(1)}, u32[]{:S(2)}, u32[]{:S(2)}) collective-permute-start(bf16[2,128,2048]{2,1,0:T(8,128)(2,1)S(1)} %constant_dynamic-slice_fusion.1), channel_id=1, source_target_pairs={{0,4},{4,0},{8,12},{12,8},{16,20},{20,16},{24,28},{28,24},{1,5},{5... | collective-permute-start | bytes 3145736 | tf_op jit(solution)/shard_map/ppermute | solution.py:394
  201.2 28.1 %collective-permute-start.24 = (bf16[1,256,2048]{2,1,0:T(8,128)(2,1)S(1)}, bf16[1,256,2048]{2,1,0:T(8,128)(2,1)S(1)}, u32[]{:S(2)}, u32[]{:S(2)}) collective-permute-start(bf16[1,256,2048]{2,1,0:T(8,128)(2,1)S(1)} %copy-done.66), channel_id=1, source_target_pairs={{0,1},{1,0},{2,3},{3,2},{4,5},{5,4},{6,7},{7,6},{8,9},{9,8},{10,11... | collective-permute-start | bytes 3145736 | tf_op jit(solution)/shard_map/ppermute | solution.py:394
  204.6 24.8 %collective-permute-start.26 = (bf16[256,1024]{1,0:T(8,128)(2,1)S(1)}, bf16[256,1024]{1,0:T(8,128)(2,1)S(1)}, u32[]{:S(2)}, u32[]{:S(2)}) collective-permute-start(bf16[256,1024]{1,0:T(8,128)(2,1)S(1)} %add_convert_fusion.3), channel_id=1, source_target_pairs={{0,16},{4,20},{8,24},{12,28},{16,0},{20,4},{24,8},{28,12},{1,17},{... | collective-permute-start | bytes 1572872 | tf_op jit(solution)/shard_map/ppermute | solution.py:394
  232.9 14.4 %collective-permute-start.30 = (bf16[256,1024]{1,0:T(8,128)(2,1)S(1)}, bf16[256,1024]{1,0:T(8,128)(2,1)S(1)}, u32[]{:S(2)}, u32[]{:S(2)}) collective-permute-start(bf16[256,1024]{1,0:T(8,128)(2,1)S(1)} %add_convert_fusion.2), channel_id=1, source_target_pairs={{0,8},{4,12},{8,0},{12,4},{16,24},{20,28},{24,16},{28,20},{1,9},{5... | collective-permute-start | bytes 1572872 | tf_op jit(solution)/shard_map/ppermute | solution.py:394
  234.9 14.4 %collective-permute-start.28 = (bf16[128,2048]{1,0:T(8,128)(2,1)S(1)}, bf16[128,2048]{1,0:T(8,128)(2,1)S(1)}, u32[]{:S(2)}, u32[]{:S(2)}) collective-permute-start(bf16[128,2048]{1,0:T(8,128)(2,1)S(1)} %fusion.6), channel_id=1, source_target_pairs={{0,1},{1,0},{2,3},{3,2},{4,5},{5,4},{6,7},{7,6},{8,9},{9,8},{10,11... | collective-permute-start | bytes 1572872 | tf_op jit(solution)/shard_map/ppermute | solution.py:394
  264.7 23.5 %collective-permute-start.34 = (bf16[512,1024]{1,0:T(8,128)(2,1)S(1)}, bf16[512,1024]{1,0:T(8,128)(2,1)S(1)}, u32[]{:S(2)}, u32[]{:S(2)}) collective-permute-start(bf16[512,1024]{1,0:T(8,128)(2,1)S(1)} %maximum_select_fusion.refs_0_), channel_id=1, source_target_pairs={{0,4},{4,0},{8,12},{12,8},{16,20},{20,16},{24,28},{28,24},{1,5},{5... | collective-permute-start | bytes 3145736 | tf_op jit(solution)/shard_map/ppermute | solution.py:394
  265.2 23.1 %collective-permute-start.33 = (bf16[2,512,512]{2,1,0:T(8,128)(2,1)S(1)}, bf16[2,512,512]{2,1,0:T(8,128)(2,1)S(1)}, u32[]{:S(2)}, u32[]{:S(2)}) collective-permute-start(bf16[2,512,512]{2,1,0:T(8,128)(2,1)S(1)} %constant_dynamic-slice_fusion), channel_id=1, source_target_pairs={{0,8},{4,12},{8,0},{12,4},{16,24},{20,28},{24,16},{28,20},{1,9},{5... | collective-permute-start | bytes 3145736 | tf_op jit(solution)/shard_map/ppermute | solution.py:394
  266.5 22.7 %collective-permute-start.32 = (bf16[1,2,512,512]{3,2,1,0:T(8,128)(2,1)S(1)}, bf16[1,2,512,512]{3,2,1,0:T(8,128)(2,1)S(1)}, u32[]{:S(2)}, u32[]{:S(2)}) collective-permute-start(bf16[1,2,512,512]{3,2,1,0:T(8,128)(2,1)S(1)} %copy-done.70), channel_id=1, source_target_pairs={{0,1},{1,0},{2,3},{3,2},{4,5},{5,4},{6,7},{7,6},{8,9},{9,8},{10,11... | collective-permute-start | bytes 3145736 | tf_op jit(solution)/shard_map/ppermute | solution.py:394
  289.2 23.1 %collective-permute-start.38 = (bf16[128,2048]{1,0:T(8,128)(2,1)S(1)}, bf16[128,2048]{1,0:T(8,128)(2,1)S(1)}, u32[]{:S(2)}, u32[]{:S(2)}) collective-permute-start(bf16[128,2048]{1,0:T(8,128)(2,1)S(1)} %add_convert_fusion.1), channel_id=1, source_target_pairs={{0,16},{4,20},{8,24},{12,28},{16,0},{20,4},{24,8},{28,12},{1,17},{... | collective-permute-start | bytes 1572872 | tf_op jit(solution)/shard_map/ppermute | solution.py:394
  293.3 19.0 %collective-permute-start.37 = (bf16[512,512]{1,0:T(8,128)(2,1)}, bf16[512,512]{1,0:T(8,128)(2,1)}, u32[]{:S(2)}, u32[]{:S(2)}) collective-permute-start(bf16[512,512]{1,0:T(8,128)(2,1)} %fusion.7), channel_id=1, source_target_pairs={{0,1},{1,0},{2,3},{3,2},{4,5},{5,4},{6,7},{7,6},{8,9},{9,8},{10,11... | collective-permute-start | bytes 1572872 | tf_op jit(solution)/shard_map/ppermute | solution.py:394
  296.1 16.2 %collective-permute-start.36 = (bf16[512,512]{1,0:T(8,128)(2,1)}, bf16[512,512]{1,0:T(8,128)(2,1)}, u32[]{:S(2)}, u32[]{:S(2)}) collective-permute-start(bf16[512,512]{1,0:T(8,128)(2,1)} %dynamic-slice_convert_fusion), channel_id=1, source_target_pairs={{0,4},{4,0},{8,12},{12,8},{16,20},{20,16},{24,28},{28,24},{1,5},{5... | collective-permute-start | bytes 1572872 | tf_op jit(solution)/shard_map/ppermute | solution.py:394
  313.1 22.9 %collective-permute-start.43 = (bf16[512,1024]{1,0:T(8,128)(2,1)S(1)}, bf16[512,1024]{1,0:T(8,128)(2,1)S(1)}, u32[]{:S(2)}, u32[]{:S(2)}) collective-permute-start(bf16[512,1024]{1,0:T(8,128)(2,1)S(1)} %copy-done.62), channel_id=1, source_target_pairs={{0,2},{2,0},{1,3},{3,1},{4,6},{6,4},{5,7},{7,5},{8,10},{10,8},{9,1... | collective-permute-start | bytes 3145736 | tf_op jit(solution)/shard_map/ppermute | solution.py:394
  313.6 23.4 %collective-permute-start.42 = (bf16[512,1024]{1,0:T(8,128)(2,1)S(1)}, bf16[512,1024]{1,0:T(8,128)(2,1)}, u32[]{:S(2)}, u32[]{:S(2)}) collective-permute-start(bf16[512,1024]{1,0:T(8,128)(2,1)S(1)} %copy-done.41), channel_id=1, source_target_pairs={{0,2},{2,0},{1,3},{3,1},{4,6},{6,4},{5,7},{7,5},{8,10},{10,8},{9,1... | collective-permute-start | bytes 3145736 | tf_op jit(solution)/shard_map/ppermute | solution.py:394
  315.8 20.2 %collective-permute-start.41 = (bf16[128,2048]{1,0:T(8,128)(2,1)}, bf16[128,2048]{1,0:T(8,128)(2,1)}, u32[]{:S(2)}, u32[]{:S(2)}) collective-permute-start(bf16[128,2048]{1,0:T(8,128)(2,1)} %add_convert_fusion), channel_id=1, source_target_pairs={{0,8},{4,12},{8,0},{12,4},{16,24},{20,28},{24,16},{28,20},{1,9},{5... | collective-permute-start | bytes 1572872 | tf_op jit(solution)/shard_map/ppermute | solution.py:394
  320.7 15.3 %collective-permute-start.39 = (bf16[256,512]{1,0:T(8,128)(2,1)}, bf16[256,512]{1,0:T(8,128)(2,1)}, u32[]{:S(2)}, u32[]{:S(2)}) collective-permute-start(bf16[256,512]{1,0:T(8,128)(2,1)} %dynamic-slice_convert_fusion.4), channel_id=1, source_target_pairs={{0,8},{4,12},{8,0},{12,4},{16,24},{20,28},{24,16},{28,20},{1,9},{5... | collective-permute-start | bytes 786440 | tf_op jit(solution)/shard_map/ppermute | solution.py:394
  338.9 28.5 %collective-permute-start.46 = (bf16[256,2048]{1,0:T(8,128)(2,1)S(1)}, bf16[256,2048]{1,0:T(8,128)(2,1)}, u32[]{:S(2)}, u32[]{:S(2)}) collective-permute-start(bf16[256,2048]{1,0:T(8,128)(2,1)S(1)} %maximum_select_fusion.1.refs_0_), channel_id=1, source_target_pairs={{0,4},{4,0},{8,12},{12,8},{16,20},{20,16},{24,28},{28,24},{1,5},{5... | collective-permute-start | bytes 3145736 | tf_op jit(solution)/shard_map/ppermute | solution.py:394
  342.1 25.4 %collective-permute-start.45 = (bf16[512,512]{1,0:T(8,128)(2,1)S(1)}, bf16[512,512]{1,0:T(8,128)(2,1)S(1)}, u32[]{:S(2)}, u32[]{:S(2)}) collective-permute-start(bf16[512,512]{1,0:T(8,128)(2,1)S(1)} %pad_maximum_fusion.3), channel_id=1, source_target_pairs={{0,16},{4,20},{8,24},{12,28},{16,0},{20,4},{24,8},{28,12},{1,17},{... | collective-permute-start | bytes 1572872 | tf_op jit(solution)/shard_map/ppermute | solution.py:394
  343.6 20.9 %collective-permute-start.47 = (f32[9216]{0:T(1024)S(1)}, f32[9216]{0:T(1024)S(1)}, u32[]{:S(2)}, u32[]{:S(2)}) collective-permute-start(f32[9216]{0:T(1024)S(1)} %add.187), channel_id=1, source_target_pairs={{0,4},{4,0},{8,12},{12,8},{16,20},{20,16},{24,28},{28,24},{1,5},{5... | collective-permute-start | bytes 110600 | tf_op jit(solution)/shard_map/ppermute | solution.py:394
  (143 other events, 892.0 us)

commit v4 on v3

--- a/solution.py
+++ b/solution.py
@@ -365,6 +365,59 @@
                     begin += rows
     for copy in copies:
         copy.wait()
+
+
+def fold_kernel(plan, flags, *refs):
+    count = sum(sum(counts) for _, counts, _ in plan)
+    ins, outs = list(refs[:count]), list(refs[count:])
+
+    def take(n):
+        got = ins[:n]
+        del ins[:n]
+        return got
+
+    def put(group, at=...):
+        total = group[0][at].astype(f32)
+        for ref in group[1:]:
+            total = total + ref[at].astype(f32)
+        return total.astype(bf16)
+
+    for kind, counts, where in plan:
+        groups = [take(n) for n in counts]
+        shape = groups[0][0].shape
+        if kind == "rows":
+            size = shape[-2] // 2
+            for half in (1 - flags[where], flags[where]):
+                at = (pl.ds(pl.multiple_of(half * size, 16), size), slice(None))
+                at = (slice(None),) * (len(shape) - 2) + at
+                outs.pop(0)[...] = put(groups[0], at)
+        elif kind == "slots":
+            for slot in range(shape[0]):
+                outs.pop(0)[...] = put(groups[0], slot)
+        elif kind == "pick":
+            sent, held = outs.pop(0), outs.pop(0)
+            for bit in range(2):
+
+                @pl.when(flags[where] == bit)
+                def _():
+                    held[...] = put(groups[bit])
+                    sent[...] = put(groups[1 - bit])
+
+        elif kind == "sum":
+            outs.pop(0)[...] = put(groups[0])
+        elif kind == "order":
+            out = outs.pop(0)
+            for half, group in zip((flags[where], 1 - flags[where]), groups):
+                begin = pl.multiple_of(half * shape[0], 16)
+                out[pl.ds(begin, shape[0]), :] = put(group)
+        elif kind == "join":
+            out = outs.pop(0)
+            for n, group in enumerate(groups):
+                out[n * shape[0] : (n + 1) * shape[0], :] = put(group)
+        else:
+            size = shape[0] // 2
+            for n in range(2):
+                outs.pop(0)[...] = put(groups[0], slice(n * size, (n + 1) * size))
 
 
 def place_kernel(count, flags, *refs):
@@ -453,6 +506,7 @@
                 opened.append(self)
 
         opened = []
+        begun = []
         gate = Box(flags)
 
         def step():
@@ -460,6 +514,7 @@
             for box, value in zip(opened, values):
                 box.value = value
             opened[:] = [gate]
+            begun[:] = [True]
 
         def run(name, body, args, in_specs, out_specs, out_shape, grid=(1,), **kw):
             args = [a.value if isinstance(a, Box) else a for a in args]
@@ -470,7 +525,37 @@
 
         def start(move, value, *mask):
             value = value.value if isinstance(value, Box) else value
-            return Box(move(after(value, gate.value), *mask))
+            return Box(move(after(value, gate.value) if begun else value, *mask))
+
+        LOW, HIGH = 2 + images, 3 + images
+
+        def fold(*plan):
+            ins, outs, steps = [], [], []
+            for kind, where, *groups in plan:
+                groups = [[g.value if isinstance(g, Box) else g for g in group] for group in groups]
+                for group in groups:
+                    ins += group
+                shape = groups[0][0].shape
+                half = (*shape[:-2], shape[-2] // 2, shape[-1])
+                outs += {
+                    "rows": [half, half],
+                    "slots": [shape[1:]] * shape[0],
+                    "pick": [shape, shape],
+                    "sum": [shape],
+                    "order": [(2 * shape[0], *shape[1:])],
+                    "join": [(len(groups) * shape[0], *shape[1:])],
+                    "cut": [half, half],
+                }[kind]
+                steps.append((kind, [len(g) for g in groups], where))
+            got = run(
+                "fold",
+                static(fold_kernel, steps),
+                ins,
+                [whole(v.shape) for v in ins],
+                [whole(shape) for shape in outs],
+                [like(shape, bf16) for shape in outs],
+            )
+            return [g.value for g in got]
 
 
         class Fetch:
@@ -499,11 +584,8 @@
                 self.got = []
                 for m in self.mine:
                     if self.split:
-                        rows = m.value.shape[0] // 2
-                        beside = [
-                            start(chip_swap, m.value[:rows], 1),
-                            start(chip_swap, m.value[rows:], 2),
-                        ]
+                        upper, lower = fold(("cut", 0, [m]))
+                        beside = [start(chip_swap, upper, 1), start(chip_swap, lower, 2)]
                     else:
                         beside = [start(chip_swap, m, 1)]
                     self.got.append([m, *beside, start(core_swap, m)])
@@ -619,44 +701,40 @@
                 self.sent = [start(peer, value, slot) for value, slot in zip(self.first, others)]
                 total = self.second.value
                 total = total.reshape(tensor, -1, total.shape[-1])
-                sent, self.held_b = halves(total, low, 1)
+                sent, self.held_b = fold(("rows", LOW, [total]))
                 self.moving_b = start(chip_swap, sent, 1)
 
             def k_mid(self):
                 self.total = self.source.make([0], True, [(self.came, 0, 0)], 0, 2)
 
             def t_two(self):
-                total = self.total.value.astype(f32)
-                for sent in self.sent:
-                    total = total + sent.value.astype(f32)
-                sent, self.held_a = halves(total.reshape(-1, total.shape[-1]), low, 0)
-                self.moving_a = start(chip_swap, sent.astype(bf16), 1)
-                total = self.held_b.astype(f32) + self.moving_b.value.astype(f32)
-                self.held_b = total[0]
-                self.moving_b = [start(peer, total[slot].astype(bf16), slot) for slot in others]
+                cols = self.total.value.shape[-1]
+                parts = [v.value.reshape(-1, cols) for v in (self.total, *self.sent)]
+                sent, self.held_a, self.held_b, *others_b = fold(
+                    ("rows", LOW, parts), ("slots", 0, [self.held_b, self.moving_b])
+                )
+                self.moving_a = start(chip_swap, sent, 1)
+                self.moving_b = [start(peer, v, slot) for v, slot in zip(others_b, others)]
 
             def t_z(self):
-                total_a = self.held_a.astype(f32) + self.moving_a.value.astype(f32)
-                total_b = self.held_b
-                for moving in self.moving_b:
-                    total_b = total_b + moving.value.astype(f32)
-                self.held = jnp.where(high == 0, total_a, total_b)
-                sent = jnp.where(high == 0, total_b, total_a).astype(bf16)
+                sent, self.held = fold(
+                    ("pick", HIGH, [self.held_a, self.moving_a], [self.held_b, *self.moving_b])
+                )
                 self.moving = start(chip_swap, sent, 2)
 
             def t_full(self):
                 mask = 4
                 while mask < chips:
-                    self.held = (self.held.astype(f32) + self.moving.value.astype(f32)).astype(bf16)
+                    (self.held,) = fold(("sum", 0, [self.held, self.moving]))
                     self.moving = start(chip_swap, self.held, mask)
                     mask *= 2
 
             def t_up(self):
-                self.held = (self.held.astype(f32) + self.moving.value.astype(f32)).astype(bf16)
+                (self.held,) = fold(("sum", 0, [self.held, self.moving]))
                 self.moving = start(chip_swap, self.held, 2)
 
             def t_out(self):
-                self.held = ordered(high, self.held, self.moving.value)
+                (self.held,) = fold(("order", HIGH, [self.held], [self.moving]))
                 self.moving = start(chip_swap, self.held, 1)
 
             def t_share(self):
@@ -685,54 +763,43 @@
                     grid=(4, 2),
                 )
 
-        def halves(value, bit, axis):
-            size = value.shape[axis] // 2
-            return (
-                lax.dynamic_slice_in_dim(value, (1 - bit) * size, size, axis=axis),
-                lax.dynamic_slice_in_dim(value, bit * size, size, axis=axis),
-            )
-
         class Apart(Reduce):
             def t_one(self):
                 self.sent = [start(peer, value, slot) for value, slot in zip(self.first, others)]
                 total = self.second.value
                 total = total.reshape(tensor, -1, total.shape[-1])
-                sent, self.held_b = halves(total, high, 1)
+                sent, self.held_b = fold(("rows", HIGH, [total]))
                 self.moving_b = start(chip_swap, sent, 2)
 
             def t_three(self):
-                total_a = self.held_a.astype(f32) + self.moving_a.value.astype(f32)
-                sent_a, self.held_a = halves(total_a, high, 0)
-                total_b = self.held_b
-                for moving in self.moving_b:
-                    total_b = total_b + moving.value.astype(f32)
-                sent_b, self.held_b = halves(total_b, low, 0)
-                self.moving_a = start(chip_swap, sent_a.astype(bf16), 2)
-                self.moving_b = start(chip_swap, sent_b.astype(bf16), 1)
+                sent_a, self.held_a, sent_b, self.held_b = fold(
+                    ("rows", HIGH, [self.held_a, self.moving_a]),
+                    ("rows", LOW, [self.held_b, *self.moving_b]),
+                )
+                self.moving_a = start(chip_swap, sent_a, 2)
+                self.moving_b = start(chip_swap, sent_b, 1)
 
             def t_full(self):
-                held = [
-                    h.astype(f32) + m.value.astype(f32)
-                    for h, m in ((self.held_a, self.moving_a), (self.held_b, self.moving_b))
-                ]
-                self.held = jnp.concatenate(held).astype(bf16)
+                (self.held,) = fold(
+                    ("join", 0, [self.held_a, self.moving_a], [self.held_b, self.moving_b])
+                )
                 self.moving = start(chip_swap, self.held, 4)
                 mask = 8
                 while mask < chips:
-                    self.held = (self.held.astype(f32) + self.moving.value.astype(f32)).astype(bf16)
+                    (self.held,) = fold(("sum", 0, [self.held, self.moving]))
                     self.moving = start(chip_swap, self.held, mask)
                     mask *= 2
 
             def t_up(self):
-                held, moving = (v.reshape(2, -1, v.shape[-1]) for v in (self.held, self.moving.value))
-                self.held_a = (held[0].astype(f32) + moving[0].astype(f32)).astype(bf16)
-                self.held_b = (held[1].astype(f32) + moving[1].astype(f32)).astype(bf16)
+                self.held_a, self.held_b = fold(("cut", 0, [self.held, self.moving]))
                 self.moving_a = start(chip_swap, self.held_a, 2)
                 self.moving_b = start(chip_swap, self.held_b, 1)
 
             def t_out(self):
-                self.held_a = ordered(high, self.held_a, self.moving_a.value)
-                self.held_b = ordered(low, self.held_b, self.moving_b.value)
+                self.held_a, self.held_b = fold(
+                    ("order", HIGH, [self.held_a], [self.moving_a]),
+                    ("order", LOW, [self.held_b], [self.moving_b]),
+                )
                 self.moving_a = start(chip_swap, self.held_a, 1)
                 self.moving_b = start(chip_swap, self.held_b, 2)
 
@@ -770,11 +837,6 @@
                         input_output_aliases={5: 0, 6: 1} if placed else {},
                     )
                 return placed
-
-        def ordered(bit, mine, other):
-            return jnp.where(
-                bit == 0, jnp.concatenate([mine, other]), jnp.concatenate([other, mine])
-            )
 
 
         def attend(slot, w):

time: 412 us -> 378 us (0.917)
  local copies, waits for them, and re-layouts: 53.8 us -> 21.2 us
  other arithmetic: 30 us -> 3.08 us
  waiting for transfers between devices: 122 us -> 148 us
    ppermute x60, waiting for transfers between devices: 122 us -> 148 us  [swap(): return lax.ppermute(value, axis, [(i, i ^ mask) for i in range(size)])]
    unnamed x241 -> x93, local copies, waits for them, and re-layouts: 38.2 us -> 14.4 us
    convert_element_type x7 -> x0, other arithmetic: 11.1 us -> none  [the longest x2 3.64 us: t_up(): (self.held.astype(f32) + self.moving.value.astype(f32)).astype(bf16)]
    add x8 -> x0, other arithmetic: 7.94 us -> none  [the longest x3 4.19 us: t_two(): total = self.held_b.astype(f32) + self.moving_b.value.astype(f32)]
    select_n x4 -> x0, other arithmetic: 4.96 us -> none  [ordered(): jnp.where(bit == 0, jnp.concatenate([mine, other]), jnp.concatenate([othe...]
    convert_element_type x8 -> x0, local copies, waits for them, and re-layouts: 4.81 us -> none  [the longest x3 1.99 us: t_two(): total[slot].astype(bf16)]
    pallas_call x30 -> x50, Pallas kernels: 145 us -> 145 us  [kernel_call(): pl.pallas_call(body, name=name, grid_spec=pltpu.PrefetchScalarGridSpec(nu...]
  transfers between devices with their start and end apart: 60 -> 60, of which waited for: 25 -> 33; matrix products, arithmetic and copies ran while one was open for 8% -> 2% of each run, Pallas kernels for 35% -> 36%
where the time goes in v4:
time: 378 us; the launch traced here: 374 us
  waiting for transfers between devices  148 us (39%)
  Pallas kernels  145 us (38%)
  starting transfers between devices  54.8 us (14%)
  local copies, waits for them, and re-layouts  21.2 us (6%)
    ppermute x60, waiting for transfers between devices, swap(): return lax.ppermute(value, axis, [(i, i ^ mask) for i in range(size)])  148 us
    pallas_call x50, Pallas kernels, kernel_call(): pl.pallas_call(body, name=name, grid_spec=pltpu.PrefetchScalarGridSpec(nu...  145 us
    ppermute x60, starting transfers between devices, swap(): return lax.ppermute(value, axis, [(i, i ^ mask) for i in range(size)])  54.8 us
    unnamed x93, local copies, waits for them, and re-layouts  14.4 us
  transfers between devices with their start and end apart: 60, of which 33 were waited for; matrix products, arithmetic and copies ran while one was open for 2% of the time, Pallas kernels for 36%

profile of v4, /device:TPU:0, one launch (start us, length us, event | category | flops | bytes accessed | tf_op | source)
XLA Modules:
  0.0 374.4 jit_solution(162606455249313683)
XLA Ops:
  18.9 6.0 %attend0.1 = (bf16[3,640,512]{2,1,0:T(8,128)(2,1)S(1)}, bf16[640,512]{1,0:T(8,128)(2,1)S(1)}) custom-call(s32[6]{0:T(128)S(1)} %concatenate.27.flags, bf16[640,1024]{1,0:T(8,128)(2,1)S(1)} %get-tuple-element.277.normed, bf16[3,1024,512]{2,1,0:T(8,128)(2,1)S(1)} %copy-done.3, f32[3,1,512]{2,1,0:T(1,128)S(1)} %pad_maximum_fusion.3.shift), custom_call_target="tpu_custom_call" | custom-call | flops 1000 | bytes 1000 | tf_op jit(solution)/shard_map/attend0/pallas_call | solution.py:47
  26.2 4.3 %collective-permute-done.1 = f32[3072]{0:T(1024)S(1)} collective-permute-done((f32[3072]{0:T(1024)S(1)}, f32[3072]{0:T(1024)S(1)}, u32[]{:S(2)}, u32[]{:S(2)}) %collective-permute-start.1) | collective-permute-done | bytes 12320 | tf_op jit(solution)/shard_map/ppermute | solution.py:447
  33.8 21.5 %collective-permute-done.2.refs_1_ = bf16[1024,512]{1,0:T(8,128)(2,1)} collective-permute-done((bf16[1024,512]{1,0:T(8,128)(2,1)}, bf16[1024,512]{1,0:T(8,128)(2,1)}, u32[]{:S(2)}, u32[]{:S(2)}) %collective-permute-start.2) | collective-permute-done | bytes 1048608 | tf_op jit(solution)/shard_map/ppermute | solution.py:447
  66.5 6.0 %attend1.1 = (bf16[3,640,512]{2,1,0:T(8,128)(2,1)S(1)}, bf16[640,512]{1,0:T(8,128)(2,1)S(1)}) custom-call(s32[6]{0:T(128)S(1)} %concatenate.27.flags, bf16[640,1024]{1,0:T(8,128)(2,1)S(1)} %get-tuple-element.277.normed, bf16[3,1024,512]{2,1,0:T(8,128)(2,1)S(1)} %bitcast.49, f32[3,1,512]{2,1,0:T(1,128)S(1)} %pad_maximum_fusion.4.shift), custom_call_target="tpu_custom_call" | custom-call | flops 1000 | bytes 1000 | tf_op jit(solution)/shard_map/attend1/pallas_call | solution.py:47
  78.8 4.9 %hidden0.1 = (bf16[640,2048]{1,0:T(8,128)(2,1)S(1)}, bf16[640,2048]{1,0:T(8,128)(2,1)S(1)}) custom-call(s32[6]{0:T(128)S(1)} %concatenate.27.flags, bf16[640,1024]{1,0:T(8,128)(2,1)S(1)} %get-tuple-element.292.normed.refs_0_.refs_1_, bf16[1024,2048]{1,0:T(8,128)(2,1)S(1)} %copy-done.1, f32[1,2048]{1,0:T(1,128)S(1)} %bitcast.60), custom_call_target="tpu_custom_call" | custom-call | flops 1000 | bytes 1000 | tf_op jit(solution)/shard_map/hidden0/pallas_call | solution.py:47
  87.5 4.9 %hidden1.1 = (bf16[640,2048]{1,0:T(8,128)(2,1)S(1)}, bf16[640,2048]{1,0:T(8,128)(2,1)S(1)}) custom-call(s32[6]{0:T(128)S(1)} %concatenate.27.flags, bf16[640,1024]{1,0:T(8,128)(2,1)S(1)} %get-tuple-element.292.normed.refs_0_.refs_1_, bf16[1024,2048]{1,0:T(8,128)(2,1)S(1)} %assemble.4.w.refs_7_, f32[1,2048]{1,0:T(1,128)S(1)} %bitcast.59), custom_call_target="tpu_custom_call" | custom-call | flops 1000 | bytes 1000 | tf_op jit(solution)/shard_map/hidden1/pallas_call | solution.py:47
  93.9 3.7 fc20away.1
  103.0 4.9 %collective-permute-done.12.refs_2_.refs_4_ = bf16[2,1024,1024]{2,1,0:T(8,128)(2,1)S(1)} collective-permute-done((bf16[2,1024,1024]{2,1,0:T(8,128)(2,1)S(1)}, bf16[2,1024,1024]{2,1,0:T(8,128)(2,1)S(1)}, u32[]{:S(2)}, u32[]{:S(2)}) %collective-permute-start.12) | collective-permute-done | bytes 4194336 | tf_op jit(solution)/shard_map/ppermute | solution.py:447
  112.4 3.3 collective-permute-done.14.refs_2_
  126.4 19.1 %ffn.1 = (bf16[640,2048]{1,0:T(8,128)(2,1)S(1)}, bf16[640,2048]{1,0:T(8,128)(2,1)S(1)}, f32[1,2048]{1,0:T(1,128)S(1)}, f32[1,2048]{1,0:T(1,128)S(1)}, bf16[640,1...) custom-call(s32[6]{0:T(128)S(1)} %concatenate.27.flags, ...), custom_call_target="tpu_custom_call" | custom-call | flops 1000 | bytes 1000 | tf_op jit(solution)/shard_map/ffn/pallas_call | solution.py:47
  145.5 3.9 %fc10away.1 = bf16[2,512,2048]{2,1,0:T(8,128)(2,1)S(1)} custom-call(s32[6]{0:T(128)S(1)} %concatenate.27.flags, bf16[640,1024]{1,0:T(8,128)(2,1)S(1)} %get-tuple-element.292.normed.refs_0_.refs_1_, bf16[640,1024]{1,0:T(8,128)(2,1)S(1)} %get-tuple-element.292.normed.refs_0_.refs_1_, bf16[640,2048]{1,0:T(8,128)(2,1)S(1)} %get-tuple-element.347.refs_2_.refs_1_, ...), custom_call_target="tpu_custom_call" | custom-call | flops 1000 | bytes 1000 | tf_op jit(solution)/shard_map/fc10away/pallas_call | solution.py:47
  160.1 6.4 %collective-permute-done.21.refs_3_ = bf16[256,1024]{1,0:T(8,128)(2,1)S(1)} collective-permute-done((bf16[256,1024]{1,0:T(8,128)(2,1)S(1)}, bf16[256,1024]{1,0:T(8,128)(2,1)S(1)}, u32[]{:S(2)}, u32[]{:S(2)}) %collective-permute-start.21) | collective-permute-done | bytes 524320 | tf_op jit(solution)/shard_map/ppermute | solution.py:447
  169.2 11.4 %aback0.1 = (bf16[3,640,512]{2,1,0:T(8,128)(2,1)S(1)}, f32[640,1024]{1,0:T(8,128)S(1)}, f32[2,512]{1,0:T(2,128)S(1)}) custom-call(s32[6]{0:T(128)S(1)} %concatenate.27.flags, bf16[640,1024]{1,0:T(8,128)(2,1)S(1)} %get-tuple-element.354.grad_attn.top, bf16[512,1024]{1,0:T(8,128)(2,1)S(1)} %copy-done.10, bf16[3,640,512]{2,1,0:T(8,128)(2,1)S(1)} %copy-done.22, ...), custom_call_target="tpu_custom_call" | custom-call | flops 1000 | bytes 1000 | tf_op jit(solution)/shard_map/aback0/pallas_call | solution.py:47
  189.7 11.0 %aback1.1 = (bf16[3,640,512]{2,1,0:T(8,128)(2,1)S(1)}, f32[640,1024]{1,0:T(8,128)S(1)}, f32[2,512]{1,0:T(2,128)S(1)}) custom-call(s32[6]{0:T(128)S(1)} %concatenate.27.flags, bf16[640,1024]{1,0:T(8,128)(2,1)S(1)} %get-tuple-element.354.grad_attn.top, bf16[512,1024]{1,0:T(8,128)(2,1)S(1)} %copy-done.15, bf16[3,640,512]{2,1,0:T(8,128)(2,1)S(1)} %copy-done.20, ...), custom_call_target="tpu_custom_call" | custom-call | flops 1000 | bytes 1000 | tf_op jit(solution)/shard_map/aback1/pallas_call | solution.py:47
  200.7 4.3 %qkv0away.1 = bf16[2,4,512,512]{3,2,1,0:T(8,128)(2,1)S(1)} custom-call(s32[6]{0:T(128)S(1)} %concatenate.27.flags, bf16[640,1024]{1,0:T(8,128)(2,1)S(1)} %get-tuple-element.277.normed, bf16[640,1024]{1,0:T(8,128)(2,1)S(1)} %get-tuple-element.354.grad_attn.top, bf16[640,512]{1,0:T(8,128)(2,1)S(1)} %get-tuple-element.281.refs_0_, ...), custom_call_target="tpu_custom_call" | custom-call | flops 1000 | bytes 1000 | tf_op jit(solution)/shard_map/qkv0away/pallas_call | solution.py:47
  205.0 4.4 %collective-permute-done.26.refs_1_ = bf16[256,1024]{1,0:T(8,128)(2,1)S(1)} collective-permute-done((bf16[256,1024]{1,0:T(8,128)(2,1)S(1)}, bf16[256,1024]{1,0:T(8,128)(2,1)S(1)}, u32[]{:S(2)}, u32[]{:S(2)}) %collective-permute-start.26) | collective-permute-done | bytes 524320 | tf_op jit(solution)/shard_map/ppermute | solution.py:447
  212.7 3.9 %collective-permute-done.29.refs_2_.refs_4_ = bf16[2,4,512,512]{3,2,1,0:T(8,128)(2,1)S(1)} collective-permute-done((bf16[2,4,512,512]{3,2,1,0:T(8,128)(2,1)S(1)}, bf16[2,4,512,512]{3,2,1,0:T(8,128)(2,1)S(1)}, u32[]{:S(2)}, u32[]{:S(2)}) %collective-permute-start.29) | collective-permute-done | bytes 4194336 | tf_op jit(solution)/shard_map/ppermute | solution.py:447
  220.8 3.7 collective-permute-done.30.refs_1_
  231.0 3.7 last.1
  234.7 5.1 %collective-permute-done.31.refs_1_ = bf16[128,2048]{1,0:T(8,128)(2,1)S(1)} collective-permute-done((bf16[128,2048]{1,0:T(8,128)(2,1)S(1)}, bf16[128,2048]{1,0:T(8,128)(2,1)S(1)}, u32[]{:S(2)}, u32[]{:S(2)}) %collective-permute-start.31) | collective-permute-done | bytes 524320 | tf_op jit(solution)/shard_map/ppermute | solution.py:447
  246.6 17.1 %collective-permute-done.34.refs_1_ = bf16[512,1024]{1,0:T(8,128)(2,1)S(1)} collective-permute-done((bf16[512,1024]{1,0:T(8,128)(2,1)S(1)}, bf16[512,1024]{1,0:T(8,128)(2,1)S(1)}, u32[]{:S(2)}, u32[]{:S(2)}) %collective-permute-start.34) | collective-permute-done | bytes 1048608 | tf_op jit(solution)/shard_map/ppermute | solution.py:447
  274.1 7.7 %collective-permute-done.35 = f32[9216]{0:T(1024)S(1)} collective-permute-done((f32[9216]{0:T(1024)S(1)}, f32[9216]{0:T(1024)S(1)}, u32[]{:S(2)}, u32[]{:S(2)}) %collective-permute-start.35) | collective-permute-done | bytes 36896 | tf_op jit(solution)/shard_map/ppermute | solution.py:447
  281.8 7.9 %collective-permute-done.38.refs_1_ = bf16[128,2048]{1,0:T(8,128)(2,1)S(1)} collective-permute-done((bf16[128,2048]{1,0:T(8,128)(2,1)S(1)}, bf16[128,2048]{1,0:T(8,128)(2,1)S(1)}, u32[]{:S(2)}, u32[]{:S(2)}) %collective-permute-start.38) | collective-permute-done | bytes 524320 | tf_op jit(solution)/shard_map/ppermute | solution.py:447
  295.4 5.3 %collective-permute-done.40.refs_3_ = bf16[256,512]{1,0:T(8,128)(2,1)S(1)} collective-permute-done((bf16[256,512]{1,0:T(8,128)(2,1)S(1)}, bf16[256,512]{1,0:T(8,128)(2,1)S(1)}, u32[]{:S(2)}, u32[]{:S(2)}) %collective-permute-start.40) | collective-permute-done | bytes 262176 | tf_op jit(solution)/shard_map/ppermute | solution.py:447
  300.7 9.8 %collective-permute-done.39.refs_1_ = bf16[256,512]{1,0:T(8,128)(2,1)S(1)} collective-permute-done((bf16[256,512]{1,0:T(8,128)(2,1)S(1)}, bf16[256,512]{1,0:T(8,128)(2,1)S(1)}, u32[]{:S(2)}, u32[]{:S(2)}) %collective-permute-start.39) | collective-permute-done | bytes 262176 | tf_op jit(solution)/shard_map/ppermute | solution.py:447
  315.6 5.2 %fc2join.1 = f32[2048,1024]{1,0:T(8,128)} custom-call(s32[6]{0:T(128)S(1)} %concatenate.27.flags, bf16[512,1024]{1,0:T(8,128)(2,1)S(1)} %fold.31.refs_0_, bf16[512,1024]{1,0:T(8,128)(2,1)S(1)} %collective-permute-done.34.refs_1_, bf16[512,1024]{1,0:T(8,128)(2,1)S(1)} %collective-permute-done.42.refs_2_, bf16[512,1024]{1,0:T(8,128)(2,1)S(1)} %collective-permute-done.43.refs_3_), custom_call_target="tpu_custom_call" | custom-call | flops 1000 | bytes 1000 | tf_op jit(solution)/shard_map/fc2join/pallas_call | solution.py:47
  320.8 15.5 %collective-permute-done.47 = f32[9216]{0:T(1024)S(1)} collective-permute-done((f32[9216]{0:T(1024)S(1)}, f32[9216]{0:T(1024)S(1)}, u32[]{:S(2)}, u32[]{:S(2)}) %collective-permute-start.47) | collective-permute-done | bytes 36896 | tf_op jit(solution)/shard_map/ppermute | solution.py:447
  342.2 6.7 %collective-permute-done.52 = f32[9216]{0:T(1024)S(1)} collective-permute-done((f32[9216]{0:T(1024)S(1)}, f32[9216]{0:T(1024)S(1)}, u32[]{:S(2)}, u32[]{:S(2)}) %collective-permute-start.52) | collective-permute-done | bytes 36896 | tf_op jit(solution)/shard_map/ppermute | solution.py:447
  351.3 3.1 collective-permute-start.55
  354.5 5.2 %fc1join.1 = f32[1024,2048]{1,0:T(8,128)} custom-call(s32[6]{0:T(128)S(1)} %concatenate.27.flags, bf16[256,2048]{1,0:T(8,128)(2,1)S(1)} %fold.37.refs_0_, bf16[256,2048]{1,0:T(8,128)(2,1)S(1)} %collective-permute-done.46.refs_1_, bf16[256,2048]{1,0:T(8,128)(2,1)S(1)} %collective-permute-done.50.refs_2_, bf16[256,2048]{1,0:T(8,128)(2,1)S(1)} %collective-permute-done.51.refs_3_), custom_call_target="tpu_custom_call" | custom-call | flops 1000 | bytes 1000 | tf_op jit(solution)/shard_map/fc1join/pallas_call | solution.py:47
  364.0 3.4 qkvjoin0.1
  369.3 4.6 %qkvjoin1.1 = (f32[512,1024]{1,0:T(8,128)}, f32[3,1024,512]{2,1,0:T(8,128)}) custom-call(s32[6]{0:T(128)S(1)} %concatenate.27.flags, bf16[512,512]{1,0:T(8,128)(2,1)} %collective-permute-done.56.refs_0_, bf16[512,512]{1,0:T(8,128)(2,1)} %collective-permute-done.57.refs_1_, ...), custom_call_target="tpu_custom_call", output_to_operand_aliasing={{0}: (5, {}), {1}: (6, {})} | custom-call | flops 1000 | bytes 1000 | tf_op jit(solution)/shard_map/qkvjoin1/pallas_call | solution.py:47
  (261 shorter events, 143.9 us)
Async XLA Ops:
  3.9 26.6 %collective-permute-start = (bf16[1024,512]{1,0:T(8,128)(2,1)}, bf16[1024,512]{1,0:T(8,128)(2,1)}, u32[]{:S(2)}, u32[]{:S(2)}) collective-permute-start(bf16[1024,512]{1,0:T(8,128)(2,1)} %pad_maximum_fusion), channel_id=1, source_target_pairs={{0,1},{1,0},{2,3},{3,2},{4,5},{5,4},{6,7},{7,6},{8,9},{9,8},{10,11... | collective-permute-start | bytes 3145736 | tf_op jit(solution)/shard_map/ppermute | solution.py:447
  6.9 23.6 %collective-permute-start.1 = (f32[3072]{0:T(1024)S(1)}, f32[3072]{0:T(1024)S(1)}, u32[]{:S(2)}, u32[]{:S(2)}) collective-permute-start(f32[3072]{0:T(1024)S(1)} %constant_dynamic-update-slice_fusion), channel_id=1, source_target_pairs={{0,1},{1,0},{2,3},{3,2},{4,5},{5,4},{6,7},{7,6},{8,9},{9,8},{10,11... | collective-permute-start | bytes 36872 | tf_op jit(solution)/shard_map/ppermute | solution.py:447
  30.5 24.8 %collective-permute-start.2 = (bf16[1024,512]{1,0:T(8,128)(2,1)}, bf16[1024,512]{1,0:T(8,128)(2,1)}, u32[]{:S(2)}, u32[]{:S(2)}) collective-permute-start(bf16[1024,512]{1,0:T(8,128)(2,1)} %collective-permute-done.refs_0_), channel_id=1, source_target_pairs={{0,4},{4,0},{8,12},{12,8},{16,20},{20,16},{24,28},{28,24},{1,5},{5... | collective-permute-start | bytes 3145736 | tf_op jit(solution)/shard_map/ppermute | solution.py:447
  32.3 23.0 %collective-permute-start.3 = (bf16[1024,512]{1,0:T(8,128)(2,1)}, bf16[1024,512]{1,0:T(8,128)(2,1)S(1)}, u32[]{:S(2)}, u32[]{:S(2)}) collective-permute-start(bf16[1024,512]{1,0:T(8,128)(2,1)} %collective-permute-done.refs_0_), channel_id=1, source_target_pairs={{0,2},{2,0},{1,3},{3,1},{4,6},{6,4},{5,7},{7,5},{8,10},{10,8},{9,1... | collective-permute-start | bytes 3145736 | tf_op jit(solution)/shard_map/ppermute | solution.py:447
  32.3 25.7 %collective-permute-start.4 = (bf16[256,2048]{1,0:T(8,128)(2,1)S(1)}, bf16[256,2048]{1,0:T(8,128)(2,1)}, u32[]{:S(2)}, u32[]{:S(2)}) collective-permute-start(bf16[256,2048]{1,0:T(8,128)(2,1)S(1)} %copy-done.37), channel_id=1, source_target_pairs={{0,1},{1,0},{2,3},{3,2},{4,5},{5,4},{6,7},{7,6},{8,9},{9,8},{10,11... | collective-permute-start | bytes 3145736 | tf_op jit(solution)/shard_map/ppermute | solution.py:447
  58.0 18.8 %collective-permute-start.8 = (bf16[256,2048]{1,0:T(8,128)(2,1)}, bf16[256,2048]{1,0:T(8,128)(2,1)}, u32[]{:S(2)}, u32[]{:S(2)}) collective-permute-start(bf16[256,2048]{1,0:T(8,128)(2,1)} %collective-permute-done.4.refs_0_), channel_id=1, source_target_pairs={{0,2},{2,0},{1,3},{3,1},{4,6},{6,4},{5,7},{7,5},{8,10},{10,8},{9,1... | collective-permute-start | bytes 3145736 | tf_op jit(solution)/shard_map/ppermute | solution.py:447
  61.6 13.9 %collective-permute-start.7 = (bf16[128,2048]{1,0:T(8,128)(2,1)S(1)}, bf16[128,2048]{1,0:T(8,128)(2,1)S(1)}, u32[]{:S(2)}, u32[]{:S(2)}) collective-permute-start(bf16[128,2048]{1,0:T(8,128)(2,1)S(1)} %get-tuple-element.272), channel_id=1, source_target_pairs={{0,8},{4,12},{8,0},{12,4},{16,24},{20,28},{24,16},{28,20},{1,9},{5... | collective-permute-start | bytes 1572872 | tf_op jit(solution)/shard_map/ppermute | solution.py:447
  76.8 23.9 %collective-permute-start.11 = (bf16[512,1024]{1,0:T(8,128)(2,1)S(1)}, bf16[512,1024]{1,0:T(8,128)(2,1)S(1)}, u32[]{:S(2)}, u32[]{:S(2)}) collective-permute-start(bf16[512,1024]{1,0:T(8,128)(2,1)S(1)} %pad_maximum_fusion.2), channel_id=1, source_target_pairs={{0,1},{1,0},{2,3},{3,2},{4,5},{5,4},{6,7},{7,6},{8,9},{9,8},{10,11... | collective-permute-start | bytes 3145736 | tf_op jit(solution)/shard_map/ppermute | solution.py:447
  100.7 15.3 %collective-permute-start.15 = (bf16[512,1024]{1,0:T(8,128)(2,1)S(1)}, bf16[512,1024]{1,0:T(8,128)(2,1)S(1)}, u32[]{:S(2)}, u32[]{:S(2)}) collective-permute-start(bf16[512,1024]{1,0:T(8,128)(2,1)S(1)} %collective-permute-done.11.refs_0_), channel_id=1, source_target_pairs={{0,2},{2,0},{1,3},{3,1},{4,6},{6,4},{5,7},{7,5},{8,10},{10,8},{9,1... | collective-permute-start | bytes 3145736 | tf_op jit(solution)/shard_map/ppermute | solution.py:447
  101.8 13.9 %collective-permute-start.14 = (bf16[256,1024]{1,0:T(8,128)(2,1)S(1)}, bf16[256,1024]{1,0:T(8,128)(2,1)S(1)}, u32[]{:S(2)}, u32[]{:S(2)}) collective-permute-start(bf16[256,1024]{1,0:T(8,128)(2,1)S(1)} %get-tuple-element.306), channel_id=1, source_target_pairs={{0,8},{4,12},{8,0},{12,4},{16,24},{20,28},{24,16},{28,20},{1,9},{5... | collective-permute-start | bytes 1572872 | tf_op jit(solution)/shard_map/ppermute | solution.py:447
  118.7 30.7 %collective-permute-start.17 = (bf16[2,256,1024]{2,1,0:T(8,128)(2,1)}, bf16[2,256,1024]{2,1,0:T(8,128)(2,1)}, u32[]{:S(2)}, u32[]{:S(2)}) collective-permute-start(bf16[2,256,1024]{2,1,0:T(8,128)(2,1)} %get-tuple-element.316), channel_id=1, source_target_pairs={{0,4},{4,0},{8,12},{12,8},{16,20},{20,16},{24,28},{28,24},{1,5},{5... | collective-permute-start | bytes 3145736 | tf_op jit(solution)/shard_map/ppermute | solution.py:447
  119.2 30.2 %collective-permute-start.16 = (bf16[1,512,1024]{2,1,0:T(8,128)(2,1)}, bf16[1,512,1024]{2,1,0:T(8,128)(2,1)}, u32[]{:S(2)}, u32[]{:S(2)}) collective-permute-start(bf16[1,512,1024]{2,1,0:T(8,128)(2,1)} %fc21own.1), channel_id=1, source_target_pairs={{0,1},{1,0},{2,3},{3,2},{4,5},{5,4},{6,7},{7,6},{8,9},{9,8},{10,11... | collective-permute-start | bytes 3145736 | tf_op jit(solution)/shard_map/ppermute | solution.py:447
  152.3 14.3 %collective-permute-start.21 = (bf16[256,1024]{1,0:T(8,128)(2,1)S(1)}, bf16[256,1024]{1,0:T(8,128)(2,1)S(1)}, u32[]{:S(2)}, u32[]{:S(2)}) collective-permute-start(bf16[256,1024]{1,0:T(8,128)(2,1)S(1)} %get-tuple-element.343), channel_id=1, source_target_pairs={{0,1},{1,0},{2,3},{3,2},{4,5},{5,4},{6,7},{7,6},{8,9},{9,8},{10,11... | collective-permute-start | bytes 1572872 | tf_op jit(solution)/shard_map/ppermute | solution.py:447
  152.9 13.9 %collective-permute-start.20 = (bf16[256,1024]{1,0:T(8,128)(2,1)S(1)}, bf16[256,1024]{1,0:T(8,128)(2,1)S(1)}, u32[]{:S(2)}, u32[]{:S(2)}) collective-permute-start(bf16[256,1024]{1,0:T(8,128)(2,1)S(1)} %get-tuple-element.342), channel_id=1, source_target_pairs={{0,4},{4,0},{8,12},{12,8},{16,20},{20,16},{24,28},{28,24},{1,5},{5... | collective-permute-start | bytes 1572872 | tf_op jit(solution)/shard_map/ppermute | solution.py:447
  181.5 27.9 %collective-permute-start.25 = (bf16[2,128,2048]{2,1,0:T(8,128)(2,1)S(1)}, bf16[2,128,2048]{2,1,0:T(8,128)(2,1)S(1)}, u32[]{:S(2)}, u32[]{:S(2)}) collective-permute-start(bf16[2,128,2048]{2,1,0:T(8,128)(2,1)S(1)} %get-tuple-element.365), channel_id=1, source_target_pairs={{0,4},{4,0},{8,12},{12,8},{16,20},{20,16},{24,28},{28,24},{1,5},{5... | collective-permute-start | bytes 3145736 | tf_op jit(solution)/shard_map/ppermute | solution.py:447
  183.1 26.3 %collective-permute-start.24 = (bf16[1,256,2048]{2,1,0:T(8,128)(2,1)S(1)}, bf16[1,256,2048]{2,1,0:T(8,128)(2,1)S(1)}, u32[]{:S(2)}, u32[]{:S(2)}) collective-permute-start(bf16[1,256,2048]{2,1,0:T(8,128)(2,1)S(1)} %fc11own.1), channel_id=1, source_target_pairs={{0,1},{1,0},{2,3},{3,2},{4,5},{5,4},{6,7},{7,6},{8,9},{9,8},{10,11... | collective-permute-start | bytes 3145736 | tf_op jit(solution)/shard_map/ppermute | solution.py:447
  185.2 24.2 %collective-permute-start.26 = (bf16[256,1024]{1,0:T(8,128)(2,1)S(1)}, bf16[256,1024]{1,0:T(8,128)(2,1)S(1)}, u32[]{:S(2)}, u32[]{:S(2)}) collective-permute-start(bf16[256,1024]{1,0:T(8,128)(2,1)S(1)} %fold.26.refs_0_), channel_id=1, source_target_pairs={{0,16},{4,20},{8,24},{12,28},{16,0},{20,4},{24,8},{28,12},{1,17},{... | collective-permute-start | bytes 1572872 | tf_op jit(solution)/shard_map/ppermute | solution.py:447
  210.1 14.4 %collective-permute-start.30 = (bf16[256,1024]{1,0:T(8,128)(2,1)S(1)}, bf16[256,1024]{1,0:T(8,128)(2,1)S(1)}, u32[]{:S(2)}, u32[]{:S(2)}) collective-permute-start(bf16[256,1024]{1,0:T(8,128)(2,1)S(1)} %fold.28.refs_0_), channel_id=1, source_target_pairs={{0,8},{4,12},{8,0},{12,4},{16,24},{20,28},{24,16},{28,20},{1,9},{5... | collective-permute-start | bytes 1572872 | tf_op jit(solution)/shard_map/ppermute | solution.py:447
  211.4 14.2 %collective-permute-start.28 = (bf16[128,2048]{1,0:T(8,128)(2,1)S(1)}, bf16[128,2048]{1,0:T(8,128)(2,1)S(1)}, u32[]{:S(2)}, u32[]{:S(2)}) collective-permute-start(bf16[128,2048]{1,0:T(8,128)(2,1)S(1)} %get-tuple-element.386), channel_id=1, source_target_pairs={{0,1},{1,0},{2,3},{3,2},{4,5},{5,4},{6,7},{7,6},{8,9},{9,8},{10,11... | collective-permute-start | bytes 1572872 | tf_op jit(solution)/shard_map/ppermute | solution.py:447
  240.4 23.3 %collective-permute-start.34 = (bf16[512,1024]{1,0:T(8,128)(2,1)S(1)}, bf16[512,1024]{1,0:T(8,128)(2,1)S(1)}, u32[]{:S(2)}, u32[]{:S(2)}) collective-permute-start(bf16[512,1024]{1,0:T(8,128)(2,1)S(1)} %fold.31.refs_0_), channel_id=1, source_target_pairs={{0,4},{4,0},{8,12},{12,8},{16,20},{20,16},{24,28},{28,24},{1,5},{5... | collective-permute-start | bytes 3145736 | tf_op jit(solution)/shard_map/ppermute | solution.py:447
  241.7 23.1 %collective-permute-start.33 = (bf16[2,512,512]{2,1,0:T(8,128)(2,1)S(1)}, bf16[2,512,512]{2,1,0:T(8,128)(2,1)S(1)}, u32[]{:S(2)}, u32[]{:S(2)}) collective-permute-start(bf16[2,512,512]{2,1,0:T(8,128)(2,1)S(1)} %get-tuple-element.415), channel_id=1, source_target_pairs={{0,8},{4,12},{8,0},{12,4},{16,24},{20,28},{24,16},{28,20},{1,9},{5... | collective-permute-start | bytes 3145736 | tf_op jit(solution)/shard_map/ppermute | solution.py:447
  243.4 22.7 %collective-permute-start.32 = (bf16[1,2,512,512]{3,2,1,0:T(8,128)(2,1)S(1)}, bf16[1,2,512,512]{3,2,1,0:T(8,128)(2,1)S(1)}, u32[]{:S(2)}, u32[]{:S(2)}) collective-permute-start(bf16[1,2,512,512]{3,2,1,0:T(8,128)(2,1)S(1)} %qkv1own.1), channel_id=1, source_target_pairs={{0,1},{1,0},{2,3},{3,2},{4,5},{5,4},{6,7},{7,6},{8,9},{9,8},{10,11... | collective-permute-start | bytes 3145736 | tf_op jit(solution)/shard_map/ppermute | solution.py:447
  266.8 23.0 %collective-permute-start.38 = (bf16[128,2048]{1,0:T(8,128)(2,1)S(1)}, bf16[128,2048]{1,0:T(8,128)(2,1)S(1)}, u32[]{:S(2)}, u32[]{:S(2)}) collective-permute-start(bf16[128,2048]{1,0:T(8,128)(2,1)S(1)} %fold.33.refs_0_), channel_id=1, source_target_pairs={{0,16},{4,20},{8,24},{12,28},{16,0},{20,4},{24,8},{28,12},{1,17},{... | collective-permute-start | bytes 1572872 | tf_op jit(solution)/shard_map/ppermute | solution.py:447
  270.4 19.3 %collective-permute-start.37 = (bf16[512,512]{1,0:T(8,128)(2,1)S(1)}, bf16[512,512]{1,0:T(8,128)(2,1)S(1)}, u32[]{:S(2)}, u32[]{:S(2)}) collective-permute-start(bf16[512,512]{1,0:T(8,128)(2,1)S(1)} %get-tuple-element.431), channel_id=1, source_target_pairs={{0,1},{1,0},{2,3},{3,2},{4,5},{5,4},{6,7},{7,6},{8,9},{9,8},{10,11... | collective-permute-start | bytes 1572872 | tf_op jit(solution)/shard_map/ppermute | solution.py:447
  271.9 17.9 %collective-permute-start.36 = (bf16[512,512]{1,0:T(8,128)(2,1)S(1)}, bf16[512,512]{1,0:T(8,128)(2,1)S(1)}, u32[]{:S(2)}, u32[]{:S(2)}) collective-permute-start(bf16[512,512]{1,0:T(8,128)(2,1)S(1)} %get-tuple-element.430), channel_id=1, source_target_pairs={{0,4},{4,0},{8,12},{12,8},{16,20},{20,16},{24,28},{28,24},{1,5},{5... | collective-permute-start | bytes 1572872 | tf_op jit(solution)/shard_map/ppermute | solution.py:447
  289.7 20.8 %collective-permute-start.43 = (bf16[512,1024]{1,0:T(8,128)(2,1)S(1)}, bf16[512,1024]{1,0:T(8,128)(2,1)S(1)}, u32[]{:S(2)}, u32[]{:S(2)}) collective-permute-start(bf16[512,1024]{1,0:T(8,128)(2,1)S(1)} %collective-permute-done.34.refs_1_), channel_id=1, source_target_pairs={{0,2},{2,0},{1,3},{3,1},{4,6},{6,4},{5,7},{7,5},{8,10},{10,8},{9,1... | collective-permute-start | bytes 3145736 | tf_op jit(solution)/shard_map/ppermute | solution.py:447
  289.7 20.8 %collective-permute-start.42 = (bf16[512,1024]{1,0:T(8,128)(2,1)S(1)}, bf16[512,1024]{1,0:T(8,128)(2,1)S(1)}, u32[]{:S(2)}, u32[]{:S(2)}) collective-permute-start(bf16[512,1024]{1,0:T(8,128)(2,1)S(1)} %fold.31.refs_0_), channel_id=1, source_target_pairs={{0,2},{2,0},{1,3},{3,1},{4,6},{6,4},{5,7},{7,5},{8,10},{10,8},{9,1... | collective-permute-start | bytes 3145736 | tf_op jit(solution)/shard_map/ppermute | solution.py:447
  290.9 19.6 %collective-permute-start.41 = (bf16[128,2048]{1,0:T(8,128)(2,1)S(1)}, bf16[128,2048]{1,0:T(8,128)(2,1)S(1)}, u32[]{:S(2)}, u32[]{:S(2)}) collective-permute-start(bf16[128,2048]{1,0:T(8,128)(2,1)S(1)} %fold.35.refs_0_), channel_id=1, source_target_pairs={{0,8},{4,12},{8,0},{12,4},{16,24},{20,28},{24,16},{28,20},{1,9},{5... | collective-permute-start | bytes 1572872 | tf_op jit(solution)/shard_map/ppermute | solution.py:447
  294.0 16.5 %collective-permute-start.39 = (bf16[256,512]{1,0:T(8,128)(2,1)S(1)}, bf16[256,512]{1,0:T(8,128)(2,1)S(1)}, u32[]{:S(2)}, u32[]{:S(2)}) collective-permute-start(bf16[256,512]{1,0:T(8,128)(2,1)S(1)} %get-tuple-element.442), channel_id=1, source_target_pairs={{0,8},{4,12},{8,0},{12,4},{16,24},{20,28},{24,16},{28,20},{1,9},{5... | collective-permute-start | bytes 786440 | tf_op jit(solution)/shard_map/ppermute | solution.py:447
  311.1 27.2 %collective-permute-start.46 = (bf16[256,2048]{1,0:T(8,128)(2,1)S(1)}, bf16[256,2048]{1,0:T(8,128)(2,1)S(1)}, u32[]{:S(2)}, u32[]{:S(2)}) collective-permute-start(bf16[256,2048]{1,0:T(8,128)(2,1)S(1)} %fold.37.refs_0_), channel_id=1, source_target_pairs={{0,4},{4,0},{8,12},{12,8},{16,20},{20,16},{24,28},{28,24},{1,5},{5... | collective-permute-start | bytes 3145736 | tf_op jit(solution)/shard_map/ppermute | solution.py:447
  313.4 25.0 %collective-permute-start.45 = (bf16[512,512]{1,0:T(8,128)(2,1)S(1)}, bf16[512,512]{1,0:T(8,128)(2,1)S(1)}, u32[]{:S(2)}, u32[]{:S(2)}) collective-permute-start(bf16[512,512]{1,0:T(8,128)(2,1)S(1)} %fold.36.refs_0_), channel_id=1, source_target_pairs={{0,16},{4,20},{8,24},{12,28},{16,0},{20,4},{24,8},{28,12},{1,17},{... | collective-permute-start | bytes 1572872 | tf_op jit(solution)/shard_map/ppermute | solution.py:447
  315.1 21.2 %collective-permute-start.47 = (f32[9216]{0:T(1024)S(1)}, f32[9216]{0:T(1024)S(1)}, u32[]{:S(2)}, u32[]{:S(2)}) collective-permute-start(f32[9216]{0:T(1024)S(1)} %add.66), channel_id=1, source_target_pairs={{0,4},{4,0},{8,12},{12,8},{16,20},{20,16},{24,28},{28,24},{1,5},{5... | collective-permute-start | bytes 110600 | tf_op jit(solution)/shard_map/ppermute | solution.py:447
  (69 other events, 444.4 us)

commit v5 on v4

--- a/solution.py
+++ b/solution.py
@@ -609,6 +609,59 @@
                         [pl.BlockSpec(memory_space=pl.ANY)] * len(got),
                         [whole(shape) for shape in shapes],
                         [like(shape, bf16) for shape in shapes],
+                        scratch=[pltpu.SemaphoreType.DMA((16,))],
+                    )
+                    for got in self.got
+                ]
+
+        class FetchLate(Fetch):
+            def __init__(self, shard):
+                self.split, self.shards, self.units = True, [shard], 8
+                self.own = self.places(core, low, high)[0]
+                self.pieces = []
+
+            def places(self, co, lo, hi):
+                return [(4 * co + lo, 4 * co + 2 + hi)]
+
+            def first(self):
+                rows = self.shards[0].shape[0] // 8
+                place = self.own[len(self.pieces)]
+                piece = lax.dynamic_slice_in_dim(self.shards[0], place * rows, rows, axis=0)
+                self.pieces.append([start(peer, piece, slot) for slot in others])
+
+            def second(self):
+                self.got = [
+                    [a, b, start(chip_swap, a, 1), start(chip_swap, b, 2)]
+                    + [start(core_swap, a), start(core_swap, b)]
+                    for a, b in zip(*self.pieces)
+                ]
+
+            def third(self):
+                for got in self.got:
+                    got += [start(core_swap, g) for g in got[2:4]]
+
+            def full(self):
+                def spots(f):
+                    lo, hi = f[2 + images], f[3 + images]
+                    return [
+                        place
+                        for co in (f[1 + images], 1 - f[1 + images])
+                        for place in (
+                            (4 * co + lo,),
+                            (4 * co + 2 + hi,),
+                            (4 * co + 1 - lo,),
+                            (4 * co + 3 - hi,),
+                        )
+                    ]
+
+                return [
+                    run(
+                        "assemble",
+                        static(assemble_kernel, spots, 8, 8),
+                        got,
+                        [pl.BlockSpec(memory_space=pl.ANY)] * 8,
+                        [whole(self.shards[0].shape)],
+                        [like(self.shards[0].shape, bf16)],
                         scratch=[pltpu.SemaphoreType.DMA((16,))],
                     )
                     for got in self.got
@@ -973,6 +1026,8 @@
 
         get_attn.third()
         get_fc1.second()
+        get_fc2 = FetchLate(w_fc2)
+        get_fc2.first()
         qkv, out = [w_qkv], [w_out]
         for w, w_2 in get_attn.full():
             qkv.append(w.value.reshape(3, width, part))
@@ -993,7 +1048,7 @@
         step()
 
         get_fc1.third()
-        get_fc2 = Fetch([w_fc2], True)
+        get_fc2.first()
         fc1 = [w_fc1] + [w for w, in get_fc1.full()]
         for slot in slots:
             hide(slot)
@@ -1057,8 +1112,6 @@
             whole(shape2),
             like(shape2, bf16),
         )
-        step()
-
         w3.t_one()
         w1.t_out()
         w3.k_mid()

time: 378 us -> 375 us (level)
    ppermute x60 -> x62, waiting for transfers between devices: 148 us -> 146 us  [swap(): return lax.ppermute(value, axis, [(i, i ^ mask) for i in range(size)])]
    ppermute x60 -> x62, starting transfers between devices: 54.8 us -> 53.9 us  [swap(): return lax.ppermute(value, axis, [(i, i ^ mask) for i in range(size)])]
    pallas_call x50 -> x49, Pallas kernels: 145 us -> 144 us  [kernel_call(): pl.pallas_call(body, name=name, grid_spec=pltpu.PrefetchScalarGridSpec(nu...]
  transfers between devices with their start and end apart: 60 -> 62, of which waited for: 33 -> 29; matrix products, arithmetic and copies ran while one was open for 2% -> 2% of each run, Pallas kernels for 36% -> 36%
where the time goes in v5:
time: 375 us; the launch traced here: 371 us
  waiting for transfers between devices  146 us (39%)
  Pallas kernels  144 us (38%)
  starting transfers between devices  53.9 us (14%)
  local copies, waits for them, and re-layouts  20.9 us (6%)
    ppermute x62, waiting for transfers between devices, swap(): return lax.ppermute(value, axis, [(i, i ^ mask) for i in range(size)])  146 us
    pallas_call x49, Pallas kernels, kernel_call(): pl.pallas_call(body, name=name, grid_spec=pltpu.PrefetchScalarGridSpec(nu...  144 us
    ppermute x62, starting transfers between devices, swap(): return lax.ppermute(value, axis, [(i, i ^ mask) for i in range(size)])  53.9 us
    unnamed x93, local copies, waits for them, and re-layouts  14.1 us
  transfers between devices with their start and end apart: 62, of which 29 were waited for; matrix products, arithmetic and copies ran while one was open for 2% of the time, Pallas kernels for 36%

profile of v5, /device:TPU:0, one launch (start us, length us, event | category | flops | bytes accessed | tf_op | source)
XLA Modules:
  0.0 370.8 jit_solution(13446490537102553832)
XLA Ops:
  3.9 2.9 collective-permute-start
  18.8 6.0 %attend0.1 = (bf16[3,640,512]{2,1,0:T(8,128)(2,1)S(1)}, bf16[640,512]{1,0:T(8,128)(2,1)S(1)}) custom-call(s32[6]{0:T(128)S(1)} %concatenate.24.flags, bf16[640,1024]{1,0:T(8,128)(2,1)S(1)} %get-tuple-element.277.normed, bf16[3,1024,512]{2,1,0:T(8,128)(2,1)S(1)} %copy-done.3, f32[3,1,512]{2,1,0:T(1,128)S(1)} %pad_maximum_fusion.2.shift), custom_call_target="tpu_custom_call" | custom-call | flops 1000 | bytes 1000 | tf_op jit(solution)/shard_map/attend0/pallas_call | solution.py:47
  26.1 4.4 %collective-permute-done.1 = f32[3072]{0:T(1024)S(1)} collective-permute-done((f32[3072]{0:T(1024)S(1)}, f32[3072]{0:T(1024)S(1)}, u32[]{:S(2)}, u32[]{:S(2)}) %collective-permute-start.1) | collective-permute-done | bytes 12320 | tf_op jit(solution)/shard_map/ppermute | solution.py:447
  33.8 21.5 %collective-permute-done.2.refs_1_ = bf16[1024,512]{1,0:T(8,128)(2,1)} collective-permute-done((bf16[1024,512]{1,0:T(8,128)(2,1)}, bf16[1024,512]{1,0:T(8,128)(2,1)}, u32[]{:S(2)}, u32[]{:S(2)}) %collective-permute-start.2) | collective-permute-done | bytes 1048608 | tf_op jit(solution)/shard_map/ppermute | solution.py:447
  68.0 6.0 %attend1.1 = (bf16[3,640,512]{2,1,0:T(8,128)(2,1)S(1)}, bf16[640,512]{1,0:T(8,128)(2,1)S(1)}) custom-call(s32[6]{0:T(128)S(1)} %concatenate.24.flags, bf16[640,1024]{1,0:T(8,128)(2,1)S(1)} %get-tuple-element.277.normed, bf16[3,1024,512]{2,1,0:T(8,128)(2,1)S(1)} %bitcast.49, f32[3,1,512]{2,1,0:T(1,128)S(1)} %pad_maximum_fusion.3.shift), custom_call_target="tpu_custom_call" | custom-call | flops 1000 | bytes 1000 | tf_op jit(solution)/shard_map/attend1/pallas_call | solution.py:47
  79.1 4.9 %hidden0.1 = (bf16[640,2048]{1,0:T(8,128)(2,1)S(1)}, bf16[640,2048]{1,0:T(8,128)(2,1)S(1)}) custom-call(s32[6]{0:T(128)S(1)} %concatenate.24.flags, bf16[640,1024]{1,0:T(8,128)(2,1)S(1)} %get-tuple-element.292.normed.refs_0_.refs_1_, bf16[1024,2048]{1,0:T(8,128)(2,1)S(1)} %copy-done.1, f32[1,2048]{1,0:T(1,128)S(1)} %bitcast.60), custom_call_target="tpu_custom_call" | custom-call | flops 1000 | bytes 1000 | tf_op jit(solution)/shard_map/hidden0/pallas_call | solution.py:47
  87.8 4.9 %hidden1.1 = (bf16[640,2048]{1,0:T(8,128)(2,1)S(1)}, bf16[640,2048]{1,0:T(8,128)(2,1)S(1)}) custom-call(s32[6]{0:T(128)S(1)} %concatenate.24.flags, bf16[640,1024]{1,0:T(8,128)(2,1)S(1)} %get-tuple-element.292.normed.refs_0_.refs_1_, bf16[1024,2048]{1,0:T(8,128)(2,1)S(1)} %assemble.4.w.refs_7_, f32[1,2048]{1,0:T(1,128)S(1)} %bitcast.59), custom_call_target="tpu_custom_call" | custom-call | flops 1000 | bytes 1000 | tf_op jit(solution)/shard_map/hidden1/pallas_call | solution.py:47
  94.3 3.7 fc20away.1
  100.3 4.9 %collective-permute-done.13.refs_2_.refs_4_ = bf16[2,1024,1024]{2,1,0:T(8,128)(2,1)S(1)} collective-permute-done((bf16[2,1024,1024]{2,1,0:T(8,128)(2,1)S(1)}, bf16[2,1024,1024]{2,1,0:T(8,128)(2,1)S(1)}, u32[]{:S(2)}, u32[]{:S(2)}) %collective-permute-start.13) | collective-permute-done | bytes 4194336 | tf_op jit(solution)/shard_map/ppermute | solution.py:447
  123.3 19.1 %ffn.1 = (bf16[640,2048]{1,0:T(8,128)(2,1)S(1)}, bf16[640,2048]{1,0:T(8,128)(2,1)S(1)}, f32[1,2048]{1,0:T(1,128)S(1)}, f32[1,2048]{1,0:T(1,128)S(1)}, bf16[640,1...) custom-call(s32[6]{0:T(128)S(1)} %concatenate.24.flags, ...), custom_call_target="tpu_custom_call" | custom-call | flops 1000 | bytes 1000 | tf_op jit(solution)/shard_map/ffn/pallas_call | solution.py:47
  142.4 3.9 %fc10away.1 = bf16[2,512,2048]{2,1,0:T(8,128)(2,1)S(1)} custom-call(s32[6]{0:T(128)S(1)} %concatenate.24.flags, bf16[640,1024]{1,0:T(8,128)(2,1)S(1)} %get-tuple-element.292.normed.refs_0_.refs_1_, bf16[640,1024]{1,0:T(8,128)(2,1)S(1)} %get-tuple-element.292.normed.refs_0_.refs_1_, bf16[640,2048]{1,0:T(8,128)(2,1)S(1)} %get-tuple-element.346.refs_2_.refs_1_, ...), custom_call_target="tpu_custom_call" | custom-call | flops 1000 | bytes 1000 | tf_op jit(solution)/shard_map/fc10away/pallas_call | solution.py:47
  157.0 6.4 %collective-permute-done.23.refs_3_ = bf16[256,1024]{1,0:T(8,128)(2,1)S(1)} collective-permute-done((bf16[256,1024]{1,0:T(8,128)(2,1)S(1)}, bf16[256,1024]{1,0:T(8,128)(2,1)S(1)}, u32[]{:S(2)}, u32[]{:S(2)}) %collective-permute-start.23) | collective-permute-done | bytes 524320 | tf_op jit(solution)/shard_map/ppermute | solution.py:447
  167.1 11.4 %aback0.1 = (bf16[3,640,512]{2,1,0:T(8,128)(2,1)S(1)}, f32[640,1024]{1,0:T(8,128)S(1)}, f32[2,512]{1,0:T(2,128)S(1)}) custom-call(s32[6]{0:T(128)S(1)} %concatenate.24.flags, bf16[640,1024]{1,0:T(8,128)(2,1)S(1)} %get-tuple-element.353.grad_attn.top, bf16[512,1024]{1,0:T(8,128)(2,1)S(1)} %copy-done.10, bf16[3,640,512]{2,1,0:T(8,128)(2,1)S(1)} %copy-done.22, ...), custom_call_target="tpu_custom_call" | custom-call | flops 1000 | bytes 1000 | tf_op jit(solution)/shard_map/aback0/pallas_call | solution.py:47
  181.2 2.7 collective-permute-start.28
  185.4 11.0 %aback1.1 = (bf16[3,640,512]{2,1,0:T(8,128)(2,1)S(1)}, f32[640,1024]{1,0:T(8,128)S(1)}, f32[2,512]{1,0:T(2,128)S(1)}) custom-call(s32[6]{0:T(128)S(1)} %concatenate.24.flags, bf16[640,1024]{1,0:T(8,128)(2,1)S(1)} %get-tuple-element.353.grad_attn.top, bf16[512,1024]{1,0:T(8,128)(2,1)S(1)} %copy-done.15, bf16[3,640,512]{2,1,0:T(8,128)(2,1)S(1)} %copy-done.20, ...), custom_call_target="tpu_custom_call" | custom-call | flops 1000 | bytes 1000 | tf_op jit(solution)/shard_map/aback1/pallas_call | solution.py:47
  196.4 4.3 %qkv0away.1 = bf16[2,4,512,512]{3,2,1,0:T(8,128)(2,1)S(1)} custom-call(s32[6]{0:T(128)S(1)} %concatenate.24.flags, bf16[640,1024]{1,0:T(8,128)(2,1)S(1)} %get-tuple-element.277.normed, bf16[640,1024]{1,0:T(8,128)(2,1)S(1)} %get-tuple-element.353.grad_attn.top, bf16[640,512]{1,0:T(8,128)(2,1)S(1)} %get-tuple-element.281.refs_0_, ...), custom_call_target="tpu_custom_call" | custom-call | flops 1000 | bytes 1000 | tf_op jit(solution)/shard_map/qkv0away/pallas_call | solution.py:47
  200.6 4.9 %collective-permute-done.28.refs_1_ = bf16[256,1024]{1,0:T(8,128)(2,1)S(1)} collective-permute-done((bf16[256,1024]{1,0:T(8,128)(2,1)S(1)}, bf16[256,1024]{1,0:T(8,128)(2,1)S(1)}, u32[]{:S(2)}, u32[]{:S(2)}) %collective-permute-start.28) | collective-permute-done | bytes 524320 | tf_op jit(solution)/shard_map/ppermute | solution.py:447
  216.9 3.7 collective-permute-done.32.refs_1_
  233.6 3.7 last.1
  237.2 23.7 %collective-permute-done.33.refs_1_ = bf16[128,2048]{1,0:T(8,128)(2,1)S(1)} collective-permute-done((bf16[128,2048]{1,0:T(8,128)(2,1)S(1)}, bf16[128,2048]{1,0:T(8,128)(2,1)S(1)}, u32[]{:S(2)}, u32[]{:S(2)}) %collective-permute-start.33) | collective-permute-done | bytes 524320 | tf_op jit(solution)/shard_map/ppermute | solution.py:447
  261.6 3.3 collective-permute-start.40
  268.7 9.6 %collective-permute-done.37 = f32[9216]{0:T(1024)S(1)} collective-permute-done((f32[9216]{0:T(1024)S(1)}, f32[9216]{0:T(1024)S(1)}, u32[]{:S(2)}, u32[]{:S(2)}) %collective-permute-start.37) | collective-permute-done | bytes 36896 | tf_op jit(solution)/shard_map/ppermute | solution.py:447
  278.3 7.9 %collective-permute-done.40.refs_1_ = bf16[128,2048]{1,0:T(8,128)(2,1)S(1)} collective-permute-done((bf16[128,2048]{1,0:T(8,128)(2,1)S(1)}, bf16[128,2048]{1,0:T(8,128)(2,1)S(1)}, u32[]{:S(2)}, u32[]{:S(2)}) %collective-permute-start.40) | collective-permute-done | bytes 524320 | tf_op jit(solution)/shard_map/ppermute | solution.py:447
  290.8 6.4 %collective-permute-done.42.refs_3_ = bf16[256,512]{1,0:T(8,128)(2,1)S(1)} collective-permute-done((bf16[256,512]{1,0:T(8,128)(2,1)S(1)}, bf16[256,512]{1,0:T(8,128)(2,1)S(1)}, u32[]{:S(2)}, u32[]{:S(2)}) %collective-permute-start.42) | collective-permute-done | bytes 262176 | tf_op jit(solution)/shard_map/ppermute | solution.py:447
  297.2 9.7 %collective-permute-done.41.refs_1_ = bf16[256,512]{1,0:T(8,128)(2,1)S(1)} collective-permute-done((bf16[256,512]{1,0:T(8,128)(2,1)S(1)}, bf16[256,512]{1,0:T(8,128)(2,1)S(1)}, u32[]{:S(2)}, u32[]{:S(2)}) %collective-permute-start.41) | collective-permute-done | bytes 262176 | tf_op jit(solution)/shard_map/ppermute | solution.py:447
  312.3 5.2 %fc2join.1 = f32[2048,1024]{1,0:T(8,128)} custom-call(s32[6]{0:T(128)S(1)} %concatenate.24.flags, bf16[512,1024]{1,0:T(8,128)(2,1)S(1)} %fold.29.refs_0_, bf16[512,1024]{1,0:T(8,128)(2,1)S(1)} %collective-permute-done.36.refs_1_, bf16[512,1024]{1,0:T(8,128)(2,1)S(1)} %collective-permute-done.44.refs_2_, bf16[512,1024]{1,0:T(8,128)(2,1)S(1)} %collective-permute-done.45.refs_3_), custom_call_target="tpu_custom_call" | custom-call | flops 1000 | bytes 1000 | tf_op jit(solution)/shard_map/fc2join/pallas_call | solution.py:47
  317.4 15.3 %collective-permute-done.49 = f32[9216]{0:T(1024)S(1)} collective-permute-done((f32[9216]{0:T(1024)S(1)}, f32[9216]{0:T(1024)S(1)}, u32[]{:S(2)}, u32[]{:S(2)}) %collective-permute-start.49) | collective-permute-done | bytes 36896 | tf_op jit(solution)/shard_map/ppermute | solution.py:447
  338.6 6.7 %collective-permute-done.54 = f32[9216]{0:T(1024)S(1)} collective-permute-done((f32[9216]{0:T(1024)S(1)}, f32[9216]{0:T(1024)S(1)}, u32[]{:S(2)}, u32[]{:S(2)}) %collective-permute-start.54) | collective-permute-done | bytes 36896 | tf_op jit(solution)/shard_map/ppermute | solution.py:447
  346.8 3.3 collective-permute-start.57
  350.1 5.2 %fc1join.1 = f32[1024,2048]{1,0:T(8,128)} custom-call(s32[6]{0:T(128)S(1)} %concatenate.24.flags, bf16[256,2048]{1,0:T(8,128)(2,1)S(1)} %fold.35.refs_0_, bf16[256,2048]{1,0:T(8,128)(2,1)S(1)} %collective-permute-done.48.refs_1_, bf16[256,2048]{1,0:T(8,128)(2,1)S(1)} %collective-permute-done.52.refs_2_, bf16[256,2048]{1,0:T(8,128)(2,1)S(1)} %collective-permute-done.53.refs_3_), custom_call_target="tpu_custom_call" | custom-call | flops 1000 | bytes 1000 | tf_op jit(solution)/shard_map/fc1join/pallas_call | solution.py:47
  360.5 3.4 qkvjoin0.1
  365.8 4.6 %qkvjoin1.1 = (f32[512,1024]{1,0:T(8,128)}, f32[3,1024,512]{2,1,0:T(8,128)}) custom-call(s32[6]{0:T(128)S(1)} %concatenate.24.flags, bf16[512,512]{1,0:T(8,128)(2,1)} %collective-permute-done.58.refs_0_, bf16[512,512]{1,0:T(8,128)(2,1)} %collective-permute-done.59.refs_1_, ...), custom_call_target="tpu_custom_call", output_to_operand_aliasing={{0}: (5, {}), {1}: (6, {})} | custom-call | flops 1000 | bytes 1000 | tf_op jit(solution)/shard_map/qkvjoin1/pallas_call | solution.py:47
  (263 shorter events, 133.7 us)
Async XLA Ops:
  3.9 26.6 %collective-permute-start = (bf16[1024,512]{1,0:T(8,128)(2,1)}, bf16[1024,512]{1,0:T(8,128)(2,1)}, u32[]{:S(2)}, u32[]{:S(2)}) collective-permute-start(bf16[1024,512]{1,0:T(8,128)(2,1)} %pad_maximum_fusion), channel_id=1, source_target_pairs={{0,1},{1,0},{2,3},{3,2},{4,5},{5,4},{6,7},{7,6},{8,9},{9,8},{10,11... | collective-permute-start | bytes 3145736 | tf_op jit(solution)/shard_map/ppermute | solution.py:447
  6.9 23.6 %collective-permute-start.1 = (f32[3072]{0:T(1024)S(1)}, f32[3072]{0:T(1024)S(1)}, u32[]{:S(2)}, u32[]{:S(2)}) collective-permute-start(f32[3072]{0:T(1024)S(1)} %constant_dynamic-update-slice_fusion), channel_id=1, source_target_pairs={{0,1},{1,0},{2,3},{3,2},{4,5},{5,4},{6,7},{7,6},{8,9},{9,8},{10,11... | collective-permute-start | bytes 36872 | tf_op jit(solution)/shard_map/ppermute | solution.py:447
  30.5 24.8 %collective-permute-start.2 = (bf16[1024,512]{1,0:T(8,128)(2,1)}, bf16[1024,512]{1,0:T(8,128)(2,1)}, u32[]{:S(2)}, u32[]{:S(2)}) collective-permute-start(bf16[1024,512]{1,0:T(8,128)(2,1)} %collective-permute-done.refs_0_), channel_id=1, source_target_pairs={{0,4},{4,0},{8,12},{12,8},{16,20},{20,16},{24,28},{28,24},{1,5},{5... | collective-permute-start | bytes 3145736 | tf_op jit(solution)/shard_map/ppermute | solution.py:447
  32.3 23.0 %collective-permute-start.3 = (bf16[1024,512]{1,0:T(8,128)(2,1)}, bf16[1024,512]{1,0:T(8,128)(2,1)S(1)}, u32[]{:S(2)}, u32[]{:S(2)}) collective-permute-start(bf16[1024,512]{1,0:T(8,128)(2,1)} %collective-permute-done.refs_0_), channel_id=1, source_target_pairs={{0,2},{2,0},{1,3},{3,1},{4,6},{6,4},{5,7},{7,5},{8,10},{10,8},{9,1... | collective-permute-start | bytes 3145736 | tf_op jit(solution)/shard_map/ppermute | solution.py:447
  32.3 25.7 %collective-permute-start.4 = (bf16[256,2048]{1,0:T(8,128)(2,1)S(1)}, bf16[256,2048]{1,0:T(8,128)(2,1)}, u32[]{:S(2)}, u32[]{:S(2)}) collective-permute-start(bf16[256,2048]{1,0:T(8,128)(2,1)S(1)} %copy-done.37), channel_id=1, source_target_pairs={{0,1},{1,0},{2,3},{3,2},{4,5},{5,4},{6,7},{7,6},{8,9},{9,8},{10,11... | collective-permute-start | bytes 3145736 | tf_op jit(solution)/shard_map/ppermute | solution.py:447
  58.0 19.1 %collective-permute-start.8 = (bf16[256,2048]{1,0:T(8,128)(2,1)}, bf16[256,2048]{1,0:T(8,128)(2,1)}, u32[]{:S(2)}, u32[]{:S(2)}) collective-permute-start(bf16[256,2048]{1,0:T(8,128)(2,1)} %collective-permute-done.4.refs_0_), channel_id=1, source_target_pairs={{0,2},{2,0},{1,3},{3,1},{4,6},{6,4},{5,7},{7,5},{8,10},{10,8},{9,1... | collective-permute-start | bytes 3145736 | tf_op jit(solution)/shard_map/ppermute | solution.py:447
  61.7 14.9 %collective-permute-start.7 = (bf16[128,2048]{1,0:T(8,128)(2,1)S(1)}, bf16[128,2048]{1,0:T(8,128)(2,1)S(1)}, u32[]{:S(2)}, u32[]{:S(2)}) collective-permute-start(bf16[128,2048]{1,0:T(8,128)(2,1)S(1)} %get-tuple-element.271), channel_id=1, source_target_pairs={{0,8},{4,12},{8,0},{12,4},{16,24},{20,28},{24,16},{28,20},{1,9},{5... | collective-permute-start | bytes 1572872 | tf_op jit(solution)/shard_map/ppermute | solution.py:447
  77.6 20.3 %collective-permute-start.12 = (bf16[256,1024]{1,0:T(8,128)(2,1)S(1)}, bf16[256,1024]{1,0:T(8,128)(2,1)S(1)}, u32[]{:S(2)}, u32[]{:S(2)}) collective-permute-start(bf16[256,1024]{1,0:T(8,128)(2,1)S(1)} %get-tuple-element.290), channel_id=1, source_target_pairs={{0,1},{1,0},{2,3},{3,2},{4,5},{5,4},{6,7},{7,6},{8,9},{9,8},{10,11... | collective-permute-start | bytes 1572872 | tf_op jit(solution)/shard_map/ppermute | solution.py:447
  98.0 14.3 %collective-permute-start.15 = (bf16[256,1024]{1,0:T(8,128)(2,1)S(1)}, bf16[256,1024]{1,0:T(8,128)(2,1)S(1)}, u32[]{:S(2)}, u32[]{:S(2)}) collective-permute-start(bf16[256,1024]{1,0:T(8,128)(2,1)S(1)} %collective-permute-done.12.refs_1_), channel_id=1, source_target_pairs={{0,8},{4,12},{8,0},{12,4},{16,24},{20,28},{24,16},{28,20},{1,9},{5... | collective-permute-start | bytes 1572872 | tf_op jit(solution)/shard_map/ppermute | solution.py:447
  98.7 14.2 %collective-permute-start.14 = (bf16[256,1024]{1,0:T(8,128)(2,1)S(1)}, bf16[256,1024]{1,0:T(8,128)(2,1)S(1)}, u32[]{:S(2)}, u32[]{:S(2)}) collective-permute-start(bf16[256,1024]{1,0:T(8,128)(2,1)S(1)} %collective-permute-done.9.refs_0_), channel_id=1, source_target_pairs={{0,4},{4,0},{8,12},{12,8},{16,20},{20,16},{24,28},{28,24},{1,5},{5... | collective-permute-start | bytes 1572872 | tf_op jit(solution)/shard_map/ppermute | solution.py:447
  115.5 30.8 %collective-permute-start.19 = (bf16[2,256,1024]{2,1,0:T(8,128)(2,1)}, bf16[2,256,1024]{2,1,0:T(8,128)(2,1)}, u32[]{:S(2)}, u32[]{:S(2)}) collective-permute-start(bf16[2,256,1024]{2,1,0:T(8,128)(2,1)} %get-tuple-element.314), channel_id=1, source_target_pairs={{0,4},{4,0},{8,12},{12,8},{16,20},{20,16},{24,28},{28,24},{1,5},{5... | collective-permute-start | bytes 3145736 | tf_op jit(solution)/shard_map/ppermute | solution.py:447
  117.1 29.2 %collective-permute-start.18 = (bf16[1,512,1024]{2,1,0:T(8,128)(2,1)}, bf16[1,512,1024]{2,1,0:T(8,128)(2,1)}, u32[]{:S(2)}, u32[]{:S(2)}) collective-permute-start(bf16[1,512,1024]{2,1,0:T(8,128)(2,1)} %fc21own.1), channel_id=1, source_target_pairs={{0,1},{1,0},{2,3},{3,2},{4,5},{5,4},{6,7},{7,6},{8,9},{9,8},{10,11... | collective-permute-start | bytes 3145736 | tf_op jit(solution)/shard_map/ppermute | solution.py:447
  149.2 14.3 %collective-permute-start.23 = (bf16[256,1024]{1,0:T(8,128)(2,1)S(1)}, bf16[256,1024]{1,0:T(8,128)(2,1)S(1)}, u32[]{:S(2)}, u32[]{:S(2)}) collective-permute-start(bf16[256,1024]{1,0:T(8,128)(2,1)S(1)} %get-tuple-element.342), channel_id=1, source_target_pairs={{0,1},{1,0},{2,3},{3,2},{4,5},{5,4},{6,7},{7,6},{8,9},{9,8},{10,11... | collective-permute-start | bytes 1572872 | tf_op jit(solution)/shard_map/ppermute | solution.py:447
  179.3 26.2 %collective-permute-start.27 = (bf16[2,128,2048]{2,1,0:T(8,128)(2,1)S(1)}, bf16[2,128,2048]{2,1,0:T(8,128)(2,1)S(1)}, u32[]{:S(2)}, u32[]{:S(2)}) collective-permute-start(bf16[2,128,2048]{2,1,0:T(8,128)(2,1)S(1)} %get-tuple-element.364), channel_id=1, source_target_pairs={{0,4},{4,0},{8,12},{12,8},{16,20},{20,16},{24,28},{28,24},{1,5},{5... | collective-permute-start | bytes 3145736 | tf_op jit(solution)/shard_map/ppermute | solution.py:447
  179.9 25.7 %collective-permute-start.26 = (bf16[1,256,2048]{2,1,0:T(8,128)(2,1)S(1)}, bf16[1,256,2048]{2,1,0:T(8,128)(2,1)S(1)}, u32[]{:S(2)}, u32[]{:S(2)}) collective-permute-start(bf16[1,256,2048]{2,1,0:T(8,128)(2,1)S(1)} %fc11own.1), channel_id=1, source_target_pairs={{0,1},{1,0},{2,3},{3,2},{4,5},{5,4},{6,7},{7,6},{8,9},{9,8},{10,11... | collective-permute-start | bytes 3145736 | tf_op jit(solution)/shard_map/ppermute | solution.py:447
  181.2 24.3 %collective-permute-start.28 = (bf16[256,1024]{1,0:T(8,128)(2,1)S(1)}, bf16[256,1024]{1,0:T(8,128)(2,1)S(1)}, u32[]{:S(2)}, u32[]{:S(2)}) collective-permute-start(bf16[256,1024]{1,0:T(8,128)(2,1)S(1)} %fold.24.refs_0_), channel_id=1, source_target_pairs={{0,16},{4,20},{8,24},{12,28},{16,0},{20,4},{24,8},{28,12},{1,17},{... | collective-permute-start | bytes 1572872 | tf_op jit(solution)/shard_map/ppermute | solution.py:447
  206.2 14.4 %collective-permute-start.32 = (bf16[256,1024]{1,0:T(8,128)(2,1)S(1)}, bf16[256,1024]{1,0:T(8,128)(2,1)S(1)}, u32[]{:S(2)}, u32[]{:S(2)}) collective-permute-start(bf16[256,1024]{1,0:T(8,128)(2,1)S(1)} %fold.26.refs_0_), channel_id=1, source_target_pairs={{0,8},{4,12},{8,0},{12,4},{16,24},{20,28},{24,16},{28,20},{1,9},{5... | collective-permute-start | bytes 1572872 | tf_op jit(solution)/shard_map/ppermute | solution.py:447
  207.6 14.1 %collective-permute-start.30 = (bf16[128,2048]{1,0:T(8,128)(2,1)S(1)}, bf16[128,2048]{1,0:T(8,128)(2,1)S(1)}, u32[]{:S(2)}, u32[]{:S(2)}) collective-permute-start(bf16[128,2048]{1,0:T(8,128)(2,1)S(1)} %get-tuple-element.385), channel_id=1, source_target_pairs={{0,1},{1,0},{2,3},{3,2},{4,5},{5,4},{6,7},{7,6},{8,9},{9,8},{10,11... | collective-permute-start | bytes 1572872 | tf_op jit(solution)/shard_map/ppermute | solution.py:447
  223.5 37.5 %collective-permute-start.36 = (bf16[512,1024]{1,0:T(8,128)(2,1)S(1)}, bf16[512,1024]{1,0:T(8,128)(2,1)S(1)}, u32[]{:S(2)}, u32[]{:S(2)}) collective-permute-start(bf16[512,1024]{1,0:T(8,128)(2,1)S(1)} %fold.29.refs_0_), channel_id=1, source_target_pairs={{0,4},{4,0},{8,12},{12,8},{16,20},{20,16},{24,28},{28,24},{1,5},{5... | collective-permute-start | bytes 3145736 | tf_op jit(solution)/shard_map/ppermute | solution.py:447
  225.7 35.2 %collective-permute-start.35 = (bf16[2,512,512]{2,1,0:T(8,128)(2,1)S(1)}, bf16[2,512,512]{2,1,0:T(8,128)(2,1)S(1)}, u32[]{:S(2)}, u32[]{:S(2)}) collective-permute-start(bf16[2,512,512]{2,1,0:T(8,128)(2,1)S(1)} %get-tuple-element.406), channel_id=1, source_target_pairs={{0,8},{4,12},{8,0},{12,4},{16,24},{20,28},{24,16},{28,20},{1,9},{5... | collective-permute-start | bytes 3145736 | tf_op jit(solution)/shard_map/ppermute | solution.py:447
  227.5 33.4 %collective-permute-start.34 = (bf16[1,2,512,512]{3,2,1,0:T(8,128)(2,1)S(1)}, bf16[1,2,512,512]{3,2,1,0:T(8,128)(2,1)S(1)}, u32[]{:S(2)}, u32[]{:S(2)}) collective-permute-start(bf16[1,2,512,512]{3,2,1,0:T(8,128)(2,1)S(1)} %qkv1own.1), channel_id=1, source_target_pairs={{0,1},{1,0},{2,3},{3,2},{4,5},{5,4},{6,7},{7,6},{8,9},{9,8},{10,11... | collective-permute-start | bytes 3145736 | tf_op jit(solution)/shard_map/ppermute | solution.py:447
  228.9 32.0 %collective-permute-start.33 = (bf16[128,2048]{1,0:T(8,128)(2,1)S(1)}, bf16[128,2048]{1,0:T(8,128)(2,1)S(1)}, u32[]{:S(2)}, u32[]{:S(2)}) collective-permute-start(bf16[128,2048]{1,0:T(8,128)(2,1)S(1)} %get-tuple-element.396), channel_id=1, source_target_pairs={{0,8},{4,12},{8,0},{12,4},{16,24},{20,28},{24,16},{28,20},{1,9},{5... | collective-permute-start | bytes 1572872 | tf_op jit(solution)/shard_map/ppermute | solution.py:447
  261.6 24.5 %collective-permute-start.40 = (bf16[128,2048]{1,0:T(8,128)(2,1)S(1)}, bf16[128,2048]{1,0:T(8,128)(2,1)S(1)}, u32[]{:S(2)}, u32[]{:S(2)}) collective-permute-start(bf16[128,2048]{1,0:T(8,128)(2,1)S(1)} %fold.31.refs_0_), channel_id=1, source_target_pairs={{0,16},{4,20},{8,24},{12,28},{16,0},{20,4},{24,8},{28,12},{1,17},{... | collective-permute-start | bytes 1572872 | tf_op jit(solution)/shard_map/ppermute | solution.py:447
  266.0 20.2 %collective-permute-start.39 = (bf16[512,512]{1,0:T(8,128)(2,1)S(1)}, bf16[512,512]{1,0:T(8,128)(2,1)S(1)}, u32[]{:S(2)}, u32[]{:S(2)}) collective-permute-start(bf16[512,512]{1,0:T(8,128)(2,1)S(1)} %get-tuple-element.429), channel_id=1, source_target_pairs={{0,1},{1,0},{2,3},{3,2},{4,5},{5,4},{6,7},{7,6},{8,9},{9,8},{10,11... | collective-permute-start | bytes 1572872 | tf_op jit(solution)/shard_map/ppermute | solution.py:447
  266.7 19.5 %collective-permute-start.38 = (bf16[512,512]{1,0:T(8,128)(2,1)S(1)}, bf16[512,512]{1,0:T(8,128)(2,1)S(1)}, u32[]{:S(2)}, u32[]{:S(2)}) collective-permute-start(bf16[512,512]{1,0:T(8,128)(2,1)S(1)} %get-tuple-element.428), channel_id=1, source_target_pairs={{0,4},{4,0},{8,12},{12,8},{16,20},{20,16},{24,28},{28,24},{1,5},{5... | collective-permute-start | bytes 1572872 | tf_op jit(solution)/shard_map/ppermute | solution.py:447
  286.2 20.8 %collective-permute-start.45 = (bf16[512,1024]{1,0:T(8,128)(2,1)S(1)}, bf16[512,1024]{1,0:T(8,128)(2,1)S(1)}, u32[]{:S(2)}, u32[]{:S(2)}) collective-permute-start(bf16[512,1024]{1,0:T(8,128)(2,1)S(1)} %collective-permute-done.36.refs_1_), channel_id=1, source_target_pairs={{0,2},{2,0},{1,3},{3,1},{4,6},{6,4},{5,7},{7,5},{8,10},{10,8},{9,1... | collective-permute-start | bytes 3145736 | tf_op jit(solution)/shard_map/ppermute | solution.py:447
  286.2 20.8 %collective-permute-start.44 = (bf16[512,1024]{1,0:T(8,128)(2,1)S(1)}, bf16[512,1024]{1,0:T(8,128)(2,1)S(1)}, u32[]{:S(2)}, u32[]{:S(2)}) collective-permute-start(bf16[512,1024]{1,0:T(8,128)(2,1)S(1)} %fold.29.refs_0_), channel_id=1, source_target_pairs={{0,2},{2,0},{1,3},{3,1},{4,6},{6,4},{5,7},{7,5},{8,10},{10,8},{9,1... | collective-permute-start | bytes 3145736 | tf_op jit(solution)/shard_map/ppermute | solution.py:447
  287.4 19.6 %collective-permute-start.43 = (bf16[128,2048]{1,0:T(8,128)(2,1)S(1)}, bf16[128,2048]{1,0:T(8,128)(2,1)S(1)}, u32[]{:S(2)}, u32[]{:S(2)}) collective-permute-start(bf16[128,2048]{1,0:T(8,128)(2,1)S(1)} %fold.33.refs_0_), channel_id=1, source_target_pairs={{0,8},{4,12},{8,0},{12,4},{16,24},{20,28},{24,16},{28,20},{1,9},{5... | collective-permute-start | bytes 1572872 | tf_op jit(solution)/shard_map/ppermute | solution.py:447
  290.4 16.5 %collective-permute-start.41 = (bf16[256,512]{1,0:T(8,128)(2,1)S(1)}, bf16[256,512]{1,0:T(8,128)(2,1)S(1)}, u32[]{:S(2)}, u32[]{:S(2)}) collective-permute-start(bf16[256,512]{1,0:T(8,128)(2,1)S(1)} %get-tuple-element.440), channel_id=1, source_target_pairs={{0,8},{4,12},{8,0},{12,4},{16,24},{20,28},{24,16},{28,20},{1,9},{5... | collective-permute-start | bytes 786440 | tf_op jit(solution)/shard_map/ppermute | solution.py:447
  307.6 26.2 %collective-permute-start.48 = (bf16[256,2048]{1,0:T(8,128)(2,1)S(1)}, bf16[256,2048]{1,0:T(8,128)(2,1)S(1)}, u32[]{:S(2)}, u32[]{:S(2)}) collective-permute-start(bf16[256,2048]{1,0:T(8,128)(2,1)S(1)} %fold.35.refs_0_), channel_id=1, source_target_pairs={{0,4},{4,0},{8,12},{12,8},{16,20},{20,16},{24,28},{28,24},{1,5},{5... | collective-permute-start | bytes 3145736 | tf_op jit(solution)/shard_map/ppermute | solution.py:447
  308.8 25.0 %collective-permute-start.47 = (bf16[512,512]{1,0:T(8,128)(2,1)S(1)}, bf16[512,512]{1,0:T(8,128)(2,1)S(1)}, u32[]{:S(2)}, u32[]{:S(2)}) collective-permute-start(bf16[512,512]{1,0:T(8,128)(2,1)S(1)} %fold.34.refs_0_), channel_id=1, source_target_pairs={{0,16},{4,20},{8,24},{12,28},{16,0},{20,4},{24,8},{28,12},{1,17},{... | collective-permute-start | bytes 1572872 | tf_op jit(solution)/shard_map/ppermute | solution.py:447
  310.8 22.0 %collective-permute-start.49 = (f32[9216]{0:T(1024)S(1)}, f32[9216]{0:T(1024)S(1)}, u32[]{:S(2)}, u32[]{:S(2)}) collective-permute-start(f32[9216]{0:T(1024)S(1)} %add.66), channel_id=1, source_target_pairs={{0,4},{4,0},{8,12},{12,8},{16,20},{20,16},{24,28},{28,24},{1,5},{5... | collective-permute-start | bytes 110600 | tf_op jit(solution)/shard_map/ppermute | solution.py:447
  (71 other events, 503.3 us)
